TPU v7x, 32 devices: a whole 2x2x4 slice. The times are simulated.
32 devices in a mesh: seq: 4 (over x, core), row: 4 (over z), col: 2 (over y).
Axes of the slice: x: 2, y: 2, z: 4, core: 2. Of those that a mesh axis runs over, the one named last changes fastest.
Arguments:
- tokens: bfloat16 [8192, 768], P(('seq', 'row')), may hold values from -6 to 6
- cotangent: bfloat16 [8192, 768], P(('seq', 'row'), 'col'), may hold values from -6 to 6
- lengths: int32 [3], replicated, may hold values from 1024 to 4096, as said below
- block_order: int32 [16], replicated, may hold values from 0 to 15, each once
- attention_gain: float32 [768], P('col'), may hold values from 0.5 to 1.5
- attention_shift: float32 [768], P('col'), may hold values from -1.75 to 1.75
- feedforward_gain: float32 [768], P('col'), may hold values from 0.5 to 1.5
- feedforward_shift: float32 [768], P('col'), may hold values from -1.75 to 1.75
- query_weight: bfloat16 [768, 768], P('col', 'row'), may hold values from -0.21875 to 0.21875
- query_bias: float32 [768], P('row'), may hold values from -1.75 to 1.75
- keyval_weight: bfloat16 [768, 128], P('col'), may hold values from -0.21875 to 0.21875
- keyval_bias: float32 [128], replicated, may hold values from -1.75 to 1.75
- upward_weight: bfloat16 [768, 3072], P('col', 'row'), may hold values from -0.21875 to 0.21875
- upward_bias: float32 [3072], P('row'), may hold values from -1.75 to 1.75
- output_weight: bfloat16 [768, 768], P('row', 'col'), may hold values from -0.75 to 0.75
- output_bias: float32 [768], P('col'), may hold values from -1.75 to 1.75
- down_weight: bfloat16 [3072, 768], P('row', 'col'), may hold values from -0.109375 to 0.109375
- down_bias: float32 [768], P('col'), may hold values from -1.75 to 1.75
Outputs:
- layer_output: bfloat16 [8192, 768], P(('seq', 'row'), 'col')
- keyval_cache: bfloat16 [8192, 128], P(('seq', 'col'))
- tokens_grad: bfloat16 [8192, 768], P(('seq', 'row'), 'col')
- attention_gain_grad: float32 [768], P('col')
- attention_shift_grad: float32 [768], P('col')
- feedforward_gain_grad: float32 [768], P('col')
- feedforward_shift_grad: float32 [768], P('col')
- query_weight_grad: float32 [768, 768], P('col', 'row')
- query_bias_grad: float32 [768], P('row')
- keyval_weight_grad: float32 [768, 128], P('col', 'row')
- keyval_bias_grad: float32 [128], P('row')
- upward_weight_grad: float32 [768, 3072], P('col', 'row')
- upward_bias_grad: float32 [3072], P('row')
- output_weight_grad: float32 [768, 768], P('row', 'col')
- output_bias_grad: float32 [768], P('col')
- down_weight_grad: float32 [3072, 768], P('row', 'col')
- down_bias_grad: float32 [768], P('col')
Inputs may be any that keep to these rules, and one draw needn't show every extreme that they name: Every length is a whole multiple of 512, the lengths sum to 8192, and the longest is exactly 4096. `block_order`: each block number appears once.
All inputs are finite; a program needn't handle non-finite values.
Results may differ from a plain program's by a relative error of at most 0.025.
Values may be sent and summed in bfloat16 or wider, within the bound.
No kernel may reach another device: no remote copies, remote signals or barrier semaphores. Data moves between devices by JAX's collectives and lax.ppermute only.
A program may use at most 256 MiB of HBM per device.

v0:
```python
import jax
import jax.numpy as jnp
from jax import lax
from jax.sharding import PartitionSpec as P

HD = 64
ROT = 16
BLOCK = 512
LONGEST = 16


EPS = 1e-05
NEGATIVE = -1e30


def spin_tables(positions, half_rot):
    exponent = jnp.arange(half_rot, dtype=jnp.float32) * (1.0 / half_rot)
    frequency = 1.0 / 10000.0**exponent
    angles = positions.astype(jnp.float32)[:, None] * frequency[None, :]
    return (jnp.cos(angles), jnp.sin(angles))


def spin(values_in, cosine_table, sine_table, half_rot):
    front_half = values_in[..., :half_rot]
    behind = values_in[..., half_rot : 2 * half_rot]
    return jnp.concatenate(
        [
            front_half * cosine_table - behind * sine_table,
            behind * cosine_table + front_half * sine_table,
            values_in[..., 2 * half_rot :],
        ],
        axis=-1,
    )


def standardize(values_in):
    row_mean = jnp.mean(values_in, axis=1, keepdims=True)
    spread = jnp.mean(values_in * values_in, axis=1, keepdims=True) - row_mean * row_mean
    inverse_root = lax.rsqrt(spread + EPS)
    return ((values_in - row_mean) * inverse_root, inverse_root)


def deal(arrays, target):
    group_size = lax.axis_size(("seq", "col"))
    leading = arrays[0].shape[0]
    flats = [member.reshape(1, leading, group_size, -1) for member in arrays]
    widths = [flat.shape[-1] for flat in flats]
    joined = jnp.concatenate(flats, axis=3)
    spread = lax.all_to_all(joined, ("seq", "col"), split_axis=2, concat_axis=0, tiled=True)
    placed = jnp.take(spread.reshape(-1, spread.shape[-1]), target, axis=0)
    placed = placed.reshape(group_size, leading, 1, spread.shape[-1])
    landed = lax.all_to_all(placed, ("seq", "col"), split_axis=0, concat_axis=2, tiled=True)
    results = []
    offset = 0
    for member, width in zip(arrays, widths):
        results.append(landed[..., offset : offset + width].reshape(member.shape))
        offset = offset + width
    return results


def block_attention(query_block, grad_block, own_block, first_block, fetch, store, buffer_init):
    score_scale = HD ** (-0.5)
    heads = query_block.shape[1]
    lower = jnp.arange(BLOCK)[None, :] <= jnp.arange(BLOCK)[:, None]

    def scores_of(key_part, key_block):
        raw_scores = (
            jnp.einsum("ihd,kd->hik", query_block, key_part, preferred_element_type=jnp.float32)
            * score_scale
        )
        allowed = lower | (key_block < own_block)
        return jnp.where(allowed[None], raw_scores, NEGATIVE)

    def max_pass(key_block, state_pair):
        running_top, running_sum = state_pair
        pair_rows = fetch(key_block)
        scores = scores_of(pair_rows[:, :HD], key_block)
        new_top = jnp.maximum(running_top, jnp.max(scores, axis=2))
        running_sum = running_sum * jnp.exp(running_top - new_top) + jnp.sum(
            jnp.exp(scores - new_top[:, :, None]), axis=2
        )
        return (new_top, running_sum)

    start_pair = (
        jnp.full((heads, BLOCK), NEGATIVE, jnp.float32),
        jnp.zeros((heads, BLOCK), jnp.float32),
    )
    running_top, running_sum = lax.fori_loop(first_block, own_block + 1, max_pass, start_pair)
    log_total = running_top + jnp.log(running_sum)

    def value_pass(key_block, mixed_sum):
        pair_rows = fetch(key_block)
        weights = jnp.exp(scores_of(pair_rows[:, :HD], key_block) - log_total[:, :, None]).astype(
            jnp.bfloat16
        )
        return mixed_sum + jnp.einsum(
            "hik,kd->ihd", weights, pair_rows[:, HD:], preferred_element_type=jnp.float32
        )

    mixed_sum = lax.fori_loop(
        first_block, own_block + 1, value_pass, jnp.zeros(query_block.shape, jnp.float32)
    )
    row_dots = jnp.transpose(jnp.einsum("ihd,ihd->ih", grad_block.astype(jnp.float32), mixed_sum))

    def grad_pass(key_block, state_pair):
        buffer_now, grad_query = state_pair
        pair_rows = fetch(key_block)
        key_part = pair_rows[:, :HD]
        value_part = pair_rows[:, HD:]
        probs = jnp.exp(scores_of(key_part, key_block) - log_total[:, :, None])
        grad_probs = jnp.einsum(
            "ihd,kd->hik", grad_block, value_part, preferred_element_type=jnp.float32
        )
        grad_scores = (probs * (grad_probs - row_dots[:, :, None])).astype(jnp.bfloat16)
        grad_query = (
            grad_query
            + jnp.einsum("hik,kd->ihd", grad_scores, key_part, preferred_element_type=jnp.float32)
            * score_scale
        )
        grad_keys = (
            jnp.einsum("hik,ihd->kd", grad_scores, query_block, preferred_element_type=jnp.float32)
            * score_scale
        )
        grad_values = jnp.einsum(
            "hik,ihd->kd",
            probs.astype(jnp.bfloat16),
            grad_block,
            preferred_element_type=jnp.float32,
        )
        contribution = jnp.concatenate([grad_keys, grad_values], axis=1).astype(jnp.bfloat16)
        return (store(buffer_now, key_block, contribution), grad_query)

    buffer_out, grad_query = lax.fori_loop(
        first_block,
        own_block + 1,
        grad_pass,
        (buffer_init, jnp.zeros(query_block.shape, jnp.float32)),
    )
    return (mixed_sum, grad_query, buffer_out)


def on_device(
    tokens,
    cotangent,
    lengths,
    block_order,
    attention_gain,
    attention_shift,
    feedforward_gain,
    feedforward_shift,
    query_weight,
    query_bias,
    keyval_weight,
    keyval_bias,
    upward_weight,
    upward_bias,
    output_weight,
    output_bias,
    down_weight,
    down_bias,
):
    row_count = lax.axis_size("row")
    col_count = lax.axis_size("col")
    row_me = lax.axis_index("row")
    col_me = lax.axis_index("col")
    group_me = lax.axis_index(("seq", "col"))
    block_total = block_order.shape[0]
    max_blocks = min(LONGEST, block_total // 2)
    own_rows = tokens.shape[0]
    model_width = tokens.shape[1]
    feature_span = query_weight.shape[0]
    query_width = query_weight.shape[1]
    pair_width = keyval_weight.shape[1]
    upward_width = upward_weight.shape[1]
    local_heads = query_width // HD
    half_rot = ROT // 2
    left_width = query_width + pair_width
    counter = jnp.arange(block_total, dtype=jnp.int32)
    inverse = jnp.sum(
        jnp.where(block_order[:, None] == counter[None, :], counter[:, None], 0), axis=0
    )
    all_x, all_dy = (
        lax.all_gather(tokens, "row", axis=0, tiled=True),
        lax.all_gather(cotangent, "row", axis=0, tiled=True),
    )
    normed_full, inverse_roots = standardize(all_x.astype(jnp.float32))
    normed = lax.dynamic_slice_in_dim(normed_full, col_me * feature_span, feature_span, 1)
    first_in = (normed * attention_gain + attention_shift).astype(jnp.bfloat16)
    second_in = (normed * feedforward_gain + feedforward_shift).astype(jnp.bfloat16)
    left_weight = jnp.concatenate([query_weight, keyval_weight], axis=1)
    out_weight = jnp.concatenate([output_weight, down_weight], axis=0)
    seq_rows = all_x.shape[0]
    local_rows = seq_rows // col_count
    half_blocks = local_rows // BLOCK
    projected = lax.psum_scatter(
        jnp.concatenate(
            [
                jnp.dot(first_in, left_weight, preferred_element_type=jnp.float32),
                jnp.dot(second_in, upward_weight, preferred_element_type=jnp.float32),
                lax.dot_general(
                    all_dy, out_weight, (((1,), (1,)), ((), ())), preferred_element_type=jnp.float32
                ),
            ],
            axis=1,
        ).astype(jnp.bfloat16),
        "col",
        scatter_dimension=0,
        tiled=True,
    ).astype(jnp.float32)
    upward_end = left_width + upward_width
    query_pre = projected[:, :query_width] + query_bias
    keyval_pre = projected[:, query_width:left_width] + keyval_bias
    upward = projected[:, left_width:upward_end] + upward_bias
    grad_mixed = projected[:, upward_end : upward_end + query_width].astype(jnp.bfloat16)
    gelu_value, gelu_back = jax.vjp(
        lambda field_in: jax.nn.gelu(field_in, approximate=False), upward
    )
    hidden = gelu_value.astype(jnp.bfloat16)
    grad_upward = gelu_back(projected[:, upward_end + query_width :])[0].astype(jnp.bfloat16)
    seq_blocks = lengths // BLOCK
    block_starts = jnp.cumsum(seq_blocks) - seq_blocks

    def tables_of(blocks):
        firsts = jnp.max(
            jnp.where(block_starts[None, :] <= blocks[:, None], block_starts[None, :], 0), axis=1
        )
        positions = (
            (blocks - firsts)[:, None] * BLOCK + jnp.arange(BLOCK, dtype=jnp.int32)[None, :]
        ).reshape(-1)
        cosine_table, sine_table = spin_tables(positions, half_rot)
        return (firsts, cosine_table, sine_table)

    given_blocks = group_me * half_blocks + jnp.arange(half_blocks, dtype=jnp.int32)
    given_firsts, given_cos, given_sin = tables_of(given_blocks)
    owners = jnp.take(block_order, given_blocks)
    owner_firsts, owner_cos, owner_sin = tables_of(owners)
    query_rot = spin(
        query_pre.reshape(local_rows, local_heads, HD),
        given_cos[:, None, :],
        given_sin[:, None, :],
        half_rot,
    ).astype(jnp.bfloat16)
    keyval_rot = jnp.concatenate(
        [spin(keyval_pre[:, :HD], given_cos, given_sin, half_rot), keyval_pre[:, HD:]], axis=1
    ).astype(jnp.bfloat16)
    query_blocks = query_rot.reshape(half_blocks, BLOCK, local_heads, HD)
    grad_blocks = grad_mixed.reshape(half_blocks, BLOCK, local_heads, HD)
    extended_len = half_blocks
    level_count = 0
    while extended_len < max_blocks - 1 + half_blocks:
        extended_len = extended_len * 2
        level_count = level_count + 1
    dealt_queries, dealt_grads = deal((query_blocks, grad_blocks), block_order)
    all_keys = lax.all_gather(keyval_rot, ("seq", "col"), axis=0, tiled=True).reshape(
        block_total, BLOCK, pair_width
    )

    def fetch_all(key_block):
        return lax.dynamic_index_in_dim(all_keys, key_block, 0, keepdims=False)

    def store_all(buffer_now, key_block, contribution):
        old_part = lax.dynamic_index_in_dim(buffer_now, key_block, 0, keepdims=False)
        return lax.dynamic_update_index_in_dim(
            buffer_now, old_part + contribution.astype(jnp.float32), key_block, 0
        )

    def dense_block(buffer_in, inputs):
        query_block, grad_block, own_block, first_block = inputs
        mixed_sum, grad_query, buffer_out = block_attention(
            query_block, grad_block, own_block, first_block, fetch_all, store_all, buffer_in
        )
        return (buffer_out, (mixed_sum, grad_query))

    key_buffer, (mixed_sums, grad_queries) = lax.scan(
        dense_block,
        jnp.zeros((block_total, BLOCK, pair_width), jnp.float32),
        (dealt_queries, dealt_grads, owners, owner_firsts),
    )
    cache_rows = jnp.take(all_keys, owners, axis=0)
    mixed_back = mixed_sums.reshape(half_blocks, BLOCK, query_width).astype(jnp.bfloat16)
    turned = spin(
        grad_queries.reshape(local_rows, local_heads, HD),
        owner_cos[:, None, :],
        -owner_sin[:, None, :],
        half_rot,
    )
    mixed_back, query_back = (
        mixed_back,
        turned.reshape(half_blocks, BLOCK, query_width).astype(jnp.bfloat16),
    )
    mixed_given, grad_query_given = deal((mixed_back, query_back), inverse)
    key_grads = lax.psum_scatter(
        key_buffer.reshape(-1, pair_width), ("seq", "col"), scatter_dimension=0, tiled=True
    )
    grad_keyval = jnp.concatenate(
        [spin(key_grads[:, :HD], given_cos, -given_sin, half_rot), key_grads[:, HD:]], axis=1
    ).astype(jnp.bfloat16)
    branch_in = jnp.concatenate([mixed_given.reshape(local_rows, query_width), hidden], axis=1)
    branch_all = lax.all_gather(branch_in, "col", axis=0, tiled=True)
    branch_total = lax.psum_scatter(
        jnp.dot(branch_all, out_weight, preferred_element_type=jnp.float32).astype(jnp.bfloat16),
        "row",
        scatter_dimension=0,
        tiled=True,
    ).astype(jnp.float32)
    residual_own = lax.dynamic_slice_in_dim(tokens, col_me * feature_span, feature_span, 1).astype(
        jnp.float32
    )
    layer_out = (residual_own + branch_total + output_bias + down_bias).astype(jnp.bfloat16)
    grad_inputs = jnp.concatenate(
        [grad_query_given.reshape(local_rows, query_width), grad_keyval, grad_upward], axis=1
    )
    all_grads = lax.all_gather(grad_inputs, "col", axis=0, tiled=True)
    grad_first = lax.dot_general(
        all_grads[:, :left_width],
        left_weight,
        (((1,), (1,)), ((), ())),
        preferred_element_type=jnp.float32,
    )
    grad_second = lax.dot_general(
        all_grads[:, left_width:],
        upward_weight,
        (((1,), (1,)), ((), ())),
        preferred_element_type=jnp.float32,
    )
    stat_rows = jnp.stack(
        [
            jnp.concatenate(
                [jnp.sum(grad_first * normed, axis=0), jnp.sum(grad_second * normed, axis=0)]
            ),
            jnp.concatenate([jnp.sum(grad_first, axis=0), jnp.sum(grad_second, axis=0)]),
        ]
    )
    pair_grads = lax.dot_general(
        all_grads[:, query_width:left_width],
        first_in,
        (((0,), (0,)), ((), ())),
        preferred_element_type=jnp.float32,
    )
    pair_table = pair_grads.reshape(row_count, -1, 2 * feature_span)
    pair_bias = jnp.sum(all_grads[:, query_width:left_width], axis=0, dtype=jnp.float32).reshape(
        row_count, 1, -1
    )
    bias_rows = jnp.pad(pair_bias, ((0, 0), (0, 0), (0, 2 * feature_span - pair_bias.shape[-1])))
    paired_grads = jnp.concatenate([grad_first, grad_second], axis=1).reshape(
        row_count, own_rows, 2 * feature_span
    )
    norm_table = jnp.concatenate(
        [
            paired_grads,
            jnp.broadcast_to(stat_rows[None], (row_count, 2, 2 * feature_span)),
            pair_table,
            bias_rows,
        ],
        axis=1,
    )
    norm_table = norm_table.reshape(-1, 2 * feature_span)
    summed_rows = lax.psum_scatter(
        norm_table.astype(jnp.bfloat16), "row", scatter_dimension=0, tiled=True
    ).astype(jnp.float32)
    grad_norm = (
        summed_rows[:own_rows, :feature_span] * attention_gain
        + summed_rows[:own_rows, feature_span:] * feedforward_gain
    )
    normed_own = lax.dynamic_slice_in_dim(normed, row_me * own_rows, own_rows, 0)
    roots_own = lax.dynamic_slice_in_dim(inverse_roots, row_me * own_rows, own_rows, 0)
    moment_one, moment_two = lax.psum(
        (
            jnp.sum(grad_norm, axis=1, keepdims=True),
            jnp.sum(grad_norm * normed_own, axis=1, keepdims=True),
        ),
        "col",
    )
    grad_tokens = (
        cotangent.astype(jnp.float32)
        + roots_own
        * (grad_norm - moment_one / model_width - normed_own * (moment_two / model_width))
    ).astype(jnp.bfloat16)
    grad_query_w = lax.dot_general(
        first_in,
        all_grads[:, :query_width],
        (((0,), (0,)), ((), ())),
        preferred_element_type=jnp.float32,
    )
    grad_up = lax.dot_general(
        second_in,
        all_grads[:, left_width:],
        (((0,), (0,)), ((), ())),
        preferred_element_type=jnp.float32,
    )
    grad_out = lax.dot_general(
        branch_all, all_dy, (((0,), (0,)), ((), ())), preferred_element_type=jnp.float32
    )
    bias_query = jnp.sum(all_grads[:, :query_width], axis=0, dtype=jnp.float32)
    bias_up = jnp.sum(all_grads[:, left_width:], axis=0, dtype=jnp.float32)
    bias_out = jnp.sum(all_dy, axis=0, dtype=jnp.float32)
    extra_rows = summed_rows[own_rows:]
    sum_query, sum_up, sum_out, sum_bias_query, sum_bias_up, sum_bias_out, sum_extra = (
        lax.psum(grad_query_w.astype(jnp.bfloat16), "seq").astype(jnp.float32),
        lax.psum(grad_up.astype(jnp.bfloat16), "seq").astype(jnp.float32),
        lax.psum(grad_out.astype(jnp.bfloat16), "seq").astype(jnp.float32),
        lax.psum(bias_query.astype(jnp.bfloat16), "seq").astype(jnp.float32),
        lax.psum(bias_up.astype(jnp.bfloat16), "seq").astype(jnp.float32),
        lax.psum(bias_out.astype(jnp.bfloat16), "seq").astype(jnp.float32),
        lax.psum(extra_rows.astype(jnp.bfloat16), "seq").astype(jnp.float32),
    )
    piece_rows = pair_table.shape[1]
    pair_piece = sum_extra[2 : 2 + piece_rows].reshape(pair_width // row_count, feature_span)
    keyval_weight_out = jnp.transpose(pair_piece)
    keyval_bias_out = sum_extra[2 + piece_rows, : pair_width // row_count]
    return (
        layer_out,
        cache_rows.reshape(local_rows, pair_width),
        grad_tokens,
        sum_extra[0, :feature_span],
        sum_extra[1, :feature_span],
        sum_extra[0, feature_span:],
        sum_extra[1, feature_span:],
        sum_query,
        sum_bias_query,
        keyval_weight_out,
        keyval_bias_out,
        sum_up,
        sum_bias_up,
        sum_out[:query_width],
        sum_bias_out,
        sum_out[query_width:],
        sum_bias_out,
    )


def solution(mesh):
    in_specs = (
        P(("seq", "row"), None),
        P(("seq", "row"), "col"),
        P(),
        P(),
        P("col"),
        P("col"),
        P("col"),
        P("col"),
        P("col", "row"),
        P("row"),
        P("col", None),
        P(),
        P("col", "row"),
        P("row"),
        P("row", "col"),
        P("col"),
        P("row", "col"),
        P("col"),
    )
    out_specs = (
        P(("seq", "row"), "col"),
        P(("seq", "col"), None),
        P(("seq", "row"), "col"),
        P("col"),
        P("col"),
        P("col"),
        P("col"),
        P("col", "row"),
        P("row"),
        P("col", "row"),
        P("row"),
        P("col", "row"),
        P("row"),
        P("row", "col"),
        P("col"),
        P("row", "col"),
        P("col"),
    )
    return jax.shard_map(
        on_device, mesh=mesh, in_specs=in_specs, out_specs=out_specs, check_vma=False
    )
```

profile of v0, /device:TPU:0, one launch (start us, length us, event | category | flops | bytes accessed | tf_op | source)
XLA Modules:
  0.0 930.7 jit_solution(5056491906633612154)
XLA Ops:
  11.9 37.5 %all-gather.8.cloned.1.call-done = bf16[2048,384]{1,0:T(8,128)(2,1)} async-done(((bf16[512,384]{1,0:T(8,128)(2,1)}), bf16[2048,384]{1,0:T(8,128)(2,1)}) %all-gather.8.cloned.1.call-update) | async-done | bytes 1572880 | tf_op jit(solution)/shard_map/all_gather | solution.py:184
  49.4 5.6 convert_bitcast_fusion
  55.1 58.3 %all-gather.6.cloned.1.call-done = bf16[2048,768]{1,0:T(8,128)(2,1)} async-done(((bf16[512,768]{1,0:T(8,128)(2,1)}), bf16[2048,768]{1,0:T(8,128)(2,1)}) %all-gather.6.cloned.1.call-update) | async-done | bytes 3145744 | tf_op jit(solution)/shard_map/all_gather | solution.py:183
  113.4 3.0 convert_reduce_fusion
  122.7 4.1 pad_maximum_fusion
  129.2 95.6 %reduce-scatter.4.cloned.1.call-done = bf16[1024,2048]{0,1:T(8,128)(2,1)} async-done(((bf16[2048,2048]{0,1:T(8,128)(2,1)}), bf16[1024,2048]{0,1:T(8,128)(2,1)}) %reduce-scatter.4.cloned.1.call-update) | async-done | bytes 4194320 | tf_op jit(solution)/shard_map/reduce_scatter | solution.py:195
  226.7 3.2 convert_element_type.176
  230.0 3.1 copy-done.2
  237.7 3.5 all-to-all-start
  242.8 10.2 %all-to-all-done = bf16[1,2,8,24576]{3,1,0,2:T(2,128)(2,1)S(1)} async-done(((bf16[1,2,8,24576]{3,1,0,2:T(2,128)(2,1)}), bf16[1,2,8,24576]{3,1,0,2:T(2,128)(2,1)S(1)}, u32[]{:S(2)}, u32[]{:S(2)}) %all-to-all-start) | async-done | bytes 786464 | tf_op jit(solution)/shard_map/all_to_all | solution.py:49
  255.8 3.7 all-to-all-start.1
  259.6 16.6 %all-to-all-done.1 = bf16[8,2,1,24576]{3,1,2,0:T(2,128)(2,1)S(1)} async-done(((bf16[8,2,1,24576]{3,1,2,0:T(2,128)(2,1)}), bf16[8,2,1,24576]{3,1,2,0:T(2,128)(2,1)S(1)}, u32[]{:S(2)}, u32[]{:S(2)}) %all-to-all-start.1) | async-done | bytes 786464 | tf_op jit(solution)/shard_map/all_to_all | solution.py:52
  281.9 3.2 copy.151
  285.1 2.5 broadcast_in_dim.146
  287.7 92.9 %while.54 = (s32[]{:T(128)}, f32[16,512,128]{1,2,0:T(8,128)}, bf16[2,512,3,64]{1,3,2,0:T(8,128)(2,1)}, f32[2,512,3,64]{1,0,3,2:T(2,128)S(1)}, s32[2]{0:T(128)S(1...) while((s32[]{:T(128)}, f32[16,512,128]{1,2,0:T(8,128)}, ...), condition=%wide.region_15.17_spmd, body=%wide.region_6.16_spmd.sunk | while | flops 824413184 | bytes 31931420 | solution.py:274
  290.9 12.8 %while.55 = (s32[]{:T(128)}, f32[3,512]{1,0:T(4,128)S(1)}, f32[3,512]{1,0:T(4,128)S(1)}, s32[]{:T(128)}, s32[]{:T(128)}, /*index=5*/bf16[16,512,128]{1,2,0:T(8,1...) while((s32[]{:T(128)}, f32[3,512]{1,0:T(4,128)S(1)}, ...), condition=%wide.region_10.11_spmd.clone, body=%wide.region_7.10_spmd.clone.sunk | while | flops 106695688 | bytes 7682205 | solution.py:88
  303.7 11.8 %while.56 = (s32[]{:T(128)}, f32[512,3,64]{0,2,1:T(8,128)S(1)}, s32[]{:T(128)}, bf16[16,512,128]{1,2,0:T(8,128)(2,1)}, s32[]{:T(128)}, /*index=5*/bf16[512,3,64]...) while((s32[]{:T(128)}, f32[512,3,64]{0,2,1:T(8,128)S(1)}, ...), condition=%wide.region_12.13_spmd.clone, body=%wide.region_11.12_spmd.clone.sunk | while | flops 205094912 | bytes 1906845 | solution.py:100
  316.3 36.3 %while.57 = (s32[]{:T(128)}, f32[16,512,128]{1,2,0:T(8,128)}, f32[512,3,64]{0,2,1:T(8,128)S(1)}, s32[]{:T(128)}, s32[]{:T(128)}, /*index=5*/bf16[16,512,128]{1,2...) while((s32[]{:T(128)}, f32[16,512,128]{1,2,0:T(8,128)}, ...), condition=%wide.region_14.15_spmd.clone, body=%wide.region_13.14_spmd.clone.sunk | while | flops 512327680 | bytes 17782968 | solution.py:133
  353.0 3.6 dynamic_update_slice.18
  359.9 3.2 while.55
  363.1 2.9 while.56
  366.9 9.6 %while.57 = (s32[]{:T(128)}, f32[16,512,128]{1,2,0:T(8,128)}, f32[512,3,64]{0,2,1:T(8,128)S(1)}, s32[]{:T(128)}, s32[]{:T(128)}, /*index=5*/bf16[16,512,128]{1,2...) while((s32[]{:T(128)}, f32[16,512,128]{1,2,0:T(8,128)}, ...), condition=%wide.region_14.15_spmd.clone, body=%wide.region_13.14_spmd.clone.sunk | while | flops 512327680 | bytes 17782968 | solution.py:133
  376.9 3.6 dynamic_update_slice.18
  386.8 106.7 %all-to-all-start.2 = ((bf16[1,2,8,24576]{3,1,0,2:T(2,128)(2,1)}), bf16[1,2,8,24576]{3,1,0,2:T(2,128)(2,1)S(1)}, u32[]{:S(2)}, u32[]{:S(2)}) async-start(bf16[1,2,8,24576]{3,1,0,2:T(2,128)(2,1)} %copy.115), calls=%async_computation.3 | async-start | bytes 1572864 | tf_op jit(solution)/shard_map/all_to_all | solution.py:49
  493.7 4.9 copy.146
  498.6 6.7 all-to-all-done.2
  507.3 14.2 %all_to_all.66 = bf16[8,2,1,24576]{3,1,2,0:T(2,128)(2,1)S(1)} all-to-all(bf16[8,2,1,24576]{3,1,2,0:T(2,128)(2,1)S(1)} %bitcast.286), channel_id=1, replica_groups=mesh['seq'=4,'row'=4,'col'=2] {'seq','col'}, dimensions={0} | all-to-all | bytes 1572864 | tf_op jit(solution)/shard_map/all_to_all | solution.py:52
  525.0 26.1 %reduce-scatter.8.cloned.1.call-done = f32[1024,128]{0,1:T(8,128)} async-done(((f32[8192,128]{0,1:T(8,128)}), f32[1024,128]{0,1:T(8,128)}) %reduce-scatter.8.cloned.1.call-update) | async-done | bytes 524304 | tf_op jit(solution)/shard_map/reduce_scatter | solution.py:292
  554.2 9.2 fusion.58
  563.4 3.2 multiply_convert_fusion
  568.9 53.1 %all-gather.12.cloned.1.call-done = bf16[2048,960]{0,1:T(8,128)(2,1)} async-done(((bf16[1024,960]{0,1:T(8,128)(2,1)}), bf16[2048,960]{0,1:T(8,128)(2,1)}) %all-gather.12.cloned.1.call-update) | async-done | bytes 3932176 | tf_op jit(solution)/shard_map/all_gather | solution.py:299
  622.0 5.6 convolution_convert_fusion.3
  627.6 55.6 %all-gather.14.cloned.1.call-done = bf16[2048,1088]{0,1:T(8,128)(2,1)} async-done(((bf16[1024,1088]{0,1:T(8,128)(2,1)}), bf16[2048,1088]{0,1:T(8,128)(2,1)}) %all-gather.14.cloned.1.call-update) | async-done | bytes 4456464 | tf_op jit(solution)/shard_map/all_gather | solution.py:313
  683.3 2.4 convolution_convert_fusion.4
  685.6 5.2 fusion.59
  691.1 5.6 convolution_convert_fusion.1
  700.3 3.9 fusion.56
  704.3 3.1 multiply_reduce_fusion.2
  709.9 4.6 convert_element_type.192
  719.0 2.2 copy.149
  721.2 3.5 copy.119
  727.5 2.4 slice_reduce_fusion
  730.0 2.7 all-reduce.10.cloned.1.call-done
  739.2 31.2 %reduce-scatter.6.cloned.1.call-done = bf16[512,384]{1,0:T(8,128)(2,1)} async-done(((bf16[2048,384]{1,0:T(8,128)(2,1)}), bf16[512,384]{1,0:T(8,128)(2,1)}) %reduce-scatter.6.cloned.1.call-update) | async-done | bytes 393232 | tf_op jit(solution)/shard_map/reduce_scatter | solution.py:300
  772.3 124.6 %all-reduce.8.cloned.1.call-done = bf16[2124,768]{1,0:T(8,128)(2,1)} async-done(((bf16[2124,768]{1,0:T(8,128)(2,1)}), bf16[2124,768]{1,0:T(8,128)(2,1)}) %all-reduce.8.cloned.1.call-update) | async-done | bytes 3262480
  897.8 11.7 %all-reduce.3 = (bf16[19,768]{1,0:T(8,128)(2,1)S(1)}, bf16[192]{0:T(256)(128)(2,1)S(1)}, bf16[768]{0:T(1024)(128)(2,1)S(1)}, bf16[384]{0:T(512)(128)(2,1)S(1)}) all-reduce(bf16[19,768]{1,0:T(8,128)(2,1)S(1)} %constant_dynamic-slice_fusion, ...), channel_id=1, replica_groups=mesh['seq'=4,'row'=4,'col'=2] {'seq'}, use_global_device_ids=true, to_apply=%region_29.31 | all-reduce | flops 15936 | bytes 63744 | tf_op jit(solution)/shard_map/psum | solution.py:405
  913.8 4.9 all-reduce.2
  920.6 2.5 add_convert_fusion.3
  (359 shorter events, 136.1 us)
Async XLA Ops:
  7.2 113.4 %copy-start = (bf16[384,768]{1,0:T(8,128)(2,1)S(1)}, bf16[384,768]{1,0:T(8,128)(2,1)}, u32[]{:S(2)}) copy-start(bf16[384,768]{1,0:T(8,128)(2,1)} %param.40) | copy-start | bytes 1769476
  7.2 42.2 %all-gather.8.cloned.1.call-start = ((), (), s32[]{:S(2)}) async-start(), calls=%async_computation.8 | async-start | bytes 1966080 | tf_op jit(solution)/shard_map/all_gather | solution.py:184
  7.9 105.5 %all-gather.6.cloned.1.call-start = ((), (), s32[]{:S(2)}) async-start(), calls=%async_computation.7 | async-start | bytes 3932160 | tf_op jit(solution)/shard_map/all_gather | solution.py:183
  8.7 216.2 %reduce-scatter.4.cloned.1.call-start = ((), (), s32[]{:S(2)}) async-start(), calls=%async_computation.9 | async-start | bytes 12582912 | tf_op jit(solution)/shard_map/reduce_scatter | solution.py:195
  9.8 108.1 %copy-start.13 = (bf16[384,128]{0,1:T(8,128)(2,1)}, bf16[384,128]{0,1:T(8,128)(2,1)S(1)}, u32[]{:S(2)}) copy-start(bf16[384,128]{0,1:T(8,128)(2,1)S(1)} %copy.102) | copy-start | bytes 294916
  11.9 43.2 %copy-start.24 = (bf16[960,384]{1,0:T(8,128)(2,1)}, bf16[960,384]{1,0:T(8,128)(2,1)S(1)}, u32[]{:S(2)}) copy-start(bf16[960,384]{1,0:T(8,128)(2,1)S(1)} %constant_dynamic-update-slice_fusion) | copy-start | bytes 2211844
  117.5 3.1 copy-start.3
  117.5 3.1 copy-start.39
  129.2 104.1 %copy-start.21 = (f32[1,4,2,128]{3,1,2,0:T(4,128)}, f32[1,4,2,128]{3,1,2,0:T(4,128)S(1)}, u32[]{:S(2)}) copy-start(f32[1,4,2,128]{3,1,2,0:T(4,128)S(1)} %copy.147) | copy-start | bytes 12292
  129.2 104.1 %copy-start.30 = (f32[8]{0:T(128)}, f32[8]{0:T(128)S(1)}, u32[]{:S(2)}) copy-start(f32[8]{0:T(128)S(1)} %negate_power_fusion) | copy-start | bytes 100
  226.7 3.2 copy-start.42
  226.7 6.5 copy-start.41
  229.9 3.2 copy-start.2
  237.7 15.2 %all-to-all-start = ((bf16[1,2,8,24576]{3,1,0,2:T(2,128)(2,1)}), bf16[1,2,8,24576]{3,1,0,2:T(2,128)(2,1)S(1)}, u32[]{:S(2)}, u32[]{:S(2)}) async-start(bf16[1,2,8,24576]{3,1,0,2:T(2,128)(2,1)} %copy.105), calls=%async_computation.1 | async-start | bytes 1572864 | tf_op jit(solution)/shard_map/all_to_all | solution.py:49
  241.3 40.6 %all-gather.10.cloned.1.call-start = ((), (), s32[]{:S(2)}) async-start(), calls=%async_computation.10 | async-start | bytes 2359296 | tf_op jit(solution)/shard_map/all_gather | solution.py:254
  241.5 12.9 %copy-start.43 = (s32[16]{0:T(128)}, s32[16]{0:T(128)S(1)}, u32[]{:S(2)}) copy-start(s32[16]{0:T(128)S(1)} %select_reduce_fusion) | copy-start | bytes 196
  255.8 20.3 %all-to-all-start.1 = ((bf16[8,2,1,24576]{3,1,2,0:T(2,128)(2,1)}), bf16[8,2,1,24576]{3,1,2,0:T(2,128)(2,1)S(1)}, u32[]{:S(2)}, u32[]{:S(2)}) async-start(bf16[8,2,1,24576]{3,1,2,0:T(2,128)(2,1)} %bitcast.16), calls=%async_computation.2 | async-start | bytes 1572864 | tf_op jit(solution)/shard_map/all_to_all | solution.py:52
  287.7 93.6 %copy-start.19 = (f32[1024,8]{0,1:T(8,128)S(1)}, f32[1024,8]{0,1:T(8,128)}, u32[]{:S(2)}) copy-start(f32[1024,8]{0,1:T(8,128)} %get-tuple-element.435) | copy-start | bytes 98308
  287.7 93.7 %copy-start.20 = (f32[1024,8]{0,1:T(8,128)S(1)}, f32[1024,8]{0,1:T(8,128)}, u32[]{:S(2)}) copy-start(f32[1024,8]{0,1:T(8,128)} %get-tuple-element.436) | copy-start | bytes 98308
  383.7 109.9 %copy-start.44 = (s32[16]{0:T(128)S(1)}, s32[16]{0:T(128)}, u32[]{:S(2)}) copy-start(s32[16]{0:T(128)} %copy-done.43) | copy-start | bytes 196
  386.8 118.4 %all-to-all-start.2 = ((bf16[1,2,8,24576]{3,1,0,2:T(2,128)(2,1)}), bf16[1,2,8,24576]{3,1,0,2:T(2,128)(2,1)S(1)}, u32[]{:S(2)}, u32[]{:S(2)}) async-start(bf16[1,2,8,24576]{3,1,0,2:T(2,128)(2,1)} %copy.115), calls=%async_computation.3 | async-start | bytes 1572864 | tf_op jit(solution)/shard_map/all_to_all | solution.py:49
  493.6 57.6 %reduce-scatter.8.cloned.1.call-start = ((), (), s32[]{:S(2)}) async-start(), calls=%async_computation.13 | async-start | bytes 4718592 | tf_op jit(solution)/shard_map/reduce_scatter | solution.py:292
  498.6 123.4 %all-gather.12.cloned.1.call-start = ((), (), s32[]{:S(2)}) async-start(), calls=%async_computation.11 | async-start | bytes 5898240 | tf_op jit(solution)/shard_map/all_gather | solution.py:299
  522.1 29.0 %copy-start.22 = (f32[1,4,2,128]{3,1,2,0:T(4,128)S(1)}, f32[1,4,2,128]{3,1,2,0:T(4,128)}, u32[]{:S(2)}) copy-start(f32[1,4,2,128]{3,1,2,0:T(4,128)} %copy-done.21) | copy-start | bytes 12292
  522.1 29.0 %copy-start.31 = (f32[8]{0:T(128)S(1)}, f32[8]{0:T(128)}, u32[]{:S(2)}) copy-start(f32[8]{0:T(128)} %copy-done.30) | copy-start | bytes 100
  522.1 32.0 %copy-start.26 = (f32[768]{0:T(1024)S(1)}, f32[768]{0:T(1024)}, u32[]{:S(2)}) copy-start(f32[768]{0:T(1024)} %param.41) | copy-start | bytes 9220
  563.4 3.2 copy-start.9
  563.4 3.2 copy-start.12
  568.1 115.2 %all-gather.14.cloned.1.call-start = ((), (), s32[]{:S(2)}) async-start(), calls=%async_computation.14 | async-start | bytes 6684672 | tf_op jit(solution)/shard_map/all_gather | solution.py:313
  568.8 114.5 %copy-start.5 = (bf16[2048,384]{1,0:T(8,128)(2,1)S(1)}, bf16[2048,384]{1,0:T(8,128)(2,1)}, u32[]{:S(2)}) copy-start(bf16[2048,384]{1,0:T(8,128)(2,1)} %copy-done.4) | copy-start | bytes 4718596
  568.8 116.8 %copy-start.40 = (f32[384]{0:T(512)S(1)}, f32[384]{0:T(512)}, u32[]{:S(2)}) copy-start(f32[384]{0:T(512)} %param.34) | copy-start | bytes 4612
  568.8 116.8 %copy-start.46 = (f32[384]{0:T(512)S(1)}, f32[384]{0:T(512)}, u32[]{:S(2)}) copy-start(f32[384]{0:T(512)} %param.35) | copy-start | bytes 4612
  568.9 163.8 %all-reduce.10.cloned.1.call-start = ((), (), s32[]{:S(2)}) async-start(), calls=%async_computation.16 | async-start | bytes 2949120 | tf_op jit(solution)/shard_map/psum | solution.py:399
  685.6 5.4 copy-start.25
  690.9 79.6 %reduce-scatter.6.cloned.1.call-start = ((), (), s32[]{:S(2)}) async-start(), calls=%async_computation.12 | async-start | bytes 1966080 | tf_op jit(solution)/shard_map/reduce_scatter | solution.py:300
  696.8 200.2 %all-reduce.8.cloned.1.call-start = ((), (), s32[]{:S(2)}) async-start(), calls=%async_computation.15 | async-start | bytes 6537216
  698.1 6.2 slice-start
  700.3 4.0 slice-start.1
  700.3 4.0 copy-start.14
  700.3 4.0 copy-start.17
  714.4 4.6 copy-start.7
  729.9 40.5 %copy-start.10 = (bf16[512,768]{1,0:T(8,128)(2,1)S(1)}, bf16[512,768]{1,0:T(8,128)(2,1)}, u32[]{:S(2)}) copy-start(bf16[512,768]{1,0:T(8,128)(2,1)} %param.28) | copy-start | bytes 2359300
  729.9 40.5 %copy-start.33 = (f32[384]{0:T(512)S(1)}, f32[384]{0:T(512)}, u32[]{:S(2)}) copy-start(f32[384]{0:T(512)} %param.45) | copy-start | bytes 4612
  729.9 40.5 %copy-start.34 = (f32[384]{0:T(512)S(1)}, f32[384]{0:T(512)}, u32[]{:S(2)}) copy-start(f32[384]{0:T(512)} %param.43) | copy-start | bytes 4612
  732.6 5.5 copy-start.15
  736.5 175.5 %copy-start.29 = (f32[384]{0:T(512)S(1)}, f32[384]{0:T(512)}, u32[]{:S(2)}) copy-start(f32[384]{0:T(512)} %param.32) | copy-start | bytes 4612
  772.3 148.2 %copy-start.11 = (bf16[512,384]{1,0:T(8,128)(2,1)S(1)}, bf16[512,384]{1,0:T(8,128)(2,1)}, u32[]{:S(2)}) copy-start(bf16[512,384]{1,0:T(8,128)(2,1)} %param.29) | copy-start | bytes 1179652
  919.3 4.4 copy-start.27
  (16 other events, 23.3 us)
Sparse Core Ops, SparseCore 0:
  9.6 39.7 all-gather.7
  51.0 62.3 all-gather.5
  126.9 97.8 reduce-scatter.3
  244.5 33.8 all-gather.9
  498.7 52.4 reduce-scatter.7
  568.2 53.7 all-gather.11
  623.5 59.6 all-gather.13
  691.0 41.6 all-reduce.9
  735.0 35.3 reduce-scatter.5
  772.8 124.1 all-reduce.7
where the time goes:
time: 936 us; the launch traced here: 931 us
  waiting for transfers between devices  521 us (56%)
  starting transfers between devices  115 us (12%)
  local copies, waits for them, and re-layouts  92.2 us (10%)
  other arithmetic  66.5 us (7%)
  matrix products  64.9 us (7%)
  blocking collectives  30.9 us (3%)
  loops' own time  24.9 us (3%)
  between operations  16.2 us (2%)
    unnamed x11, waiting for transfers between devices  127 us
    all_to_all x2, starting transfers between devices, deal(): lax.all_to_all(joined, ('seq', 'col'), split_axis=2, concat_axis=0, tiled...  110 us
    reduce_scatter x1, waiting for transfers between devices, on_device(): lax.psum_scatter(jnp.concatenate([jnp.dot(first_in, left_weight, preferre...  95.6 us
    all_gather x1, waiting for transfers between devices, on_device(): lax.all_gather(tokens, 'row', axis=0, tiled=True)  58.3 us
    all_gather x1, waiting for transfers between devices, on_device(): all_grads = lax.all_gather(grad_inputs, 'col', axis=0, tiled=True)  55.6 us
    all_gather x1, waiting for transfers between devices, on_device(): branch_all = lax.all_gather(branch_in, 'col', axis=0, tiled=True)  53.1 us
    all_gather x1, waiting for transfers between devices, on_device(): lax.all_gather(cotangent, 'row', axis=0, tiled=True)  37.5 us
    reduce_scatter x1, waiting for transfers between devices, on_device(): lax.psum_scatter(jnp.dot(branch_all, out_weight, preferred_element_type=j...  31.2 us
  transfers between devices with their start and end apart: 13, of which 12 were waited for; matrix products, arithmetic and copies ran while one was open for 9% of the time, Pallas kernels for 0%

commit v1 on v0

v1 whole, which is shorter than its diff:
```python
import collections
import functools

import jax
import jax.numpy as jnp
from jax import lax
from jax.experimental import pallas as pl
from jax.experimental.pallas import tpu as pltpu
from jax.sharding import PartitionSpec as P

HD = 64
ROT = 16
BLOCK = 512
LONGEST = 16
VMEM = 60 * 1024 * 1024
Shape = collections.namedtuple("Shape", "seq_count row_count sequences heads")
HALF = 256
EPS = 1e-05
NEGATIVE = -1e30
F32 = jnp.float32
BF16 = jnp.bfloat16

NN = (((1,), (0,)), ((), ()))
NT = (((1,), (1,)), ((), ()))
TN = (((0,), (0,)), ((), ()))


def dot(left, right, dims=NN):
    return lax.dot_general(left, right, dims, preferred_element_type=F32)


def swap(value, axis, bit):
    count = lax.axis_size(axis)
    return lax.ppermute(value, axis, [(i, i ^ bit) for i in range(count)])


def swap_odd_rows(value):
    seq_count, row_count = lax.axis_size("seq"), lax.axis_size("row")
    pairs = []
    for s in range(1, seq_count, 2):
        for r in range(row_count):
            pairs.append((s * row_count + r, s * row_count + (r ^ 2)))
    moved = lax.ppermute(value, ("seq", "row"), pairs)
    return jnp.where(lax.rem(lax.axis_index("seq"), 2) == 0, value, moved)


def swap_add(value, axis, bit):
    rounded = lax.reduce_precision(value, 8, 7)
    return rounded + swap(rounded.astype(BF16), axis, bit).astype(F32)


def split_rows(vector):
    high = lax.reduce_precision(vector, 8, 7)
    return high.astype(BF16), (vector - high).astype(BF16)


def first_of(meta_ref, block, shape):
    start = jnp.int32(0)
    first = jnp.int32(0)
    for i in range(shape.sequences):
        first = jnp.where(start <= block, start, first)
        start = start + meta_ref[3 + i] // BLOCK
    return first


def attention_kernel(
    meta_ref,
    first_ref,
    dy_ref,
    cos_ref,
    sin_ref,
    small0_ref,
    small1_ref,
    kv0_ref,
    kv1_ref,
    kv2_ref,
    kv3_ref,
    *rest,
    shape,
    second,
):
    heads = shape.heads
    rest = list(rest)
    if second:
        dqw_in_ref, dow_in_ref, dqb_in_ref, dkv_in_ref = rest[:4]
        rest = rest[4:]
    out_ref, dx_ref, dqw_ref, dow_ref, dqb_ref, dkv_out_ref, last_ref = rest[:7]
    (
        qd_ref,
        probs_ref,
        high_ref,
        sums_ref,
        dots_ref,
        acc_ref,
        dq_ref,
        dkv_ref,
        kv_ref,
        low_ref,
        qw_ref,
        ow_ref,
        copy_sem,
    ) = rest[7:]
    blocks = kv_ref.shape[0]
    half = blocks // 2
    slot = pl.program_id(0)
    lanes = 2 * HD
    rows = heads * HALF
    seq, row, second_half = meta_ref[0], meta_ref[1], meta_ref[2]
    own_block = lax.bitwise_xor(seq, slot) * shape.row_count + lax.bitwise_xor(
        row, 1 - slot if second else slot
    )
    first_block = first_of(meta_ref, own_block, shape)
    before = own_block - first_block

    def slot_of(block):
        apart_row = lax.bitwise_xor(lax.rem(block, shape.row_count), row)
        apart_seq = lax.bitwise_xor(block // shape.row_count, seq)
        return apart_row + shape.row_count * (
            apart_seq // 2 + (shape.seq_count // 2) * lax.rem(apart_seq, 2)
        )

    @pl.when(slot == 0)
    def _():
        copies = [
            pltpu.make_async_copy(
                piece,
                kv_ref.at[
                    (i // 2) * half : (i // 2 + 1) * half, (i % 2) * HALF : (i % 2 + 1) * HALF, :
                ],
                copy_sem.at[i],
            )
            for i, piece in enumerate((kv0_ref, kv1_ref, kv2_ref, kv3_ref))
        ]
        if second:
            copies.append(pltpu.make_async_copy(dkv_in_ref, dkv_ref, copy_sem.at[4]))
        for copy in copies:
            copy.start()
        span = small0_ref.shape[1]
        count = heads * HD
        for i, small in enumerate((small0_ref, small1_ref)):
            part = slice(i * span, (i + 1) * span)
            qw_ref[:count, part] = small[:count, :]
            ow_ref[:count, part] = small[count : 2 * count, :]
        qw_ref[count:, :] = jnp.zeros_like(qw_ref[count:, :])
        ow_ref[count:, :] = jnp.zeros_like(ow_ref[count:, :])
        if second:
            dqw_ref[...] = dqw_in_ref[...]
            dow_ref[...] = dow_in_ref[...]
            dqb_ref[...] = dqb_in_ref[...]
        else:
            dkv_ref[...] = jnp.zeros_like(dkv_ref)
            dqw_ref[...] = jnp.zeros_like(dqw_ref)
            dow_ref[...] = jnp.zeros_like(dow_ref)
            dqb_ref[...] = jnp.zeros_like(dqb_ref)
        for copy in copies:
            copy.wait()
        if not second:
            copies = []
            dealt = last_ref.shape[0]
            group = seq * 2 + second_half
            for i in range(dealt):
                owner = meta_ref[3 + shape.sequences + group * dealt + i]
                for part in (0, 1):
                    take = jnp.where(second_half > 0, 1 - part, part) * HALF
                    copies.append(
                        pltpu.make_async_copy(
                            kv_ref.at[slot_of(owner), pl.ds(take, HALF), :],
                            last_ref.at[i, part * HALF : (part + 1) * HALF, :],
                            copy_sem.at[5 + 2 * i + part],
                        )
                    )
            for copy in copies:
                copy.start()
            for copy in copies:
                copy.wait()

    cosine = cos_ref[0]
    sine = sin_ref[0]
    lane = lax.broadcasted_iota(jnp.int32, (HALF, lanes), 1)
    front = lane < HD

    def rolled(values):
        return jnp.where(
            lane < ROT // 2,
            pltpu.roll(values, lanes - ROT // 2, 1),
            pltpu.roll(values, ROT // 2, 1),
        )

    def head_of(joined, h):
        return joined[:, (h // 2) * lanes : (h // 2 + 1) * lanes]

    def join(parts):
        tiles = []
        for h in range(0, heads, 2):
            other = parts[h + 1] if h + 1 < heads else jnp.zeros_like(parts[h])
            tiles.append(jnp.where(front, parts[h], other))
        return jnp.concatenate(tiles, axis=1)

    padded = qw_ref.shape[0]
    base = 2 * heads * HD + 7
    query_b = (
        small0_ref[base : base + 1, :padded].astype(F32)
        + small0_ref[base + 8 : base + 9, :padded].astype(F32)
    )
    pre_all = dot(first_ref[0], qw_ref[...], NT) + query_b
    d_all = dot(dy_ref[0], ow_ref[...], NT)
    for h in range(heads):
        pre = head_of(pre_all, h)
        grad = head_of(d_all, h)
        if h % 2:
            pre = pltpu.roll(pre, HD, 1)
        else:
            grad = pltpu.roll(grad, HD, 1)
        turned = jnp.where(front, pre * cosine + rolled(pre) * sine, 0.0)
        mine = slice(h * HALF, (h + 1) * HALF)
        qd_ref[mine, :] = turned.astype(BF16) * BF16(HD**-0.5)
        qd_ref[rows + h * HALF : rows + (h + 1) * HALF, :] = jnp.where(front, 0.0, grad).astype(BF16)

    high_ref[...] = jnp.full_like(high_ref, NEGATIVE)
    sums_ref[...] = jnp.zeros_like(sums_ref)

    def block_at(step):
        return slot_of(first_block + step)

    def weigh(step, mask):
        scores = dot(kv_ref[block_at(step)], qd_ref[:rows, :], NT)
        if mask:
            row_in = lax.rem(lax.broadcasted_iota(jnp.int32, (BLOCK, rows), 1), HALF)
            key_in = lax.broadcasted_iota(jnp.int32, (BLOCK, rows), 0)
            limit = jnp.where(second_half > 0, BLOCK, 0)
            keep = (key_in <= row_in) | ((key_in >= HALF) & (key_in < limit))
            scores = jnp.where(keep, scores, NEGATIVE)
        high = jnp.max(scores, axis=0, keepdims=True)
        probs = jnp.exp(scores - high)
        probs_ref[step] = probs.astype(BF16)
        high_ref[pl.ds(step, 1), :] = high
        sums_ref[pl.ds(step, 1), :] = jnp.sum(probs, axis=0, keepdims=True)

    weigh(before, True)
    lax.fori_loop(0, before, lambda step, c: (weigh(step, False), c)[1], 0)

    share = jnp.exp(high_ref[...] - jnp.max(high_ref[...], axis=0, keepdims=True))
    high_ref[...] = share / jnp.sum(share * sums_ref[...], axis=0, keepdims=True)

    def mix(step, first):
        probs = (probs_ref[step].astype(F32) * high_ref[pl.ds(step, 1), :]).astype(BF16)
        probs_ref[step] = probs
        part = dot(probs, kv_ref[block_at(step)], TN)
        if first:
            acc_ref[...] = part
        else:
            acc_ref[...] += part

    mix(before, True)
    lax.fori_loop(0, before, lambda step, c: (mix(step, False), c)[1], 0)

    parts = []
    for h in range(heads):
        mine = slice(h * HALF, (h + 1) * HALF)
        mixed = acc_ref[mine, :]
        grad = qd_ref[rows + h * HALF : rows + (h + 1) * HALF, :].astype(F32)
        dots_ref[:, mine] = jnp.sum(jnp.transpose(mixed * grad), axis=0, keepdims=True)
        parts.append(mixed if h % 2 else pltpu.roll(mixed, HD, 1))
    joined = join(parts).astype(BF16)
    out_ref[0] = dot(joined, ow_ref[...])
    dow_ref[...] += dot(joined, dy_ref[0], TN)

    def backward(step, first):
        where = block_at(step)
        block = kv_ref[where]
        probs = probs_ref[step]
        grad_probs = dot(block, qd_ref[rows:, :], NT)
        grad_scores = (probs.astype(F32) * (grad_probs - dots_ref[...])).astype(BF16)
        total = dot(jnp.concatenate([grad_scores, probs], axis=1), qd_ref[...])
        grad_q = dot(grad_scores, block, TN)
        if first:
            dq_ref[...] = grad_q
        else:
            dq_ref[...] += grad_q
        dkv_ref[where] = (dkv_ref[where].astype(F32) + total).astype(dkv_ref.dtype)

    backward(before, True)
    lax.fori_loop(0, before, lambda step, c: (backward(step, False), c)[1], 0)

    parts = []
    for h in range(heads):
        part = dq_ref[h * HALF : (h + 1) * HALF, :] * (HD**-0.5)
        part = part * cosine - rolled(part) * sine
        parts.append(pltpu.roll(part, HD, 1) if h % 2 else part)
    joined = join(parts)
    dqb_ref[...] += jnp.sum(joined, axis=0, keepdims=True)
    joined = joined.astype(BF16)
    dx_ref[0] = dot(joined, qw_ref[...])
    dqw_ref[...] += dot(joined, first_ref[0], TN)

    @pl.when(slot == 1)
    def _():
        if not second:
            copies = [pltpu.make_async_copy(dkv_ref, dkv_out_ref, copy_sem.at[0])]
            copies[0].start()
        else:
            copies = [pltpu.make_async_copy(dkv_ref.at[:half], dkv_out_ref, copy_sem.at[0])]
            copies[0].start()
            if dkv_ref.dtype == BF16:
                copies.append(pltpu.make_async_copy(dkv_ref.at[half:], last_ref, copy_sem.at[1]))
            else:
                low_ref[...] = dkv_ref[half:].astype(BF16)
                copies.append(pltpu.make_async_copy(low_ref, last_ref, copy_sem.at[1]))
            copies[1].start()
        for copy in copies:
            copy.wait()


def attention(meta, first_in, dy, cosine, sine, small, pieces, so_far, shape):
    second = so_far is not None
    _, _, width = first_in.shape
    half = pieces[0].shape[0]
    blocks = 2 * half
    lanes = 2 * HD
    heads = shape.heads
    padded = -(-heads // 2) * lanes
    rows = heads * HALF
    longest = min(LONGEST, blocks // 2)
    total_type = F32 if blocks <= 32 else BF16
    dealt = blocks // (2 * shape.seq_count)
    offset = 2 if second else 0

    def per_slot(lanes):
        return pl.BlockSpec((1, HALF, lanes), lambda i, m: (i + offset, 0, 0))

    def out_slot(lanes):
        return pl.BlockSpec((1, HALF, lanes), lambda i, m: (i, 0, 0))

    def whole(array):
        return pl.BlockSpec(
            array.shape, lambda i, m: (0,) * len(array.shape), pipeline_mode=pl.Buffered(buffer_count=1)
        )

    far = pl.BlockSpec(memory_space=pltpu.MemorySpace.HBM)
    arrays = [first_in, dy, cosine, sine, *small, *pieces]
    in_specs = [per_slot(width), per_slot(width), per_slot(lanes), per_slot(lanes)]
    in_specs += [whole(a) for a in small] + [far] * 4
    if second:
        arrays += list(so_far)
        in_specs += [whole(a) for a in so_far[:3]] + [far]
    weight = jax.ShapeDtypeStruct((padded, width), F32)
    bias = jax.ShapeDtypeStruct((1, padded), F32)
    out_shape = [
        jax.ShapeDtypeStruct((2, HALF, width), F32),
        jax.ShapeDtypeStruct((2, HALF, width), F32),
        weight,
        weight,
        bias,
        jax.ShapeDtypeStruct((half if second else blocks, BLOCK, lanes), total_type),
        jax.ShapeDtypeStruct((half if second else dealt, BLOCK, lanes), BF16),
    ]
    out_specs = [out_slot(width), out_slot(width), whole(weight), whole(weight), whole(bias), far, far]
    return pl.pallas_call(
        functools.partial(attention_kernel, shape=shape, second=second),
        grid_spec=pltpu.PrefetchScalarGridSpec(
            num_scalar_prefetch=1,
            grid=(2,),
            in_specs=in_specs,
            out_specs=out_specs,
            scratch_shapes=[
                pltpu.VMEM((2 * rows, lanes), BF16),
                pltpu.VMEM((longest, BLOCK, rows), BF16),
                pltpu.VMEM((longest, rows), F32),
                pltpu.VMEM((longest, rows), F32),
                pltpu.VMEM((1, rows), F32),
                pltpu.VMEM((rows, lanes), F32),
                pltpu.VMEM((rows, lanes), F32),
                pltpu.VMEM((blocks, BLOCK, lanes), total_type),
                pltpu.VMEM((blocks, BLOCK, lanes), BF16),
                pltpu.VMEM((half if second and blocks <= 32 else 1, BLOCK, lanes), BF16),
                pltpu.VMEM((padded, width), BF16),
                pltpu.VMEM((padded, width), BF16),
                pltpu.SemaphoreType.DMA((5 + 2 * dealt,)),
            ],
        ),
        out_shape=out_shape,
        cost_estimate=pl.CostEstimate(
            flops=12_000_000_000, bytes_accessed=15_000_000, transcendentals=15_000_000
        ),
        compiler_params=pltpu.CompilerParams(
            vmem_limit_bytes=67_043_328 if blocks > 32 else VMEM
        ),
        name="attention",
    )(meta, *arrays)


ORDER = (0, 3, 1, 2)


def tables_kernel(meta_ref, cos_ref, sin_ref, *, shape):
    seq, row, col = meta_ref[0], meta_ref[1], meta_ref[2]
    lane = lax.broadcasted_iota(jnp.int32, (HALF, 2 * HD), 1)
    inside = lax.broadcasted_iota(jnp.int32, (HALF, 2 * HD), 0) + col * HALF
    half_rot = ROT // 2
    exponent = lax.rem(lane, half_rot).astype(F32) * (1.0 / half_rot)
    frequency = jnp.where(lane < ROT, 1.0 / jnp.exp(exponent * jnp.log(jnp.full_like(exponent, 10000.0))), 0.0)
    for i, slot in enumerate(ORDER):
        block = lax.bitwise_xor(seq, slot // 2) * shape.row_count + lax.bitwise_xor(row, slot % 2)
        start = (block - first_of(meta_ref, block, shape)) * BLOCK
        angles = (inside + start).astype(F32) * frequency
        cos_ref[i] = jnp.cos(angles)
        turned = jnp.sin(angles)
        sin_ref[i] = jnp.where(lane < half_rot, -turned, jnp.where(lane < ROT, turned, 0.0))


def tables(meta, shape):
    table = jax.ShapeDtypeStruct((4, HALF, 2 * HD), F32)
    return pl.pallas_call(
        functools.partial(tables_kernel, shape=shape),
        in_specs=[pl.BlockSpec(memory_space=pltpu.SMEM)],
        out_specs=[pl.BlockSpec(memory_space=pltpu.VMEM)] * 2,
        out_shape=[table, table],
        name="tables",
    )(meta)


def forward_kernel(
    both0_ref,
    both3_ref,
    both1_ref,
    both2_ref,
    vec_ref,
    small_ref,
    up0_ref,
    up1_ref,
    down0_ref,
    down1_ref,
    first_ref,
    dy_ref,
    out_ref,
    dx_ref,
    keep_ref,
    send_ref,
    stat_ref,
    x_ref,
    up_ref,
    down_ref,
    second_ref,
    hidden_ref,
    grad_ref,
    dys_ref,
    bias_ref,
):
    step = pl.program_id(0)
    span = up0_ref.shape[0]
    here = pl.ds(pl.multiple_of(step * HALF, HALF), HALF)

    @pl.when(step == 0)
    def _():
        up_ref[:span, :] = up0_ref[...]
        up_ref[span:, :] = up1_ref[...]
        down_ref[:, :span] = down0_ref[...]
        down_ref[:, span:] = down1_ref[...]
        bias_ref[...] = jnp.zeros_like(bias_ref)

    for i, piece in enumerate((both0_ref, both3_ref, both1_ref, both2_ref)):

        @pl.when(step == i)
        def _():
            x_ref[...] = piece[0]
            dys_ref[here, :] = piece[1]

    base = small_ref.shape[0] - 16
    bias = small_ref[base : base + 8, :].astype(F32) + small_ref[base + 8 :, :].astype(F32)
    upward_b = jnp.concatenate([bias[5:6], bias[6:7]], axis=1)
    wide = x_ref[...].astype(F32)
    mean = jnp.mean(wide, axis=1, keepdims=True)
    spread = jnp.mean(wide * wide, axis=1, keepdims=True) - mean * mean
    normed = (wide - mean) * lax.rsqrt(spread + EPS)
    first_ref[0] = (normed * vec_ref[0:1, :] + vec_ref[1:2, :]).astype(BF16)
    second = (normed * vec_ref[2:3, :] + vec_ref[3:4, :]).astype(BF16)
    dy = dys_ref[here, :]
    dy_ref[0] = dy
    second_ref[here, :] = second
    upward = dot(second, up_ref[...]) + upward_b
    bell = lax.erf(upward * (2.0**-0.5)) * 0.5 + 0.5
    hidden = (upward * bell).astype(BF16)
    slope = bell + upward * jnp.exp(upward * upward * -0.5) * ((2.0 * 3.141592653589793) ** -0.5)
    grad = dot(dy, down_ref[...], NT) * slope
    bias_ref[0:1, :] += jnp.sum(grad, axis=0, keepdims=True)
    grad = grad.astype(BF16)
    hidden_ref[here, :] = hidden
    grad_ref[here, :] = grad
    out_ref[0] = dot(hidden, down_ref[...])
    dx_ref[0] = dot(grad, up_ref[...], NT) * vec_ref[2:3, :]

    @pl.when(step == 3)
    def _():
        down_grad = dot(hidden_ref[...], dys_ref[...], TN)
        keep_ref[2 * span :, :] = down_grad[:, :span].astype(BF16)
        send_ref[2 * span :, :] = down_grad[:, span:].astype(BF16)
        up_grad = dot(second_ref[...], grad_ref[...], TN)
        for i in (0, 1):
            part = slice(i * span, (i + 1) * span)
            keep_ref[part, :] = up_grad[:span, part].astype(BF16)
            send_ref[part, :] = up_grad[span:, part].astype(BF16)
        weight = up_ref[...].astype(F32)
        bias_grad = bias_ref[0:1, :]

        def as_row(values):
            column = jnp.sum(values, axis=1, keepdims=True)
            return jnp.transpose(jnp.broadcast_to(column, (2 * span, 128)))[0:1, :]

        plain = as_row(weight * bias_grad)
        stat_ref[0:1, :] = (as_row(weight * up_grad) - vec_ref[3:4, :] * plain) / vec_ref[2:3, :]
        stat_ref[1:2, :] = plain
        stat_ref[2:3, :] = bias_grad
        stat_ref[3:8, :] = jnp.zeros((5, 2 * span), F32)


def feed_forward(both, vectors, small, up, down):
    width = vectors.shape[1]
    span = width // 2
    hidden = up[0].shape[1]

    def whole(array):
        return pl.BlockSpec(
            array.shape, lambda i: (0,) * len(array.shape), pipeline_mode=pl.Buffered(buffer_count=1)
        )

    slot = pl.BlockSpec((1, HALF, width), lambda i: (i, 0, 0))
    arrays = [*both, vectors, small, *up, *down]
    half = jax.ShapeDtypeStruct((2 * span + hidden, span), BF16)
    stat = jax.ShapeDtypeStruct((8, width), F32)
    tokens = lambda kind: jax.ShapeDtypeStruct((4, HALF, width), kind)
    return pl.pallas_call(
        forward_kernel,
        grid=(4,),
        in_specs=[whole(a) for a in arrays],
        out_specs=[slot] * 4 + [whole(half), whole(half), whole(stat)],
        out_shape=[tokens(BF16), tokens(BF16), tokens(F32), tokens(F32), half, half, stat],
        scratch_shapes=[
            pltpu.VMEM((HALF, width), BF16),
            pltpu.VMEM((width, hidden), BF16),
            pltpu.VMEM((hidden, width), BF16),
            pltpu.VMEM((4 * HALF, width), BF16),
            pltpu.VMEM((4 * HALF, hidden), BF16),
            pltpu.VMEM((4 * HALF, hidden), BF16),
            pltpu.VMEM((4 * HALF, width), BF16),
            pltpu.VMEM((8, hidden), F32),
        ],
        cost_estimate=pl.CostEstimate(
            flops=7_000_000_000, bytes_accessed=20_000_000, transcendentals=3_000_000
        ),
        compiler_params=pltpu.CompilerParams(vmem_limit_bytes=VMEM),
        name="feed_forward",
    )(*arrays)


def prologue_kernel(
    where_ref, tokens_ref, dy_ref, kvw_ref, qw_ref, ow_ref, vec_ref, pack_ref, x_ref, mine_ref, small_ref
):
    col = where_ref[2]
    span = dy_ref.shape[1]
    width = tokens_ref.shape[1]
    here = pl.ds(pl.multiple_of(col * HALF, HALF), HALF)
    there = pl.ds(pl.multiple_of((1 - col) * HALF, HALF), HALF)
    pack_ref[:HALF, :] = dy_ref[there, :]
    base = HALF + 2 * HD
    pack_ref[HALF:base, :] = jnp.transpose(kvw_ref[...].astype(F32)).astype(BF16)
    vectors = vec_ref[...]
    high = vectors.astype(BF16).astype(F32)
    both = jnp.concatenate([high, vectors - high], axis=0).astype(BF16)
    pack_ref[base:, :] = both
    x_ref[:, :span] = tokens_ref[here, pl.ds(pl.multiple_of(col * span, 128), span)]
    x_ref[:, span:] = tokens_ref[here, pl.ds(pl.multiple_of((1 - col) * span, 128), span)]
    mine_ref[...] = dy_ref[here, :]
    count = qw_ref.shape[0]
    small_ref[:count, :] = qw_ref[...]
    small_ref[count : 2 * count, :] = ow_ref[...]
    small_ref[2 * count :, :] = both


def prologue(col, tokens, cotangent, keyval_weight, query_weight, output_weight, vectors):
    width = tokens.shape[1]
    span = width // 2
    rows = vectors.shape[0]
    count = query_weight.shape[0]
    vmem = pl.BlockSpec(memory_space=pltpu.VMEM)
    return pl.pallas_call(
        prologue_kernel,
        in_specs=[pl.BlockSpec(memory_space=pltpu.SMEM)] + [vmem] * 6,
        out_specs=[vmem] * 4,
        out_shape=[
            jax.ShapeDtypeStruct((HALF + 2 * HD + 2 * rows, span), BF16),
            jax.ShapeDtypeStruct((HALF, width), BF16),
            jax.ShapeDtypeStruct((HALF, span), BF16),
            jax.ShapeDtypeStruct((2 * count + 2 * rows, span), BF16),
        ],
        name="prologue",
    )(col, tokens, cotangent, keyval_weight, query_weight, output_weight, vectors)


def own_kernel(
    x_ref, mine_ref, pack_ref, got_ref, vec_ref, cos_ref, sin_ref, bias_ref, pair_ref, both_ref, kvw_ref, full_ref
):
    span = mine_ref.shape[1]
    rows = vec_ref.shape[0]
    base = HALF + 2 * HD
    other = got_ref[base : base + 2 * rows, :].astype(F32)
    full = jnp.concatenate([vec_ref[...], other[:rows] + other[rows:]], axis=1)
    full_ref[...] = full
    both_ref[0] = x_ref[...]
    both_ref[1, :, :span] = mine_ref[...]
    both_ref[1, :, span:] = got_ref[:HALF, :]
    kvw_ref[:, :span] = pack_ref[HALF:base, :]
    kvw_ref[:, span:] = got_ref[HALF:base, :]
    wide = x_ref[...].astype(F32)
    mean = jnp.mean(wide, axis=1, keepdims=True)
    spread = jnp.mean(wide * wide, axis=1, keepdims=True) - mean * mean
    normed = (wide - mean) * lax.rsqrt(spread + EPS)
    first = (normed * full[0:1, :] + full[1:2, :]).astype(BF16)
    pre = dot(first, kvw_ref[...], NT) + bias_ref[...]
    lane = lax.broadcasted_iota(jnp.int32, pre.shape, 1)
    lanes = pre.shape[1]
    rolled = jnp.where(
        lane < ROT // 2, pltpu.roll(pre, lanes - ROT // 2, 1), pltpu.roll(pre, ROT // 2, 1)
    )
    pair_ref[0] = (pre * cos_ref[0] + rolled * sin_ref[0]).astype(BF16)


def own_pairs(x_own, mine, pack, got, vectors, cosine, sine, bias):
    width = x_own.shape[1]
    vmem = pl.BlockSpec(memory_space=pltpu.VMEM)
    return pl.pallas_call(
        own_kernel,
        in_specs=[vmem] * 8,
        out_specs=[vmem] * 4,
        out_shape=[
            jax.ShapeDtypeStruct((1, HALF, 2 * HD), BF16),
            jax.ShapeDtypeStruct((2, HALF, width), BF16),
            jax.ShapeDtypeStruct((2 * HD, width), BF16),
            jax.ShapeDtypeStruct((vectors.shape[0], width), F32),
        ],
        name="own_pairs",
    )(x_own, mine, pack, got, vectors, cosine, sine, bias)


def after(value, *others):
    return lax.optimization_barrier((value,) + others)[0]


def weights_over_col(partial):
    half = partial.shape[1] // 2
    received = swap(partial[:, half:].astype(BF16), "col", 1)
    return (partial[:, :half].astype(F32) + received.astype(F32)).astype(BF16)


def weights_over_rest(moved):
    core = lax.rem(lax.axis_index("seq"), 2)
    half = moved.shape[0] // 2
    keep = lax.dynamic_slice_in_dim(moved, core * half, half, 0).astype(F32)
    send = lax.dynamic_slice_in_dim(moved, (1 - core) * half, half, 0)
    total = keep + swap(send, "seq", 1).astype(F32)
    bit = 2
    while bit < lax.axis_size("seq"):
        total = swap_add(total, "seq", bit)
        bit = bit * 2
    total = total.astype(BF16)
    other = swap(total, "seq", 1)
    first = jnp.where(core == 0, total, other)
    second = jnp.where(core == 0, other, total)
    return jnp.concatenate([first, second], axis=0).astype(F32)


def on_device(
    tokens,
    cotangent,
    lengths,
    block_order,
    attention_gain,
    attention_shift,
    feedforward_gain,
    feedforward_shift,
    query_weight,
    query_bias,
    keyval_weight,
    keyval_bias,
    upward_weight,
    upward_bias,
    output_weight,
    output_bias,
    down_weight,
    down_bias,
):
    seq_count = lax.axis_size("seq")
    row_count = lax.axis_size("row")
    col_count = lax.axis_size("col")
    seq_me = lax.axis_index("seq")
    row_me = lax.axis_index("row")
    col_me = lax.axis_index("col")
    block_total = block_order.shape[0]
    width = tokens.shape[1]
    span = width // 2
    heads = query_weight.shape[1] // HD
    head_width = heads * HD
    pair_width = 2 * HD

    shape = Shape(seq_count, row_count, lengths.shape[0], heads)
    meta = jnp.concatenate(
        [jnp.stack([seq_me, row_me, col_me]).astype(jnp.int32), lengths, block_order]
    )

    vectors = jnp.concatenate(
        [
            attention_gain,
            attention_shift,
            feedforward_gain,
            feedforward_shift,
            output_bias + down_bias,
            upward_bias,
            query_bias,
            jnp.zeros((span - head_width,), F32),
        ]
    ).reshape(8, span)
    pack, x_own, dy_mine, small = prologue(
        meta, tokens, cotangent, keyval_weight, jnp.transpose(query_weight), output_weight, vectors
    )
    received = swap(pack, "col", 1)
    cosine, sine = tables(after(meta, pack), shape)
    half_rot = ROT // 2

    def norm(values):
        wide = values.astype(F32)
        mean = jnp.mean(wide, axis=-1, keepdims=True)
        spread = jnp.mean(wide * wide, axis=-1, keepdims=True) - mean * mean
        root = lax.rsqrt(spread + EPS)
        return (wide - mean) * root, root

    def turn(values, cosine, sine):
        rolled = jnp.concatenate(
            [
                values[:, half_rot:ROT],
                values[:, :half_rot],
                jnp.zeros((values.shape[0], pair_width - ROT), F32),
            ],
            axis=1,
        )
        return values * cosine + rolled * sine

    pairs, both, keyval_full, vec_full = own_pairs(
        x_own, dy_mine, pack, received, vectors, cosine, sine, keyval_bias[None]
    )
    gain_a, shift_a, gain_f, shift_f, bias_out = [vec_full[i][None] for i in range(5)]
    steps = [("row", 1), ("row", 2)]
    bit = 2
    while bit < seq_count:
        steps.append(("seq", bit))
        bit = bit * 2
    small_own = swap_odd_rows(small)
    up_own = swap_odd_rows(upward_weight)
    small_full = (small_own, swap(small_own, "col", 1))
    both_got = None
    for i, (axis, bit) in enumerate(steps):
        got = swap(pairs, axis, bit)
        if i == 0:
            both_got = swap(after(both, got), "row", 1)
            down_own = swap_odd_rows(after(down_weight, got))
        if i == 1:
            up_full = (up_own, swap(after(up_own, got), "col", 1))
        pairs = jnp.concatenate([pairs, got], axis=0)
    pairs_col = swap(pairs, "col", 1)
    pieces = (pairs, pairs_col, swap(pairs, "seq", 1), swap(pairs_col, "seq", 1))

    first_in, dy_all, ff_out, ff_grad, ff_keep, ff_send, ff_stats = feed_forward(
        (both, swap(both_got, "seq", 1), both_got, swap(both, "seq", 1)),
        vec_full,
        small_own,
        up_full,
        (down_own, swap(after(down_own, pairs_col), "col", 1)),
    )

    ff_got = swap(ff_send, "col", 1)
    ff_sum = (ff_keep.astype(F32) + ff_got.astype(F32)).astype(BF16)
    out_a, dx_a, dquery_w, doutput_w, dquery_b, dpairs, cache_rows = attention(
        after(meta, ff_send), first_in, dy_all, cosine, sine, small_full, pieces, None, shape
    )
    ff_moved = swap_odd_rows(ff_sum)
    out_b, dx_b, dquery_w, doutput_w, dquery_b, keep_pairs, send_pairs = attention(
        after(meta, ff_sum),
        first_in,
        dy_all,
        cosine,
        sine,
        small_full,
        pieces,
        (dquery_w, doutput_w, dquery_b, dpairs),
        shape,
    )

    total = keep_pairs.astype(F32) + swap(after(send_pairs, ff_moved), "seq", 1).astype(F32)
    first_total = total
    total = total[:, :HALF] + swap(total[:, HALF:].astype(BF16), "col", 1).astype(F32)
    col_total = total
    for axis, bit in reversed(steps[1:]):
        half = total.shape[0] // 2
        total = total[:half] + swap(total[half:].astype(BF16), axis, bit).astype(F32)
    own_total = total[0] + swap(total[1].astype(BF16), "row", 1).astype(F32)
    grad_pair = turn(
        total.reshape(2 * HALF, pair_width),
        jnp.concatenate([cosine[0], cosine[2]], axis=0),
        -jnp.concatenate([sine[0], sine[2]], axis=0),
    )
    grad_keyval = dot(grad_pair.astype(BF16), jnp.concatenate([first_in[0], first_in[2]], axis=0), TN)
    own_pair = turn(own_total, cosine[0], -sine[0]).astype(BF16)
    grad_first_kv = dot(own_pair, keyval_full)

    send = jnp.stack(
        [
            out_b[1] + ff_out[3],
            out_a[1] + ff_out[1],
            dx_b[1] * gain_a + ff_grad[3],
            dx_a[1] * gain_a + ff_grad[1],
        ]
    ).astype(BF16)
    got = swap(send, "seq", 1).astype(F32)
    away = jnp.stack(
        [out_b[0] + ff_out[2] + got[1], dx_b[0] * gain_a + ff_grad[2] + got[3]]
    ).astype(BF16)
    back = swap(after(away, col_total), "row", 1).astype(F32)
    out_one = out_a[0] + ff_out[0] + got[0] + back[0]
    grad_one = dx_a[0] * gain_a + ff_grad[0] + got[2] + back[1]
    x_wide = x_own.astype(F32)
    out_rows = (x_wide + out_one + bias_out).astype(BF16)
    grad_one = grad_one + grad_first_kv * gain_a
    normed_own, root_own = norm(x_own)
    moment_one = jnp.mean(grad_one, axis=1, keepdims=True)
    moment_two = jnp.mean(grad_one * normed_own, axis=1, keepdims=True)
    dy_own = dy_all[0]
    grad_rows = (
        dy_own.astype(F32) + root_own * (grad_one - moment_one - normed_own * moment_two)
    ).astype(BF16)

    def give(rows):
        mine = rows[:, :span]
        other = swap(rows[:, span:], "col", 1)
        return jnp.concatenate(
            [jnp.where(col_me == 0, mine, other), jnp.where(col_me == 0, other, mine)], axis=0
        )

    layer_out = give(out_rows)
    grad_tokens = give(grad_rows)

    sum_ff = weights_over_rest(ff_moved)
    sum_up = jnp.concatenate([sum_ff[:span], sum_ff[span : 2 * span]], axis=1)
    sum_down = sum_ff[2 * span :]
    bias_query = jnp.pad(dquery_b[:, :head_width], ((0, 0), (0, span - head_width)))
    bias_part = jnp.concatenate([ff_stats[2].reshape(2, span), bias_query], axis=0)
    bias_part = lax.reduce_precision(jnp.concatenate([bias_part, bias_part], axis=1), 8, 7)
    small_part = jnp.concatenate(
        [
            dquery_w[:head_width],
            doutput_w[:head_width],
            jnp.pad(bias_part, ((0, 29), (0, 0))),
        ],
        axis=0,
    )
    small_part = after(small_part, first_total)
    sum_small = weights_over_rest(swap_odd_rows(after(weights_over_col(small_part), col_total)))
    sum_query = jnp.transpose(sum_small[:head_width])
    sum_output = sum_small[head_width : 2 * head_width]
    base = 2 * head_width
    sum_bias_up = sum_small[base : base + 2].reshape(-1)
    sum_bias_query = sum_small[base + 2, :head_width]

    query_wide = jnp.concatenate([part[:head_width] for part in small_full], axis=1).astype(F32)
    keyval_wide = keyval_full.astype(F32)
    bias_q = dquery_b[0, :head_width][:, None]
    pair_bias = jnp.sum(grad_pair, axis=0)
    stat_a = (
        jnp.sum(query_wide * (dquery_w[:head_width] - bias_q * shift_a), axis=0)
        + jnp.sum(keyval_wide * (grad_keyval - pair_bias[:, None] * shift_a), axis=0)
    ) / gain_a[0]
    stat_as = jnp.sum(query_wide * bias_q, axis=0) + jnp.sum(keyval_wide * pair_bias[:, None], axis=0)
    stats = jnp.concatenate([stat_a[None], stat_as[None], ff_stats[:2]], axis=0)
    pair_row = jnp.pad(pair_bias[None], ((0, 0), (0, span - pair_width)))
    pair_row = lax.reduce_precision(pair_row, 8, 7)
    dy_sum = jnp.sum(cotangent.astype(F32), axis=0)[None]
    extra = jnp.concatenate(
        [
            grad_keyval,
            stats,
            jnp.concatenate([pair_row, pair_row], axis=1),
            jnp.concatenate([dy_sum, jnp.zeros_like(dy_sum)], axis=1),
            jnp.zeros((10, width), F32),
        ],
        axis=0,
    )
    extra = extra[:, :span] + swap(extra[:, span:].astype(BF16), "col", 1).astype(F32)
    bit = 1
    while bit < seq_count:
        extra = swap_add(extra, "seq", bit)
        bit = bit * 2
    for bit in (1, 2):
        extra = swap_add(extra, "row", bit)
    part = pair_width // row_count
    keyval_weight_out = jnp.transpose(lax.dynamic_slice_in_dim(extra, row_me * part, part, 0))
    keyval_bias_out = lax.dynamic_slice_in_dim(extra[pair_width + 4], row_me * part, part, 0)
    bias_out_grad = extra[pair_width + 5]
    cache_rows = cache_rows.reshape(-1, pair_width)

    return (
        layer_out,
        cache_rows,
        grad_tokens,
        extra[pair_width],
        extra[pair_width + 1],
        extra[pair_width + 2],
        extra[pair_width + 3],
        sum_query,
        sum_bias_query,
        keyval_weight_out,
        keyval_bias_out,
        sum_up,
        sum_bias_up,
        sum_output,
        bias_out_grad,
        sum_down,
        bias_out_grad,
    )


def solution(mesh):
    in_specs = (
        P(("seq", "row"), None),
        P(("seq", "row"), "col"),
        P(),
        P(),
        P("col"),
        P("col"),
        P("col"),
        P("col"),
        P("col", "row"),
        P("row"),
        P("col", None),
        P(),
        P("col", "row"),
        P("row"),
        P("row", "col"),
        P("col"),
        P("row", "col"),
        P("col"),
    )
    out_specs = (
        P(("seq", "row"), "col"),
        P(("seq", "col"), None),
        P(("seq", "row"), "col"),
        P("col"),
        P("col"),
        P("col"),
        P("col"),
        P("col", "row"),
        P("row"),
        P("col", "row"),
        P("row"),
        P("col", "row"),
        P("row"),
        P("row", "col"),
        P("col"),
        P("row", "col"),
        P("col"),
    )
    return jax.shard_map(
        on_device, mesh=mesh, in_specs=in_specs, out_specs=out_specs, check_vma=False
    )
```

time: 936 us -> 306 us (0.33)
  waiting for transfers between devices: 521 us -> 81.1 us
  matrix products: 64.9 us -> 3.14 us
  local copies, waits for them, and re-layouts: 92.2 us -> 31.3 us
  Pallas kernels: 0 us -> 60.3 us
  other arithmetic: 66.5 us -> 33.1 us
  blocking collectives: 30.9 us -> 0 us
  loops' own time: 24.9 us -> 0 us
  starting transfers between devices: 115 us -> 93.7 us
  between operations: 16.2 us -> 1.62 us
    all_gather x5 -> x0, waiting for transfers between devices: 205 us -> none  [the longest x1 58.3 us: on_device(): lax.all_gather(tokens, 'row', axis=0, tiled=True)]
    reduce_scatter x3 -> x0, waiting for transfers between devices: 153 us -> none  [the longest x1 95.6 us: on_device(): lax.psum_scatter(jnp.concatenate([jnp.dot(first_in, left_weight, preferre...]
    unnamed x11 -> x0, waiting for transfers between devices: 127 us -> none
    all_to_all x3 -> x0, starting transfers between devices: 114 us -> none  [the longest x2 110 us: deal(): lax.all_to_all(joined, ('seq', 'col'), split_axis=2, concat_axis=0, tiled...]
    ppermute x0 -> x40, starting transfers between devices: none -> 93.7 us  [the longest x35 88.9 us: swap(): return lax.ppermute(value, axis, [(i, i ^ bit) for i in range(count)])]
    ppermute x0 -> x40, waiting for transfers between devices: none -> 81.1 us  [the longest x35 81.1 us: swap(): return lax.ppermute(value, axis, [(i, i ^ bit) for i in range(count)])]
    dot_general x45 -> x2, matrix products: 64.9 us -> 3.14 us  [dot(): return lax.dot_general(left, right, dims, preferred_element_type=F32)]
    pallas_call x0 -> x6, Pallas kernels: none -> 60.3 us  [the longest x2 36.4 us: attention(): pl.pallas_call(functools.partial(attention_kernel, shape=shape, second=se...]
  transfers between devices with their start and end apart: 13 -> 40, of which waited for: 12 -> 16; matrix products, arithmetic and copies ran while one was open for 9% -> 19% of each run, Pallas kernels for 0% -> 19%
where the time goes in v1:
time: 306 us; the launch traced here: 304 us
  starting transfers between devices  93.7 us (31%)
  waiting for transfers between devices  81.1 us (27%)
  Pallas kernels  60.3 us (20%)
  other arithmetic  33.1 us (11%)
  local copies, waits for them, and re-layouts  31.3 us (10%)
  matrix products  3.14 us (1%)
    ppermute x35, starting transfers between devices, swap(): return lax.ppermute(value, axis, [(i, i ^ bit) for i in range(count)])  88.9 us
    ppermute x35, waiting for transfers between devices, swap(): return lax.ppermute(value, axis, [(i, i ^ bit) for i in range(count)])  81.1 us
    pallas_call x2, Pallas kernels, attention(): pl.pallas_call(functools.partial(attention_kernel, shape=shape, second=se...  36.4 us
    pallas_call x1, Pallas kernels, feed_forward(): pl.pallas_call(forward_kernel, grid=(4,), in_specs=[whole(a) for a in arr...  14.8 us
    unnamed x104, local copies, waits for them, and re-layouts  7.91 us
  transfers between devices with their start and end apart: 40, of which 16 were waited for; matrix products, arithmetic and copies ran while one was open for 19% of the time, Pallas kernels for 19%

profile of v1, /device:TPU:0, one launch (start us, length us, event | category | flops | bytes accessed | tf_op | source)
XLA Modules:
  0.0 304.4 jit_solution(15366981987439272430)
XLA Ops:
  4.1 2.4 prologue.1
  6.6 3.0 collective-permute-start
  11.0 3.6 %tables.1 = (f32[4,256,128]{2,1,0:T(8,128)}, f32[4,256,128]{2,1,0:T(8,128)}) custom-call(s32[22]{0:T(128)} %concatenate.77.where_ref.meta_ref), custom_call_target="tpu_custom_call" | custom-call | tf_op jit(solution)/shard_map/tables/pallas_call | solution.py:413
  14.6 2.5 collective-permute-done.got_ref
  17.8 3.1 %own_pairs.1 = (bf16[1,256,128]{2,1,0:T(8,128)(2,1)}, bf16[2,256,768]{2,1,0:T(8,128)(2,1)}, bf16[128,768]{1,0:T(8,128)(2,1)}, f32[8,768]{1,0:T(8,128)}) custom-call(bf16[256,768]{1,0:T(8,128)(2,1)} %get-tuple-element.59.x_ref, bf16[256,384]{1,0:T(8,128)(2,1)} %get-tuple-element.60.mine_ref, bf16[400,384]{1,0:T(8,128)(2,1)} %get-tuple-element.61.pack_ref, ...), custom_call_target="tpu_custom_call" | custom-call | tf_op jit(solution)/shard_map/own_pairs/pallas_call | solution.py:630
  20.9 1.8 collective-permute-start.1
  22.9 2.5 collective-permute-done.1
  26.2 11.7 %collective-permute-start.7 = (bf16[2,256,128]{2,1,0:T(8,128)(2,1)S(1)}, bf16[2,256,128]{2,1,0:T(8,128)(2,1)S(1)}, u32[]{:S(2)}, u32[]{:S(2)}) collective-permute-start(bf16[2,256,128]{2,1,0:T(8,128)(2,1)S(1)} %pad_maximum_fusion.9), channel_id=1, source_target_pairs={{0,4},{2,6},{4,0},{6,2},{1,5},{3,7},{5,1},{7,3},{8,12},{10,14},{12... | collective-permute-start | bytes 393224 | tf_op jit(solution)/shard_map/ppermute | solution.py:34
  38.5 2.4 collective-permute-start.2
  40.9 3.9 %collective-permute-done.7 = bf16[2,256,128]{2,1,0:T(8,128)(2,1)S(1)} collective-permute-done((bf16[2,256,128]{2,1,0:T(8,128)(2,1)S(1)}, bf16[2,256,128]{2,1,0:T(8,128)(2,1)S(1)}, u32[]{:S(2)}, u32[]{:S(2)}) %collective-permute-start.7) | collective-permute-done | bytes 131104 | tf_op jit(solution)/shard_map/ppermute | solution.py:34
  45.6 1.6 collective-permute-start.10
  47.2 1.5 constant_dynamic-update-slice_fusion.3
  50.8 2.7 collective-permute-done.10
  55.2 2.1 collective-permute-start.8
  57.3 8.8 %collective-permute-done.2.both1_ref = bf16[2,256,768]{2,1,0:T(8,128)(2,1)} collective-permute-done((bf16[2,256,768]{2,1,0:T(8,128)(2,1)}, bf16[2,256,768]{2,1,0:T(8,128)(2,1)}, u32[]{:S(2)}, u32[]{:S(2)}) %collective-permute-start.2) | collective-permute-done | bytes 786464 | tf_op jit(solution)/shard_map/ppermute | solution.py:34
  67.0 3.1 %collective-permute-done.11.kv1_ref = bf16[8,256,128]{2,1,0:T(8,128)(2,1)} collective-permute-done((bf16[8,256,128]{2,1,0:T(8,128)(2,1)}, bf16[8,256,128]{2,1,0:T(8,128)(2,1)}, u32[]{:S(2)}, u32[]{:S(2)}) %collective-permute-start.11) | collective-permute-done | bytes 524320 | tf_op jit(solution)/shard_map/ppermute | solution.py:34
  72.4 2.0 collective-permute-start.13
  74.4 8.3 %collective-permute-done.8.up1_ref = bf16[384,768]{1,0:T(8,128)(2,1)} collective-permute-done((bf16[384,768]{1,0:T(8,128)(2,1)S(1)}, bf16[384,768]{1,0:T(8,128)(2,1)}, u32[]{:S(2)}, u32[]{:S(2)}) %collective-permute-start.8) | collective-permute-done | bytes 589856 | tf_op jit(solution)/shard_map/ppermute | solution.py:34
  82.7 12.5 %collective-permute-done.12.down1_ref = bf16[768,384]{1,0:T(8,128)(2,1)S(1)} collective-permute-done((bf16[768,384]{1,0:T(8,128)(2,1)}, bf16[768,384]{1,0:T(8,128)(2,1)S(1)}, u32[]{:S(2)}, u32[]{:S(2)}) %collective-permute-start.12) | collective-permute-done | bytes 589856 | tf_op jit(solution)/shard_map/ppermute | solution.py:34
  96.1 14.8 %feed_forward.1 = (bf16[4,256,768]{2,1,0:T(8,128)(2,1)}, bf16[4,256,768]{2,1,0:T(8,128)(2,1)}, f32[4,256,768]{2,1,0:T(8,128)}, f32[4,256,768]{2,1,0:T(8,128)}, b...) custom-call(bf16[2,256,768]{2,1,0:T(8,128)(2,1)} %get-tuple-element.67.both0_ref, ...), custom_call_target="tpu_custom_call" | custom-call | flops 7000000000 | bytes 20000000 | tf_op jit(solution)/shard_map/feed_forward/pallas_call | solution.py:531
  111.0 1.5 slice_reduce_fusion.1
  115.3 17.7 %attention.2 = (f32[2,256,768]{2,1,0:T(8,128)}, f32[2,256,768]{2,1,0:T(8,128)}, f32[256,768]{1,0:T(8,128)}, f32[256,768]{1,0:T(8,128)}, f32[1,256]{1,0:T(1,128)}...) custom-call(s32[22]{0:T(128)} %concatenate.77.where_ref.meta_ref, ...), custom_call_target="tpu_custom_call" | custom-call | flops 12000000000 | bytes 15000000 | tf_op jit(solution)/shard_map/attention/pallas_call | solution.py:358
  133.0 5.4 %collective-permute-done.16 = bf16[1536,384]{1,0:T(8,128)(2,1)S(1)} collective-permute-done((bf16[1536,384]{1,0:T(8,128)(2,1)}, bf16[1536,384]{1,0:T(8,128)(2,1)S(1)}, u32[]{:S(2)}, u32[]{:S(2)}) %collective-permute-start.16) | collective-permute-done | bytes 1179680 | tf_op jit(solution)/shard_map/ppermute | solution.py:34
  138.7 1.7 collective-permute-start.18
  140.4 18.7 %attention.3 = (f32[2,256,768]{2,1,0:T(8,128)}, f32[2,256,768]{2,1,0:T(8,128)}, f32[256,768]{1,0:T(8,128)}, f32[256,768]{1,0:T(8,128)}, f32[1,256]{1,0:T(1,128)}...) custom-call(s32[22]{0:T(128)} %concatenate.77.where_ref.meta_ref, ...), custom_call_target="tpu_custom_call" | custom-call | flops 12000000000 | bytes 15000000 | tf_op jit(solution)/shard_map/attention/pallas_call | solution.py:358
  159.1 3.0 add_convert_fusion.3
  162.3 3.6 %collective-permute-start.17 = (bf16[4,256,768]{2,1,0:T(8,128)(2,1)S(1)}, bf16[4,256,768]{2,1,0:T(8,128)(2,1)}, u32[]{:S(2)}, u32[]{:S(2)}) collective-permute-start(bf16[4,256,768]{2,1,0:T(8,128)(2,1)S(1)} %pad_maximum_fusion), channel_id=1, source_target_pairs={{0,8},{8,0},{16,24},{24,16},{1,9},{9,1},{17,25},{25,17},{2,10},{10... | collective-permute-start | bytes 4718600 | tf_op jit(solution)/shard_map/ppermute | solution.py:34
  168.9 4.4 %collective-permute-start.37 = (bf16[768,384]{1,0:T(8,128)(2,1)}, bf16[768,384]{1,0:T(8,128)(2,1)}, u32[]{:S(2)}, u32[]{:S(2)}) collective-permute-start(bf16[768,384]{1,0:T(8,128)(2,1)} %constant_dynamic-slice_fusion), channel_id=1, source_target_pairs={{0,8},{8,0},{16,24},{24,16},{1,9},{9,1},{17,25},{25,17},{2,10},{10... | collective-permute-start | bytes 1769480 | tf_op jit(solution)/shard_map/ppermute | solution.py:34
  175.7 1.8 convert_element_type.151
  177.6 1.3 fusion
  178.9 16.1 %collective-permute-start.38 = (bf16[768,384]{1,0:T(8,128)(2,1)S(1)}, bf16[768,384]{1,0:T(8,128)(2,1)S(1)}, u32[]{:S(2)}, u32[]{:S(2)}) collective-permute-start(bf16[768,384]{1,0:T(8,128)(2,1)S(1)} %fusion), channel_id=1, source_target_pairs={{0,16},{8,24},{16,0},{24,8},{1,17},{9,25},{17,1},{25,9},{2,18},{10... | collective-permute-start | bytes 1769480 | tf_op jit(solution)/shard_map/ppermute | solution.py:34
  195.1 1.8 fusion.17
  197.2 1.6 collective-permute-start.20
  199.4 9.7 %collective-permute-done.38 = bf16[768,384]{1,0:T(8,128)(2,1)S(1)} collective-permute-done((bf16[768,384]{1,0:T(8,128)(2,1)S(1)}, bf16[768,384]{1,0:T(8,128)(2,1)S(1)}, u32[]{:S(2)}, u32[]{:S(2)}) %collective-permute-start.38) | collective-permute-done | bytes 589856 | tf_op jit(solution)/shard_map/ppermute | solution.py:34
  211.4 6.7 %collective-permute-done.32 = bf16[416,384]{1,0:T(8,128)(2,1)S(1)} collective-permute-done((bf16[416,384]{1,0:T(8,128)(2,1)S(1)}, bf16[416,384]{1,0:T(8,128)(2,1)S(1)}, u32[]{:S(2)}, u32[]{:S(2)}) %collective-permute-start.32) | collective-permute-done | bytes 319520 | tf_op jit(solution)/shard_map/ppermute | solution.py:34
  219.1 3.4 %collective-permute-start.21 = (bf16[2,256,768]{2,1,0:T(8,128)(2,1)}, bf16[2,256,768]{2,1,0:T(8,128)(2,1)}, u32[]{:S(2)}, u32[]{:S(2)}) collective-permute-start(bf16[2,256,768]{2,1,0:T(8,128)(2,1)} %pad_maximum_fusion.2), channel_id=1, source_target_pairs={{0,2},{2,0},{4,6},{6,4},{1,3},{3,1},{5,7},{7,5},{8,10},{10,8},{12,... | collective-permute-start | bytes 2359304 | tf_op jit(solution)/shard_map/ppermute | solution.py:34
  226.2 8.7 %collective-permute-start.24 = (bf16[2,256,128]{2,1,0:T(8,128)(2,1)S(1)}, bf16[2,256,128]{2,1,0:T(8,128)(2,1)S(1)}, u32[]{:S(2)}, u32[]{:S(2)}) collective-permute-start(bf16[2,256,128]{2,1,0:T(8,128)(2,1)S(1)} %slice.428), channel_id=1, source_target_pairs={{0,4},{2,6},{4,0},{6,2},{1,5},{3,7},{5,1},{7,3},{8,12},{10,14},{12... | collective-permute-start | bytes 393224 | tf_op jit(solution)/shard_map/ppermute | solution.py:34
  235.6 9.2 %collective-permute-start.34 = (bf16[208,384]{1,0:T(8,128)(2,1)}, bf16[208,384]{1,0:T(8,128)(2,1)}, u32[]{:S(2)}, u32[]{:S(2)}) collective-permute-start(bf16[208,384]{1,0:T(8,128)(2,1)} %constant_dynamic-slice_fusion.2), channel_id=1, source_target_pairs={{0,8},{8,0},{16,24},{24,16},{1,9},{9,1},{17,25},{25,17},{2,10},{10... | collective-permute-start | bytes 479240 | tf_op jit(solution)/shard_map/ppermute | solution.py:34
  245.6 9.0 %collective-permute-start.25 = (bf16[256,128]{1,0:T(8,128)(2,1)}, bf16[256,128]{1,0:T(8,128)(2,1)}, u32[]{:S(2)}, u32[]{:S(2)}) collective-permute-start(bf16[256,128]{1,0:T(8,128)(2,1)} %fusion.41), channel_id=1, source_target_pairs={{0,2},{2,0},{4,6},{6,4},{1,3},{3,1},{5,7},{7,5},{8,10},{10,8},{12,... | collective-permute-start | bytes 196616 | tf_op jit(solution)/shard_map/ppermute | solution.py:34
  256.1 1.3 reshape_divide_fusion
  258.7 4.5 %concatenate.96 = f32[144,768]{1,0:T(8,128)} concatenate(f32[128,768]{1,0:T(8,128)} %get-tuple-element.152, f32[1,768]{1,0:T(1,128)} %reshape_divide_fusion, f32[1,768]{1,0:T(1,128)S(1)} %add.233, f32[2,768]{1,0:T(2,128)S(1)} %slice.278, f32[1,768]{1,0:T(1,128)} %pad_maximum_fusion.10, f32[1,768]{1,0:T(1,128)} %concatenate.95, f32[10,768]{1,0:T(8,128)} %broadcast_in_dim.39), dimensions={0} | concatenate | bytes 884736 | tf_op jit(solution)/shard_map/concatenate | solution.py:884
  264.2 1.7 collective-permute-start.27
  266.9 2.6 collective-permute-done.27
  273.8 4.8 %collective-permute-done.35 = bf16[208,384]{1,0:T(8,128)(2,1)S(1)} collective-permute-done((bf16[208,384]{1,0:T(8,128)(2,1)S(1)}, bf16[208,384]{1,0:T(8,128)(2,1)S(1)}, u32[]{:S(2)}, u32[]{:S(2)}) %collective-permute-start.35) | collective-permute-done | bytes 159776 | tf_op jit(solution)/shard_map/ppermute | solution.py:34
  282.9 2.0 fusion.48
  285.0 1.8 fusion.11
  286.8 1.7 collective-permute-start.22
  292.8 6.5 %collective-permute-done.31 = bf16[144,384]{1,0:T(8,128)(2,1)S(1)} collective-permute-done((bf16[144,384]{1,0:T(8,128)(2,1)S(1)}, bf16[144,384]{1,0:T(8,128)(2,1)S(1)}, u32[]{:S(2)}, u32[]{:S(2)}) %collective-permute-start.31) | collective-permute-done | bytes 110624 | tf_op jit(solution)/shard_map/ppermute | solution.py:34
  (242 shorter events, 56.2 us)
Async XLA Ops:
  6.6 10.5 %collective-permute-start = (bf16[400,384]{1,0:T(8,128)(2,1)}, bf16[400,384]{1,0:T(8,128)(2,1)S(1)}, u32[]{:S(2)}, u32[]{:S(2)}) collective-permute-start(bf16[400,384]{1,0:T(8,128)(2,1)} %get-tuple-element.61.pack_ref), channel_id=1, source_target_pairs={{0,1},{1,0},{2,3},{3,2},{4,5},{5,4},{6,7},{7,6},{8,9},{9,8},{10,11... | collective-permute-start | bytes 921608 | tf_op jit(solution)/shard_map/ppermute | solution.py:34
  9.6 62.7 %collective-permute-start.5 = (bf16[400,384]{1,0:T(8,128)(2,1)}, bf16[400,384]{1,0:T(8,128)(2,1)S(1)}, u32[]{:S(2)}, u32[]{:S(2)}) collective-permute-start(bf16[400,384]{1,0:T(8,128)(2,1)} %get-tuple-element.69), channel_id=1, source_target_pairs={{8,12},{10,14},{12,8},{14,10},{24,28},{26,30},{28,24},{30,26},{9,1... | collective-permute-start | bytes 921608 | tf_op jit(solution)/shard_map/ppermute | solution.py:43
  10.3 43.9 %collective-permute-start.6 = (bf16[384,768]{1,0:T(8,128)(2,1)S(1)}, bf16[384,768]{1,0:T(8,128)(2,1)S(1)}, u32[]{:S(2)}, u32[]{:S(2)}) collective-permute-start(bf16[384,768]{1,0:T(8,128)(2,1)S(1)} %copy-done.24), channel_id=1, source_target_pairs={{8,12},{10,14},{12,8},{14,10},{24,28},{26,30},{28,24},{30,26},{9,1... | collective-permute-start | bytes 1769480 | tf_op jit(solution)/shard_map/ppermute | solution.py:43
  17.8 30.8 %copy-start.25 = (bf16[768,384]{1,0:T(8,128)(2,1)S(1)}, bf16[768,384]{1,0:T(8,128)(2,1)}, u32[]{:S(2)}) copy-start(bf16[768,384]{1,0:T(8,128)(2,1)} %param.34) | copy-start | bytes 1769476
  20.9 4.5 %collective-permute-start.1 = (bf16[1,256,128]{2,1,0:T(8,128)(2,1)}, bf16[1,256,128]{2,1,0:T(8,128)(2,1)S(1)}, u32[]{:S(2)}, u32[]{:S(2)}) collective-permute-start(bf16[1,256,128]{2,1,0:T(8,128)(2,1)} %get-tuple-element.66), channel_id=1, source_target_pairs={{0,2},{2,0},{4,6},{6,4},{1,3},{3,1},{5,7},{7,5},{8,10},{10,8},{12,... | collective-permute-start | bytes 196616 | tf_op jit(solution)/shard_map/ppermute | solution.py:34
  26.2 18.5 %collective-permute-start.7 = (bf16[2,256,128]{2,1,0:T(8,128)(2,1)S(1)}, bf16[2,256,128]{2,1,0:T(8,128)(2,1)S(1)}, u32[]{:S(2)}, u32[]{:S(2)}) collective-permute-start(bf16[2,256,128]{2,1,0:T(8,128)(2,1)S(1)} %pad_maximum_fusion.9), channel_id=1, source_target_pairs={{0,4},{2,6},{4,0},{6,2},{1,5},{3,7},{5,1},{7,3},{8,12},{10,14},{12... | collective-permute-start | bytes 393224 | tf_op jit(solution)/shard_map/ppermute | solution.py:34
  38.5 27.6 %collective-permute-start.2 = (bf16[2,256,768]{2,1,0:T(8,128)(2,1)}, bf16[2,256,768]{2,1,0:T(8,128)(2,1)}, u32[]{:S(2)}, u32[]{:S(2)}) collective-permute-start(bf16[2,256,768]{2,1,0:T(8,128)(2,1)} %get-tuple-element.67.both0_ref), channel_id=1, source_target_pairs={{0,2},{2,0},{4,6},{6,4},{1,3},{3,1},{5,7},{7,5},{8,10},{10,8},{12,... | collective-permute-start | bytes 2359304 | tf_op jit(solution)/shard_map/ppermute | solution.py:34
  45.6 7.9 %collective-permute-start.10 = (bf16[4,256,128]{2,1,0:T(8,128)(2,1)S(1)}, bf16[4,256,128]{2,1,0:T(8,128)(2,1)S(1)}, u32[]{:S(2)}, u32[]{:S(2)}) collective-permute-start(bf16[4,256,128]{2,1,0:T(8,128)(2,1)S(1)} %pad_maximum_fusion.7), channel_id=1, source_target_pairs={{0,16},{8,24},{16,0},{24,8},{1,17},{9,25},{17,1},{25,9},{2,18},{10... | collective-permute-start | bytes 786440 | tf_op jit(solution)/shard_map/ppermute | solution.py:34
  48.6 6.5 %collective-permute-start.9 = (bf16[768,384]{1,0:T(8,128)(2,1)S(1)}, bf16[768,384]{1,0:T(8,128)(2,1)S(1)}, u32[]{:S(2)}, u32[]{:S(2)}) collective-permute-start(bf16[768,384]{1,0:T(8,128)(2,1)S(1)} %copy-done.25), channel_id=1, source_target_pairs={{8,12},{10,14},{12,8},{14,10},{24,28},{26,30},{28,24},{30,26},{9,1... | collective-permute-start | bytes 1769480 | tf_op jit(solution)/shard_map/ppermute | solution.py:43
  53.5 20.9 %collective-permute-start.4 = (bf16[2,256,768]{2,1,0:T(8,128)(2,1)}, bf16[2,256,768]{2,1,0:T(8,128)(2,1)}, u32[]{:S(2)}, u32[]{:S(2)}) collective-permute-start(bf16[2,256,768]{2,1,0:T(8,128)(2,1)} %get-tuple-element.67.both0_ref), channel_id=1, source_target_pairs={{0,8},{8,0},{16,24},{24,16},{1,9},{9,1},{17,25},{25,17},{2,10},{10... | collective-permute-start | bytes 2359304 | tf_op jit(solution)/shard_map/ppermute | solution.py:34
  55.1 15.0 %collective-permute-start.11 = (bf16[8,256,128]{2,1,0:T(8,128)(2,1)}, bf16[8,256,128]{2,1,0:T(8,128)(2,1)}, u32[]{:S(2)}, u32[]{:S(2)}) collective-permute-start(bf16[8,256,128]{2,1,0:T(8,128)(2,1)} %constant_dynamic-update-slice_fusion.kv0_ref), channel_id=1, source_target_pairs={{0,1},{1,0},{2,3},{3,2},{4,5},{5,4},{6,7},{7,6},{8,9},{9,8},{10,11... | collective-permute-start | bytes 1572872 | tf_op jit(solution)/shard_map/ppermute | solution.py:34
  55.2 27.6 %collective-permute-start.8 = (bf16[384,768]{1,0:T(8,128)(2,1)S(1)}, bf16[384,768]{1,0:T(8,128)(2,1)}, u32[]{:S(2)}, u32[]{:S(2)}) collective-permute-start(bf16[384,768]{1,0:T(8,128)(2,1)S(1)} %broadcast_select_fusion.4.up0_ref), channel_id=1, source_target_pairs={{0,1},{1,0},{2,3},{3,2},{4,5},{5,4},{6,7},{7,6},{8,9},{9,8},{10,11... | collective-permute-start | bytes 1769480 | tf_op jit(solution)/shard_map/ppermute | solution.py:34
  66.0 29.2 %collective-permute-start.3 = (bf16[2,256,768]{2,1,0:T(8,128)(2,1)}, bf16[2,256,768]{2,1,0:T(8,128)(2,1)}, u32[]{:S(2)}, u32[]{:S(2)}) collective-permute-start(bf16[2,256,768]{2,1,0:T(8,128)(2,1)} %collective-permute-done.2.both1_ref), channel_id=1, source_target_pairs={{0,8},{8,0},{16,24},{24,16},{1,9},{9,1},{17,25},{25,17},{2,10},{10... | collective-permute-start | bytes 2359304 | tf_op jit(solution)/shard_map/ppermute | solution.py:34
  70.1 25.2 %collective-permute-start.12 = (bf16[768,384]{1,0:T(8,128)(2,1)}, bf16[768,384]{1,0:T(8,128)(2,1)S(1)}, u32[]{:S(2)}, u32[]{:S(2)}) collective-permute-start(bf16[768,384]{1,0:T(8,128)(2,1)} %broadcast_select_fusion.3.down0_ref), channel_id=1, source_target_pairs={{0,1},{1,0},{2,3},{3,2},{4,5},{5,4},{6,7},{7,6},{8,9},{9,8},{10,11... | collective-permute-start | bytes 1769480 | tf_op jit(solution)/shard_map/ppermute | solution.py:34
  72.4 22.9 %copy-start.22 = (bf16[400,384]{1,0:T(8,128)(2,1)}, bf16[400,384]{1,0:T(8,128)(2,1)S(1)}, u32[]{:S(2)}) copy-start(bf16[400,384]{1,0:T(8,128)(2,1)S(1)} %broadcast_select_fusion.6.small_ref.small0_ref) | copy-start | bytes 921604
  72.4 41.1 %collective-permute-start.13 = (bf16[400,384]{1,0:T(8,128)(2,1)S(1)}, bf16[400,384]{1,0:T(8,128)(2,1)S(1)}, u32[]{:S(2)}, u32[]{:S(2)}) collective-permute-start(bf16[400,384]{1,0:T(8,128)(2,1)S(1)} %broadcast_select_fusion.6.small_ref.small0_ref), channel_id=1, source_target_pairs={{0,1},{1,0},{2,3},{3,2},{4,5},{5,4},{6,7},{7,6},{8,9},{9,8},{10,11... | collective-permute-start | bytes 921608 | tf_op jit(solution)/shard_map/ppermute | solution.py:34
  74.4 39.8 %collective-permute-start.14 = (bf16[8,256,128]{2,1,0:T(8,128)(2,1)}, bf16[8,256,128]{2,1,0:T(8,128)(2,1)S(1)}, u32[]{:S(2)}, u32[]{:S(2)}) collective-permute-start(bf16[8,256,128]{2,1,0:T(8,128)(2,1)} %constant_dynamic-update-slice_fusion.kv0_ref), channel_id=1, source_target_pairs={{0,8},{8,0},{16,24},{24,16},{1,9},{9,1},{17,25},{25,17},{2,10},{10... | collective-permute-start | bytes 1572872 | tf_op jit(solution)/shard_map/ppermute | solution.py:34
  82.7 31.5 %collective-permute-start.15 = (bf16[8,256,128]{2,1,0:T(8,128)(2,1)}, bf16[8,256,128]{2,1,0:T(8,128)(2,1)S(1)}, u32[]{:S(2)}, u32[]{:S(2)}) collective-permute-start(bf16[8,256,128]{2,1,0:T(8,128)(2,1)} %collective-permute-done.11.kv1_ref), channel_id=1, source_target_pairs={{0,8},{8,0},{16,24},{24,16},{1,9},{9,1},{17,25},{25,17},{2,10},{10... | collective-permute-start | bytes 1572872 | tf_op jit(solution)/shard_map/ppermute | solution.py:34
  110.9 27.5 %collective-permute-start.16 = (bf16[1536,384]{1,0:T(8,128)(2,1)}, bf16[1536,384]{1,0:T(8,128)(2,1)S(1)}, u32[]{:S(2)}, u32[]{:S(2)}) collective-permute-start(bf16[1536,384]{1,0:T(8,128)(2,1)} %get-tuple-element.73), channel_id=1, source_target_pairs={{0,1},{1,0},{2,3},{3,2},{4,5},{5,4},{6,7},{7,6},{8,9},{9,8},{10,11... | collective-permute-start | bytes 3538952 | tf_op jit(solution)/shard_map/ppermute | solution.py:34
  115.3 23.1 %copy-start.21 = (bf16[1536,384]{1,0:T(8,128)(2,1)S(1)}, bf16[1536,384]{1,0:T(8,128)(2,1)}, u32[]{:S(2)}) copy-start(bf16[1536,384]{1,0:T(8,128)(2,1)} %get-tuple-element.79) | copy-start | bytes 3538948
  138.7 28.2 %collective-permute-start.18 = (bf16[1536,384]{1,0:T(8,128)(2,1)S(1)}, bf16[1536,384]{1,0:T(8,128)(2,1)}, u32[]{:S(2)}, u32[]{:S(2)}) collective-permute-start(bf16[1536,384]{1,0:T(8,128)(2,1)S(1)} %add_convert_fusion), channel_id=1, source_target_pairs={{8,12},{10,14},{12,8},{14,10},{24,28},{26,30},{28,24},{30,26},{9,1... | collective-permute-start | bytes 3538952 | tf_op jit(solution)/shard_map/ppermute | solution.py:43
  162.3 13.4 %collective-permute-start.17 = (bf16[4,256,768]{2,1,0:T(8,128)(2,1)S(1)}, bf16[4,256,768]{2,1,0:T(8,128)(2,1)}, u32[]{:S(2)}, u32[]{:S(2)}) collective-permute-start(bf16[4,256,768]{2,1,0:T(8,128)(2,1)S(1)} %pad_maximum_fusion), channel_id=1, source_target_pairs={{0,8},{8,0},{16,24},{24,16},{1,9},{9,1},{17,25},{25,17},{2,10},{10... | collective-permute-start | bytes 4718600 | tf_op jit(solution)/shard_map/ppermute | solution.py:34
  168.9 8.6 %collective-permute-start.37 = (bf16[768,384]{1,0:T(8,128)(2,1)}, bf16[768,384]{1,0:T(8,128)(2,1)}, u32[]{:S(2)}, u32[]{:S(2)}) collective-permute-start(bf16[768,384]{1,0:T(8,128)(2,1)} %constant_dynamic-slice_fusion), channel_id=1, source_target_pairs={{0,8},{8,0},{16,24},{24,16},{1,9},{9,1},{17,25},{25,17},{2,10},{10... | collective-permute-start | bytes 1769480 | tf_op jit(solution)/shard_map/ppermute | solution.py:34
  174.2 22.7 %collective-permute-start.19 = (bf16[8,512,128]{2,1,0:T(8,128)(2,1)}, bf16[8,512,128]{2,1,0:T(8,128)(2,1)S(1)}, u32[]{:S(2)}, u32[]{:S(2)}) collective-permute-start(bf16[8,512,128]{2,1,0:T(8,128)(2,1)} %get-tuple-element.91), channel_id=1, source_target_pairs={{0,8},{8,0},{16,24},{24,16},{1,9},{9,1},{17,25},{25,17},{2,10},{10... | collective-permute-start | bytes 3145736 | tf_op jit(solution)/shard_map/ppermute | solution.py:34
  178.9 30.1 %collective-permute-start.38 = (bf16[768,384]{1,0:T(8,128)(2,1)S(1)}, bf16[768,384]{1,0:T(8,128)(2,1)S(1)}, u32[]{:S(2)}, u32[]{:S(2)}) collective-permute-start(bf16[768,384]{1,0:T(8,128)(2,1)S(1)} %fusion), channel_id=1, source_target_pairs={{0,16},{8,24},{16,0},{24,8},{1,17},{9,25},{17,1},{25,9},{2,18},{10... | collective-permute-start | bytes 1769480 | tf_op jit(solution)/shard_map/ppermute | solution.py:34
  197.2 21.0 %collective-permute-start.20 = (bf16[8,256,128]{2,1,0:T(8,128)(2,1)S(1)}, bf16[8,256,128]{2,1,0:T(8,128)(2,1)S(1)}, u32[]{:S(2)}, u32[]{:S(2)}) collective-permute-start(bf16[8,256,128]{2,1,0:T(8,128)(2,1)S(1)} %slice.425), channel_id=1, source_target_pairs={{0,1},{1,0},{2,3},{3,2},{4,5},{5,4},{6,7},{7,6},{8,9},{9,8},{10,11... | collective-permute-start | bytes 1572872 | tf_op jit(solution)/shard_map/ppermute | solution.py:34
  198.8 19.3 %collective-permute-start.32 = (bf16[416,384]{1,0:T(8,128)(2,1)S(1)}, bf16[416,384]{1,0:T(8,128)(2,1)S(1)}, u32[]{:S(2)}, u32[]{:S(2)}) collective-permute-start(bf16[416,384]{1,0:T(8,128)(2,1)S(1)} %slice.426), channel_id=1, source_target_pairs={{0,1},{1,0},{2,3},{3,2},{4,5},{5,4},{6,7},{7,6},{8,9},{9,8},{10,11... | collective-permute-start | bytes 958472 | tf_op jit(solution)/shard_map/ppermute | solution.py:34
  210.4 13.0 %collective-permute-start.39 = (bf16[768,384]{1,0:T(8,128)(2,1)S(1)}, bf16[768,384]{1,0:T(8,128)(2,1)S(1)}, u32[]{:S(2)}, u32[]{:S(2)}) collective-permute-start(bf16[768,384]{1,0:T(8,128)(2,1)S(1)} %add_convert_fusion.1), channel_id=1, source_target_pairs={{0,8},{8,0},{16,24},{24,16},{1,9},{9,1},{17,25},{25,17},{2,10},{10... | collective-permute-start | bytes 1769480 | tf_op jit(solution)/shard_map/ppermute | solution.py:34
  218.4 7.7 %collective-permute-start.23 = (bf16[4,256,128]{2,1,0:T(8,128)(2,1)S(1)}, bf16[4,256,128]{2,1,0:T(8,128)(2,1)S(1)}, u32[]{:S(2)}, u32[]{:S(2)}) collective-permute-start(bf16[4,256,128]{2,1,0:T(8,128)(2,1)S(1)} %slice.427), channel_id=1, source_target_pairs={{0,16},{8,24},{16,0},{24,8},{1,17},{9,25},{17,1},{25,9},{2,18},{10... | collective-permute-start | bytes 786440 | tf_op jit(solution)/shard_map/ppermute | solution.py:34
  219.1 62.5 %collective-permute-start.21 = (bf16[2,256,768]{2,1,0:T(8,128)(2,1)}, bf16[2,256,768]{2,1,0:T(8,128)(2,1)}, u32[]{:S(2)}, u32[]{:S(2)}) collective-permute-start(bf16[2,256,768]{2,1,0:T(8,128)(2,1)} %pad_maximum_fusion.2), channel_id=1, source_target_pairs={{0,2},{2,0},{4,6},{6,4},{1,3},{3,1},{5,7},{7,5},{8,10},{10,8},{12,... | collective-permute-start | bytes 2359304 | tf_op jit(solution)/shard_map/ppermute | solution.py:34
  222.5 12.3 %collective-permute-start.33 = (bf16[416,384]{1,0:T(8,128)(2,1)S(1)}, bf16[416,384]{1,0:T(8,128)(2,1)S(1)}, u32[]{:S(2)}, u32[]{:S(2)}) collective-permute-start(bf16[416,384]{1,0:T(8,128)(2,1)S(1)} %add_convert_fusion.6), channel_id=1, source_target_pairs={{8,12},{10,14},{12,8},{14,10},{24,28},{26,30},{28,24},{30,26},{9,1... | collective-permute-start | bytes 958472 | tf_op jit(solution)/shard_map/ppermute | solution.py:43
  226.1 28.7 %copy-start.28 = (f32[256,128]{1,0:T(8,128)S(1)}, f32[256,128]{1,0:T(8,128)}, u32[]{:S(2)}) copy-start(f32[256,128]{1,0:T(8,128)} %get-tuple-element.136) | copy-start | bytes 393220
  226.1 28.7 %copy-start.29 = (f32[256,128]{1,0:T(8,128)S(1)}, f32[256,128]{1,0:T(8,128)}, u32[]{:S(2)}) copy-start(f32[256,128]{1,0:T(8,128)} %get-tuple-element.137) | copy-start | bytes 393220
  226.1 28.7 %copy-start.30 = (f32[256,128]{1,0:T(8,128)S(1)}, f32[256,128]{1,0:T(8,128)}, u32[]{:S(2)}) copy-start(f32[256,128]{1,0:T(8,128)} %get-tuple-element.153) | copy-start | bytes 393220
  226.1 28.7 %copy-start.31 = (f32[256,128]{1,0:T(8,128)S(1)}, f32[256,128]{1,0:T(8,128)}, u32[]{:S(2)}) copy-start(f32[256,128]{1,0:T(8,128)} %get-tuple-element.154) | copy-start | bytes 393220
  226.1 28.7 %copy-start.45 = (f32[128]{0:T(128)S(1)}, f32[128]{0:T(128)}, u32[]{:S(2)}) copy-start(f32[128]{0:T(128)} %pad.49.clone) | copy-start | bytes 1540
  226.2 18.7 %collective-permute-start.24 = (bf16[2,256,128]{2,1,0:T(8,128)(2,1)S(1)}, bf16[2,256,128]{2,1,0:T(8,128)(2,1)S(1)}, u32[]{:S(2)}, u32[]{:S(2)}) collective-permute-start(bf16[2,256,128]{2,1,0:T(8,128)(2,1)S(1)} %slice.428), channel_id=1, source_target_pairs={{0,4},{2,6},{4,0},{6,2},{1,5},{3,7},{5,1},{7,3},{8,12},{10,14},{12... | collective-permute-start | bytes 393224 | tf_op jit(solution)/shard_map/ppermute | solution.py:34
  235.6 35.0 %collective-permute-start.34 = (bf16[208,384]{1,0:T(8,128)(2,1)}, bf16[208,384]{1,0:T(8,128)(2,1)}, u32[]{:S(2)}, u32[]{:S(2)}) collective-permute-start(bf16[208,384]{1,0:T(8,128)(2,1)} %constant_dynamic-slice_fusion.2), channel_id=1, source_target_pairs={{0,8},{8,0},{16,24},{24,16},{1,9},{9,1},{17,25},{25,17},{2,10},{10... | collective-permute-start | bytes 479240 | tf_op jit(solution)/shard_map/ppermute | solution.py:34
  245.6 20.3 %collective-permute-start.25 = (bf16[256,128]{1,0:T(8,128)(2,1)}, bf16[256,128]{1,0:T(8,128)(2,1)}, u32[]{:S(2)}, u32[]{:S(2)}) collective-permute-start(bf16[256,128]{1,0:T(8,128)(2,1)} %fusion.41), channel_id=1, source_target_pairs={{0,2},{2,0},{4,6},{6,4},{1,3},{3,1},{5,7},{7,5},{8,10},{10,8},{12,... | collective-permute-start | bytes 196616 | tf_op jit(solution)/shard_map/ppermute | solution.py:34
  264.2 5.3 %collective-permute-start.27 = (bf16[144,384]{1,0:T(8,128)(2,1)S(1)}, bf16[144,384]{1,0:T(8,128)(2,1)S(1)}, u32[]{:S(2)}, u32[]{:S(2)}) collective-permute-start(bf16[144,384]{1,0:T(8,128)(2,1)S(1)} %slice.429), channel_id=1, source_target_pairs={{0,1},{1,0},{2,3},{3,2},{4,5},{5,4},{6,7},{7,6},{8,9},{9,8},{10,11... | collective-permute-start | bytes 331784 | tf_op jit(solution)/shard_map/ppermute | solution.py:34
  270.5 2.2 collective-permute-start.28
  271.6 7.0 %collective-permute-start.35 = (bf16[208,384]{1,0:T(8,128)(2,1)S(1)}, bf16[208,384]{1,0:T(8,128)(2,1)S(1)}, u32[]{:S(2)}, u32[]{:S(2)}) collective-permute-start(bf16[208,384]{1,0:T(8,128)(2,1)S(1)} %fusion.27), channel_id=1, source_target_pairs={{0,16},{8,24},{16,0},{24,8},{1,17},{9,25},{17,1},{25,9},{2,18},{10... | collective-permute-start | bytes 479240 | tf_op jit(solution)/shard_map/ppermute | solution.py:34
  272.8 7.8 %collective-permute-start.29 = (bf16[144,384]{1,0:T(8,128)(2,1)S(1)}, bf16[144,384]{1,0:T(8,128)(2,1)S(1)}, u32[]{:S(2)}, u32[]{:S(2)}) collective-permute-start(bf16[144,384]{1,0:T(8,128)(2,1)S(1)} %fusion.33), channel_id=1, source_target_pairs={{0,16},{8,24},{16,0},{24,8},{1,17},{9,25},{17,1},{25,9},{2,18},{10... | collective-permute-start | bytes 331784 | tf_op jit(solution)/shard_map/ppermute | solution.py:34
  279.6 9.4 %collective-permute-start.36 = (bf16[208,384]{1,0:T(8,128)(2,1)S(1)}, bf16[208,384]{1,0:T(8,128)(2,1)S(1)}, u32[]{:S(2)}, u32[]{:S(2)}) collective-permute-start(bf16[208,384]{1,0:T(8,128)(2,1)S(1)} %add_convert_fusion.7), channel_id=1, source_target_pairs={{0,8},{8,0},{16,24},{24,16},{1,9},{9,1},{17,25},{25,17},{2,10},{10... | collective-permute-start | bytes 479240 | tf_op jit(solution)/shard_map/ppermute | solution.py:34
  281.3 9.9 %collective-permute-start.30 = (bf16[144,384]{1,0:T(8,128)(2,1)}, bf16[144,384]{1,0:T(8,128)(2,1)}, u32[]{:S(2)}, u32[]{:S(2)}) collective-permute-start(bf16[144,384]{1,0:T(8,128)(2,1)} %get-tuple-element.117), channel_id=1, source_target_pairs={{0,2},{2,0},{4,6},{6,4},{1,3},{3,1},{5,7},{7,5},{8,10},{10,8},{12,... | collective-permute-start | bytes 331784 | tf_op jit(solution)/shard_map/ppermute | solution.py:34
  286.8 15.3 %collective-permute-start.22 = (bf16[256,384]{1,0:T(8,128)(2,1)S(1)}, bf16[256,384]{1,0:T(8,128)(2,1)S(1)}, u32[]{:S(2)}, u32[]{:S(2)}) collective-permute-start(bf16[256,384]{1,0:T(8,128)(2,1)S(1)} %slice.305), channel_id=1, source_target_pairs={{0,1},{1,0},{2,3},{3,2},{4,5},{5,4},{6,7},{7,6},{8,9},{9,8},{10,11... | collective-permute-start | bytes 589832 | tf_op jit(solution)/shard_map/ppermute | solution.py:34
  288.5 14.4 %collective-permute-start.26 = (bf16[256,384]{1,0:T(8,128)(2,1)S(1)}, bf16[256,384]{1,0:T(8,128)(2,1)S(1)}, u32[]{:S(2)}, u32[]{:S(2)}) collective-permute-start(bf16[256,384]{1,0:T(8,128)(2,1)S(1)} %slice.317), channel_id=1, source_target_pairs={{0,1},{1,0},{2,3},{3,2},{4,5},{5,4},{6,7},{7,6},{8,9},{9,8},{10,11... | collective-permute-start | bytes 589832 | tf_op jit(solution)/shard_map/ppermute | solution.py:34
  292.2 7.2 %collective-permute-start.31 = (bf16[144,384]{1,0:T(8,128)(2,1)S(1)}, bf16[144,384]{1,0:T(8,128)(2,1)S(1)}, u32[]{:S(2)}, u32[]{:S(2)}) collective-permute-start(bf16[144,384]{1,0:T(8,128)(2,1)S(1)} %fusion.34), channel_id=1, source_target_pairs={{0,4},{2,6},{4,0},{6,2},{1,5},{3,7},{5,1},{7,3},{8,12},{10,14},{12... | collective-permute-start | bytes 331784 | tf_op jit(solution)/shard_map/ppermute | solution.py:34
  (43 other events, 370.3 us)

commit v2 on v1

--- a/solution.py
+++ b/solution.py
@@ -44,6 +44,22 @@
     return jnp.where(lax.rem(lax.axis_index("seq"), 2) == 0, value, moved)
 
 
+def fetch_quarter(value):
+    seq_count, row_count = lax.axis_size("seq"), lax.axis_size("row")
+    seq_me = lax.axis_index("seq")
+    odd = range(1, seq_count, 2)
+    over_z = [(s * row_count + r, s * row_count + (r ^ 2)) for s in odd for r in range(row_count)]
+    over_x = [(s, s ^ 2) for s in odd]
+    side = lax.rem(seq_me // 2, 2)
+    half = value.shape[0] // 2
+    got = lax.ppermute(lax.dynamic_slice_in_dim(value, side * half, half, 0), ("seq", "row"), over_z)
+    other = lax.ppermute(got, "seq", over_x)
+    low = jnp.where(side == 0, got, other)
+    high = jnp.where(side == 0, other, got)
+    moved = jnp.concatenate([low, high], axis=0)
+    return jnp.where(lax.rem(seq_me, 2) == 0, value, moved)
+
+
 def swap_add(value, axis, bit):
     rounded = lax.reduce_precision(value, 8, 7)
     return rounded + swap(rounded.astype(BF16), axis, bit).astype(F32)
@@ -69,12 +85,13 @@
     dy_ref,
     cos_ref,
     sin_ref,
+    ff_out_ref,
+    ff_grad_ref,
+    vec_ref,
     small0_ref,
     small1_ref,
     kv0_ref,
     kv1_ref,
-    kv2_ref,
-    kv3_ref,
     *rest,
     shape,
     second,
@@ -82,11 +99,16 @@
     heads = shape.heads
     rest = list(rest)
     if second:
-        dqw_in_ref, dow_in_ref, dqb_in_ref, dkv_in_ref = rest[:4]
-        rest = rest[4:]
-    out_ref, dx_ref, dqw_ref, dow_ref, dqb_ref, dkv_out_ref, last_ref = rest[:7]
+        stats_ref, dqw_in_ref, dow_in_ref, dqb_in_ref, dkv_in_ref = rest[:5]
+        rest = rest[5:]
+        stay_ref, go_ref, keep_ref, send_ref, stat_ref, dkv_out_ref, last_ref = rest[:7]
+        dqw_ref, dow_ref, dqb_ref = rest[7:10]
+        rest = rest[10:]
+    else:
+        stay_ref, go_ref, dqw_ref, dow_ref, dqb_ref, dkv_out_ref, last_ref = rest[:7]
+        rest = rest[7:]
     (
-        qd_ref,
+    qd_ref,
         probs_ref,
         high_ref,
         sums_ref,
@@ -99,7 +121,8 @@
         qw_ref,
         ow_ref,
         copy_sem,
-    ) = rest[7:]
+        late_sem,
+    ) = rest
     blocks = kv_ref.shape[0]
     half = blocks // 2
     slot = pl.program_id(0)
@@ -119,21 +142,46 @@
             apart_seq // 2 + (shape.seq_count // 2) * lax.rem(apart_seq, 2)
         )
 
+    def put(index, rows):
+        @pl.when(slot == 0)
+        def _():
+            stay_ref[index] = rows
+
+        @pl.when(slot == 1)
+        def _():
+            go_ref[index] = rows.astype(BF16)
+
+    pieces = [
+        pltpu.make_async_copy(piece, kv_ref.at[i * half : (i + 1) * half], copy_sem.at[i])
+        for i, piece in enumerate((kv0_ref, kv1_ref))
+    ]
+    if second:
+        late = [
+            pltpu.make_async_copy(source, target, late_sem.at[i])
+            for i, (source, target) in enumerate(
+                (
+                    (dkv_in_ref, dkv_ref),
+                    (dqw_in_ref, dqw_ref),
+                    (dow_in_ref, dow_ref),
+                    (dqb_in_ref, dqb_ref),
+                )
+            )
+        ]
+    else:
+        late = [
+            pltpu.make_async_copy(low_ref, dkv_ref.at[i : i + 1], late_sem.at[i]) for i in range(blocks)
+        ]
+
     @pl.when(slot == 0)
     def _():
-        copies = [
-            pltpu.make_async_copy(
-                piece,
-                kv_ref.at[
-                    (i // 2) * half : (i // 2 + 1) * half, (i % 2) * HALF : (i % 2 + 1) * HALF, :
-                ],
-                copy_sem.at[i],
-            )
-            for i, piece in enumerate((kv0_ref, kv1_ref, kv2_ref, kv3_ref))
-        ]
-        if second:
-            copies.append(pltpu.make_async_copy(dkv_in_ref, dkv_ref, copy_sem.at[4]))
-        for copy in copies:
+        for copy in pieces:
+            copy.start()
+        if not second:
+            low_ref[...] = jnp.zeros_like(low_ref)
+            dqw_ref[...] = jnp.zeros_like(dqw_ref)
+            dow_ref[...] = jnp.zeros_like(dow_ref)
+            dqb_ref[...] = jnp.zeros_like(dqb_ref)
+        for copy in late:
             copy.start()
         span = small0_ref.shape[1]
         count = heads * HD
@@ -143,36 +191,6 @@
             ow_ref[:count, part] = small[count : 2 * count, :]
         qw_ref[count:, :] = jnp.zeros_like(qw_ref[count:, :])
         ow_ref[count:, :] = jnp.zeros_like(ow_ref[count:, :])
-        if second:
-            dqw_ref[...] = dqw_in_ref[...]
-            dow_ref[...] = dow_in_ref[...]
-            dqb_ref[...] = dqb_in_ref[...]
-        else:
-            dkv_ref[...] = jnp.zeros_like(dkv_ref)
-            dqw_ref[...] = jnp.zeros_like(dqw_ref)
-            dow_ref[...] = jnp.zeros_like(dow_ref)
-            dqb_ref[...] = jnp.zeros_like(dqb_ref)
-        for copy in copies:
-            copy.wait()
-        if not second:
-            copies = []
-            dealt = last_ref.shape[0]
-            group = seq * 2 + second_half
-            for i in range(dealt):
-                owner = meta_ref[3 + shape.sequences + group * dealt + i]
-                for part in (0, 1):
-                    take = jnp.where(second_half > 0, 1 - part, part) * HALF
-                    copies.append(
-                        pltpu.make_async_copy(
-                            kv_ref.at[slot_of(owner), pl.ds(take, HALF), :],
-                            last_ref.at[i, part * HALF : (part + 1) * HALF, :],
-                            copy_sem.at[5 + 2 * i + part],
-                        )
-                    )
-            for copy in copies:
-                copy.start()
-            for copy in copies:
-                copy.wait()
 
     cosine = cos_ref[0]
     sine = sin_ref[0]
@@ -216,6 +234,11 @@
         qd_ref[mine, :] = turned.astype(BF16) * BF16(HD**-0.5)
         qd_ref[rows + h * HALF : rows + (h + 1) * HALF, :] = jnp.where(front, 0.0, grad).astype(BF16)
 
+    @pl.when(slot == 0)
+    def _():
+        for copy in pieces:
+            copy.wait()
+
     high_ref[...] = jnp.full_like(high_ref, NEGATIVE)
     sums_ref[...] = jnp.zeros_like(sums_ref)
 
@@ -254,6 +277,11 @@
     mix(before, True)
     lax.fori_loop(0, before, lambda step, c: (mix(step, False), c)[1], 0)
 
+    @pl.when(slot == 0)
+    def _():
+        for copy in late:
+            copy.wait()
+
     parts = []
     for h in range(heads):
         mine = slice(h * HALF, (h + 1) * HALF)
@@ -262,7 +290,7 @@
         dots_ref[:, mine] = jnp.sum(jnp.transpose(mixed * grad), axis=0, keepdims=True)
         parts.append(mixed if h % 2 else pltpu.roll(mixed, HD, 1))
     joined = join(parts).astype(BF16)
-    out_ref[0] = dot(joined, ow_ref[...])
+    put(0, ff_out_ref[0] + dot(joined, ow_ref[...]))
     dow_ref[...] += dot(joined, dy_ref[0], TN)
 
     def backward(step, first):
@@ -290,14 +318,28 @@
     joined = join(parts)
     dqb_ref[...] += jnp.sum(joined, axis=0, keepdims=True)
     joined = joined.astype(BF16)
-    dx_ref[0] = dot(joined, qw_ref[...])
+    put(1, ff_grad_ref[0] + dot(joined, qw_ref[...]) * vec_ref[0:1, :])
     dqw_ref[...] += dot(joined, first_ref[0], TN)
 
     @pl.when(slot == 1)
     def _():
         if not second:
             copies = [pltpu.make_async_copy(dkv_ref, dkv_out_ref, copy_sem.at[0])]
-            copies[0].start()
+            dealt = last_ref.shape[0]
+            group = seq * 2 + second_half
+            for i in range(dealt):
+                owner = meta_ref[3 + shape.sequences + group * dealt + i]
+                for part in (0, 1):
+                    take = jnp.where(second_half > 0, 1 - part, part) * HALF
+                    copies.append(
+                        pltpu.make_async_copy(
+                            kv_ref.at[slot_of(owner), pl.ds(take, HALF), :],
+                            last_ref.at[i, part * HALF : (part + 1) * HALF, :],
+                            copy_sem.at[1 + 2 * i + part],
+                        )
+                    )
+            for copy in copies:
+                copy.start()
         else:
             copies = [pltpu.make_async_copy(dkv_ref.at[:half], dkv_out_ref, copy_sem.at[0])]
             copies[0].start()
@@ -307,11 +349,39 @@
                 low_ref[...] = dkv_ref[half:].astype(BF16)
                 copies.append(pltpu.make_async_copy(low_ref, last_ref, copy_sem.at[1]))
             copies[1].start()
+            count = heads * HD
+            span = small0_ref.shape[1]
+            bias_up = stats_ref[2:3, :]
+            bias_q = dqb_ref[...]
+            for i, target in enumerate((keep_ref, send_ref)):
+                part = slice(i * span, (i + 1) * span)
+                target[:count, :] = dqw_ref[:count, part].astype(BF16)
+                target[count : 2 * count, :] = dow_ref[:count, part].astype(BF16)
+                rows_of = jnp.concatenate(
+                    [
+                        bias_up[:, :span],
+                        bias_up[:, span:],
+                        jnp.concatenate([bias_q, jnp.zeros((1, span - padded), F32)], axis=1),
+                        jnp.zeros((5, span), F32),
+                    ],
+                    axis=0,
+                )
+                target[2 * count :, :] = jnp.concatenate(
+                    [rows_of, jnp.zeros((target.shape[0] - 2 * count - 8, span), F32)], axis=0
+                ).astype(BF16)
+            weight = qw_ref[...].astype(F32)
+            column = jnp.transpose(jnp.broadcast_to(bias_q, (8, padded)))[:, 0:1]
+            plain = jnp.sum(weight * column, axis=0, keepdims=True)
+            stat_ref[0:1, :] = (
+                jnp.sum(weight * dqw_ref[...], axis=0, keepdims=True) - vec_ref[1:2, :] * plain
+            ) / vec_ref[0:1, :]
+            stat_ref[1:2, :] = plain
+            stat_ref[2:8, :] = jnp.zeros((6, 2 * span), F32)
         for copy in copies:
             copy.wait()
 
 
-def attention(meta, first_in, dy, cosine, sine, small, pieces, so_far, shape):
+def attention(meta, first_in, dy, cosine, sine, ff, vectors, small, pieces, so_far, shape):
     second = so_far is not None
     _, _, width = first_in.shape
     half = pieces[0].shape[0]
@@ -328,33 +398,36 @@
     def per_slot(lanes):
         return pl.BlockSpec((1, HALF, lanes), lambda i, m: (i + offset, 0, 0))
 
-    def out_slot(lanes):
-        return pl.BlockSpec((1, HALF, lanes), lambda i, m: (i, 0, 0))
-
     def whole(array):
         return pl.BlockSpec(
             array.shape, lambda i, m: (0,) * len(array.shape), pipeline_mode=pl.Buffered(buffer_count=1)
         )
 
     far = pl.BlockSpec(memory_space=pltpu.MemorySpace.HBM)
-    arrays = [first_in, dy, cosine, sine, *small, *pieces]
+    arrays = [first_in, dy, cosine, sine, *ff, vectors, *small, *pieces]
     in_specs = [per_slot(width), per_slot(width), per_slot(lanes), per_slot(lanes)]
-    in_specs += [whole(a) for a in small] + [far] * 4
+    in_specs += [per_slot(width)] * 2 + [whole(vectors)] + [whole(a) for a in small] + [far] * 2
+    weight = jax.ShapeDtypeStruct((padded, width), F32)
+    bias = jax.ShapeDtypeStruct((1, padded), F32)
+    tokens = jax.ShapeDtypeStruct((2, HALF, width), F32)
     if second:
         arrays += list(so_far)
-        in_specs += [whole(a) for a in so_far[:3]] + [far]
-    weight = jax.ShapeDtypeStruct((padded, width), F32)
-    bias = jax.ShapeDtypeStruct((1, padded), F32)
+        in_specs += [whole(so_far[0])] + [far] * 4
+        part = jax.ShapeDtypeStruct((2 * heads * HD + 32, width // 2), BF16)
+        sums = [part, part, jax.ShapeDtypeStruct((8, width), F32)]
+        kept = [pltpu.VMEM(a.shape, F32) for a in (weight, weight, bias)]
+    else:
+        sums = [weight, weight, bias]
+        kept = []
     out_shape = [
-        jax.ShapeDtypeStruct((2, HALF, width), F32),
-        jax.ShapeDtypeStruct((2, HALF, width), F32),
-        weight,
-        weight,
-        bias,
+        tokens,
+        jax.ShapeDtypeStruct(tokens.shape, BF16),
+        *sums,
         jax.ShapeDtypeStruct((half if second else blocks, BLOCK, lanes), total_type),
         jax.ShapeDtypeStruct((half if second else dealt, BLOCK, lanes), BF16),
     ]
-    out_specs = [out_slot(width), out_slot(width), whole(weight), whole(weight), whole(bias), far, far]
+    out_specs = [whole(tokens)] * 2 + [whole(a) for a in sums] + [far, far]
+    low = BF16 if second else total_type
     return pl.pallas_call(
         functools.partial(attention_kernel, shape=shape, second=second),
         grid_spec=pltpu.PrefetchScalarGridSpec(
@@ -362,7 +435,8 @@
             grid=(2,),
             in_specs=in_specs,
             out_specs=out_specs,
-            scratch_shapes=[
+            scratch_shapes=kept
+            + [
                 pltpu.VMEM((2 * rows, lanes), BF16),
                 pltpu.VMEM((longest, BLOCK, rows), BF16),
                 pltpu.VMEM((longest, rows), F32),
@@ -372,10 +446,11 @@
                 pltpu.VMEM((rows, lanes), F32),
                 pltpu.VMEM((blocks, BLOCK, lanes), total_type),
                 pltpu.VMEM((blocks, BLOCK, lanes), BF16),
-                pltpu.VMEM((half if second and blocks <= 32 else 1, BLOCK, lanes), BF16),
+                pltpu.VMEM((half if second and blocks <= 32 else 1, BLOCK, lanes), low),
                 pltpu.VMEM((padded, width), BF16),
                 pltpu.VMEM((padded, width), BF16),
-                pltpu.SemaphoreType.DMA((5 + 2 * dealt,)),
+                pltpu.SemaphoreType.DMA((2 + 2 * dealt,)),
+                pltpu.SemaphoreType.DMA((4 if second else blocks,)),
             ],
         ),
         out_shape=out_shape,
@@ -395,21 +470,21 @@
 def tables_kernel(meta_ref, cos_ref, sin_ref, *, shape):
     seq, row, col = meta_ref[0], meta_ref[1], meta_ref[2]
     lane = lax.broadcasted_iota(jnp.int32, (HALF, 2 * HD), 1)
-    inside = lax.broadcasted_iota(jnp.int32, (HALF, 2 * HD), 0) + col * HALF
+    inside = lax.broadcasted_iota(jnp.int32, (HALF, 2 * HD), 0)
     half_rot = ROT // 2
     exponent = lax.rem(lane, half_rot).astype(F32) * (1.0 / half_rot)
     frequency = jnp.where(lane < ROT, 1.0 / jnp.exp(exponent * jnp.log(jnp.full_like(exponent, 10000.0))), 0.0)
-    for i, slot in enumerate(ORDER):
+    for i, (slot, half) in enumerate([(slot, col) for slot in ORDER] + [(0, 1 - col)]):
         block = lax.bitwise_xor(seq, slot // 2) * shape.row_count + lax.bitwise_xor(row, slot % 2)
         start = (block - first_of(meta_ref, block, shape)) * BLOCK
-        angles = (inside + start).astype(F32) * frequency
+        angles = (inside + (start + half * HALF)).astype(F32) * frequency
         cos_ref[i] = jnp.cos(angles)
         turned = jnp.sin(angles)
         sin_ref[i] = jnp.where(lane < half_rot, -turned, jnp.where(lane < ROT, turned, 0.0))
 
 
 def tables(meta, shape):
-    table = jax.ShapeDtypeStruct((4, HALF, 2 * HD), F32)
+    table = jax.ShapeDtypeStruct((5, HALF, 2 * HD), F32)
     return pl.pallas_call(
         functools.partial(tables_kernel, shape=shape),
         in_specs=[pl.BlockSpec(memory_space=pltpu.SMEM)],
@@ -567,8 +642,10 @@
     high = vectors.astype(BF16).astype(F32)
     both = jnp.concatenate([high, vectors - high], axis=0).astype(BF16)
     pack_ref[base:, :] = both
-    x_ref[:, :span] = tokens_ref[here, pl.ds(pl.multiple_of(col * span, 128), span)]
-    x_ref[:, span:] = tokens_ref[here, pl.ds(pl.multiple_of((1 - col) * span, 128), span)]
+    for i, rows in enumerate((here, there)):
+        part = slice(i * HALF, (i + 1) * HALF)
+        x_ref[part, :span] = tokens_ref[rows, pl.ds(pl.multiple_of(col * span, 128), span)]
+        x_ref[part, span:] = tokens_ref[rows, pl.ds(pl.multiple_of((1 - col) * span, 128), span)]
     mine_ref[...] = dy_ref[here, :]
     count = qw_ref.shape[0]
     small_ref[:count, :] = qw_ref[...]
@@ -588,7 +665,7 @@
         out_specs=[vmem] * 4,
         out_shape=[
             jax.ShapeDtypeStruct((HALF + 2 * HD + 2 * rows, span), BF16),
-            jax.ShapeDtypeStruct((HALF, width), BF16),
+            jax.ShapeDtypeStruct((2 * HALF, width), BF16),
             jax.ShapeDtypeStruct((HALF, span), BF16),
             jax.ShapeDtypeStruct((2 * count + 2 * rows, span), BF16),
         ],
@@ -605,7 +682,7 @@
     other = got_ref[base : base + 2 * rows, :].astype(F32)
     full = jnp.concatenate([vec_ref[...], other[:rows] + other[rows:]], axis=1)
     full_ref[...] = full
-    both_ref[0] = x_ref[...]
+    both_ref[0] = x_ref[:HALF, :]
     both_ref[1, :, :span] = mine_ref[...]
     both_ref[1, :, span:] = got_ref[:HALF, :]
     kvw_ref[:, :span] = pack_ref[HALF:base, :]
@@ -615,13 +692,17 @@
     spread = jnp.mean(wide * wide, axis=1, keepdims=True) - mean * mean
     normed = (wide - mean) * lax.rsqrt(spread + EPS)
     first = (normed * full[0:1, :] + full[1:2, :]).astype(BF16)
-    pre = dot(first, kvw_ref[...], NT) + bias_ref[...]
-    lane = lax.broadcasted_iota(jnp.int32, pre.shape, 1)
-    lanes = pre.shape[1]
-    rolled = jnp.where(
-        lane < ROT // 2, pltpu.roll(pre, lanes - ROT // 2, 1), pltpu.roll(pre, ROT // 2, 1)
-    )
-    pair_ref[0] = (pre * cos_ref[0] + rolled * sin_ref[0]).astype(BF16)
+    pre_all = dot(first, kvw_ref[...], NT) + bias_ref[...]
+    lanes = pre_all.shape[1]
+    lane = lax.broadcasted_iota(jnp.int32, (HALF, lanes), 1)
+    for i in (0, 1):
+        pre = pre_all[i * HALF : (i + 1) * HALF, :]
+        rolled = jnp.where(
+            lane < ROT // 2, pltpu.roll(pre, lanes - ROT // 2, 1), pltpu.roll(pre, ROT // 2, 1)
+        )
+        pair_ref[0, i * HALF : (i + 1) * HALF, :] = (
+            pre * cos_ref[4 * i] + rolled * sin_ref[4 * i]
+        ).astype(BF16)
 
 
 def own_pairs(x_own, mine, pack, got, vectors, cosine, sine, bias):
@@ -632,7 +713,7 @@
         in_specs=[vmem] * 8,
         out_specs=[vmem] * 4,
         out_shape=[
-            jax.ShapeDtypeStruct((1, HALF, 2 * HD), BF16),
+            jax.ShapeDtypeStruct((1, 2 * HALF, 2 * HD), BF16),
             jax.ShapeDtypeStruct((2, HALF, width), BF16),
             jax.ShapeDtypeStruct((2 * HD, width), BF16),
             jax.ShapeDtypeStruct((vectors.shape[0], width), F32),
@@ -641,31 +722,114 @@
     )(x_own, mine, pack, got, vectors, cosine, sine, bias)
 
 
+def pairs_kernel(
+    keep_ref, got_ref, cos_ref, sin_ref, first_ref, kvw_ref, vec_ref, stat_ref, ff_ref, dys_ref, mine_ref, send_ref
+):
+    span = mine_ref.shape[1]
+    lanes = 2 * HD
+    lane = lax.broadcasted_iota(jnp.int32, (HALF, lanes), 1)
+    total = keep_ref[...] + got_ref[...].astype(F32)
+    weight = jnp.zeros((lanes, 2 * span), F32)
+    bias = jnp.zeros((1, lanes), F32)
+    for i in (0, 1):
+        part = total[i]
+        rolled = jnp.where(
+            lane < ROT // 2, pltpu.roll(part, lanes - ROT // 2, 1), pltpu.roll(part, ROT // 2, 1)
+        )
+        turned = part * cos_ref[2 * i] - rolled * sin_ref[2 * i]
+        bias = bias + jnp.sum(turned, axis=0, keepdims=True)
+        weight = weight + dot(turned.astype(BF16), first_ref[2 * i], TN)
+    kvw = kvw_ref[...].astype(F32)
+    column = jnp.transpose(jnp.broadcast_to(bias, (8, lanes)))[:, 0:1]
+    plain = jnp.sum(kvw * column, axis=0, keepdims=True)
+    gain = (jnp.sum(kvw * weight, axis=0, keepdims=True) - vec_ref[1:2, :] * plain) / vec_ref[0:1, :]
+    fill = jnp.zeros((1, span - lanes), F32)
+    bias = jnp.concatenate([bias.astype(BF16).astype(F32), fill], axis=1)
+    for i, target in enumerate((mine_ref, send_ref)):
+        part = slice(i * span, (i + 1) * span)
+        target[:lanes, :] = weight[:, part].astype(target.dtype)
+        rows = jnp.concatenate(
+            [
+                stat_ref[0:1, part] + gain[:, part],
+                stat_ref[1:2, part] + plain[:, part],
+                ff_ref[0:2, part],
+                bias,
+                dys_ref[...] if i == 0 else jnp.zeros((1, span), F32),
+                jnp.zeros((10, span), F32),
+            ],
+            axis=0,
+        )
+        target[lanes:, :] = rows.astype(target.dtype)
+
+
+def pair_sums(keep, got, cosine, sine, first_in, keyval, vectors, stats, ff_stats, dy_sum):
+    width = keyval.shape[1]
+    vmem = pl.BlockSpec(memory_space=pltpu.VMEM)
+    return pl.pallas_call(
+        pairs_kernel,
+        in_specs=[vmem] * 10,
+        out_specs=[vmem] * 2,
+        out_shape=[
+            jax.ShapeDtypeStruct((2 * HD + 16, width // 2), F32),
+            jax.ShapeDtypeStruct((2 * HD + 16, width // 2), BF16),
+        ],
+        name="pair_sums",
+    )(keep, got, cosine, sine, first_in, keyval, vectors, stats, ff_stats, dy_sum)
+
+
+def rows_kernel(
+    own_ref,
+    got_ref,
+    cos_ref,
+    sin_ref,
+    kvw_ref,
+    vec_ref,
+    x_ref,
+    dy_ref,
+    keep_ref,
+    core_ref,
+    back_ref,
+    mine_ref,
+    send_ref,
+):
+    span = mine_ref.shape[2]
+    lanes = 2 * HD
+    lane = lax.broadcasted_iota(jnp.int32, (HALF, lanes), 1)
+    part = own_ref[0] + got_ref[...].astype(F32)
+    rolled = jnp.where(
+        lane < ROT // 2, pltpu.roll(part, lanes - ROT // 2, 1), pltpu.roll(part, ROT // 2, 1)
+    )
+    turned = (part * cos_ref[0] - rolled * sin_ref[0]).astype(BF16)
+    wide = x_ref[:HALF, :].astype(F32)
+    mean = jnp.mean(wide, axis=1, keepdims=True)
+    spread = jnp.mean(wide * wide, axis=1, keepdims=True) - mean * mean
+    root = lax.rsqrt(spread + EPS)
+    normed = (wide - mean) * root
+    grad = keep_ref[1] + core_ref[1].astype(F32) + back_ref[1].astype(F32) + dot(turned, kvw_ref[...]) * vec_ref[0:1, :]
+    one = jnp.mean(grad, axis=1, keepdims=True)
+    two = jnp.mean(grad * normed, axis=1, keepdims=True)
+    grad = dy_ref[0].astype(F32) + root * (grad - one - normed * two)
+    out = wide + keep_ref[0] + core_ref[0].astype(F32) + back_ref[0].astype(F32) + vec_ref[4:5, :]
+    for i, rows in enumerate((out.astype(BF16), grad.astype(BF16))):
+        mine_ref[i] = rows[:, :span]
+        send_ref[i] = rows[:, span:]
+
+
+def own_rows(own, got, cosine, sine, keyval, vectors, x_block, dy, keep, core, back):
+    width = keyval.shape[1]
+    vmem = pl.BlockSpec(memory_space=pltpu.VMEM)
+    half = jax.ShapeDtypeStruct((2, HALF, width // 2), BF16)
+    return pl.pallas_call(
+        rows_kernel,
+        in_specs=[vmem] * 11,
+        out_specs=[vmem] * 2,
+        out_shape=[half, half],
+        name="own_rows",
+    )(own, got, cosine, sine, keyval, vectors, x_block, dy, keep, core, back)
+
+
 def after(value, *others):
     return lax.optimization_barrier((value,) + others)[0]
-
-
-def weights_over_col(partial):
-    half = partial.shape[1] // 2
-    received = swap(partial[:, half:].astype(BF16), "col", 1)
-    return (partial[:, :half].astype(F32) + received.astype(F32)).astype(BF16)
-
-
-def weights_over_rest(moved):
-    core = lax.rem(lax.axis_index("seq"), 2)
-    half = moved.shape[0] // 2
-    keep = lax.dynamic_slice_in_dim(moved, core * half, half, 0).astype(F32)
-    send = lax.dynamic_slice_in_dim(moved, (1 - core) * half, half, 0)
-    total = keep + swap(send, "seq", 1).astype(F32)
-    bit = 2
-    while bit < lax.axis_size("seq"):
-        total = swap_add(total, "seq", bit)
-        bit = bit * 2
-    total = total.astype(BF16)
-    other = swap(total, "seq", 1)
-    first = jnp.where(core == 0, total, other)
-    second = jnp.where(core == 0, other, total)
-    return jnp.concatenate([first, second], axis=0).astype(F32)
 
 
 def on_device(
@@ -718,180 +882,128 @@
             jnp.zeros((span - head_width,), F32),
         ]
     ).reshape(8, span)
-    pack, x_own, dy_mine, small = prologue(
+    pack, x_block, dy_mine, small = prologue(
         meta, tokens, cotangent, keyval_weight, jnp.transpose(query_weight), output_weight, vectors
     )
     received = swap(pack, "col", 1)
     cosine, sine = tables(after(meta, pack), shape)
-    half_rot = ROT // 2
-
-    def norm(values):
-        wide = values.astype(F32)
-        mean = jnp.mean(wide, axis=-1, keepdims=True)
-        spread = jnp.mean(wide * wide, axis=-1, keepdims=True) - mean * mean
-        root = lax.rsqrt(spread + EPS)
-        return (wide - mean) * root, root
-
-    def turn(values, cosine, sine):
-        rolled = jnp.concatenate(
-            [
-                values[:, half_rot:ROT],
-                values[:, :half_rot],
-                jnp.zeros((values.shape[0], pair_width - ROT), F32),
-            ],
-            axis=1,
-        )
-        return values * cosine + rolled * sine
-
+
+    small_own = swap_odd_rows(small)
+    up_own = fetch_quarter(upward_weight)
     pairs, both, keyval_full, vec_full = own_pairs(
-        x_own, dy_mine, pack, received, vectors, cosine, sine, keyval_bias[None]
-    )
-    gain_a, shift_a, gain_f, shift_f, bias_out = [vec_full[i][None] for i in range(5)]
+        x_block, dy_mine, pack, received, vectors, cosine, sine, keyval_bias[None]
+    )
     steps = [("row", 1), ("row", 2)]
     bit = 2
     while bit < seq_count:
         steps.append(("seq", bit))
         bit = bit * 2
-    small_own = swap_odd_rows(small)
-    up_own = swap_odd_rows(upward_weight)
     small_full = (small_own, swap(small_own, "col", 1))
-    both_got = None
     for i, (axis, bit) in enumerate(steps):
         got = swap(pairs, axis, bit)
         if i == 0:
             both_got = swap(after(both, got), "row", 1)
-            down_own = swap_odd_rows(after(down_weight, got))
-        if i == 1:
-            up_full = (up_own, swap(after(up_own, got), "col", 1))
+            down_own = fetch_quarter(after(down_weight, got))
         pairs = jnp.concatenate([pairs, got], axis=0)
-    pairs_col = swap(pairs, "col", 1)
-    pieces = (pairs, pairs_col, swap(pairs, "seq", 1), swap(pairs_col, "seq", 1))
+    pieces = (pairs, swap(pairs, "seq", 1))
+    up_full = (up_own, swap(up_own, "col", 1))
 
     first_in, dy_all, ff_out, ff_grad, ff_keep, ff_send, ff_stats = feed_forward(
         (both, swap(both_got, "seq", 1), both_got, swap(both, "seq", 1)),
-        vec_full,
+        after(vec_full, got, small_full[1]),
         small_own,
         up_full,
-        (down_own, swap(after(down_own, pairs_col), "col", 1)),
+        (down_own, swap(down_own, "col", 1)),
     )
 
     ff_got = swap(ff_send, "col", 1)
-    ff_sum = (ff_keep.astype(F32) + ff_got.astype(F32)).astype(BF16)
-    out_a, dx_a, dquery_w, doutput_w, dquery_b, dpairs, cache_rows = attention(
-        after(meta, ff_send), first_in, dy_all, cosine, sine, small_full, pieces, None, shape
-    )
+    ff = (ff_out, ff_grad)
+    stay_a, go_a, dquery_w, doutput_w, dquery_b, dpairs, cache_rows = attention(
+        after(meta, ff_send), first_in, dy_all, cosine, sine, ff, vec_full, small_full, pieces, None, shape
+    )
+    ff_sum = (after(ff_keep, go_a).astype(F32) + ff_got.astype(F32)).astype(BF16)
     ff_moved = swap_odd_rows(ff_sum)
-    out_b, dx_b, dquery_w, doutput_w, dquery_b, keep_pairs, send_pairs = attention(
+    core_a = swap(go_a, "seq", 1)
+    stay_b, go_b, small_keep, small_send, stats, keep_pairs, send_pairs = attention(
         after(meta, ff_sum),
         first_in,
         dy_all,
         cosine,
         sine,
+        ff,
+        vec_full,
         small_full,
         pieces,
-        (dquery_w, doutput_w, dquery_b, dpairs),
+        (ff_stats, dquery_w, doutput_w, dquery_b, dpairs),
         shape,
     )
 
-    total = keep_pairs.astype(F32) + swap(after(send_pairs, ff_moved), "seq", 1).astype(F32)
-    first_total = total
-    total = total[:, :HALF] + swap(total[:, HALF:].astype(BF16), "col", 1).astype(F32)
-    col_total = total
-    for axis, bit in reversed(steps[1:]):
+    send_pairs = after(send_pairs, ff_moved, core_a)
+    got = swap(send_pairs, "seq", 1)
+    col_send = (keep_pairs[:, HALF:].astype(F32) + got[:, HALF:].astype(F32)).astype(BF16)
+    col_got = swap(col_send, "col", 1)
+    away = (stay_b + core_a.astype(F32)).astype(BF16)
+    back = swap(after(away, got), "row", 1)
+    core_b = swap(after(go_b, col_send), "seq", 1)
+    core = lax.rem(seq_me, 2)
+
+    def core_halves(moved):
+        half = moved.shape[0] // 2
+        keep = lax.dynamic_slice_in_dim(moved, core * half, half, 0)
+        return keep, lax.dynamic_slice_in_dim(moved, (1 - core) * half, half, 0)
+
+    def over_seq(value):
+        bit = 2
+        while bit < seq_count:
+            value = swap_add(value, "seq", bit)
+            bit = bit * 2
+        return value.astype(BF16)
+
+    def both_halves(value):
+        other = swap(value, "seq", 1)
+        first = jnp.where(core == 0, value, other)
+        second = jnp.where(core == 0, other, value)
+        return jnp.concatenate([first, second], axis=0).astype(F32)
+
+    ff_keep, ff_away = core_halves(after(ff_moved, col_send))
+    ff_part = over_seq(ff_keep.astype(F32) + swap(ff_away, "seq", 1).astype(F32))
+    total = keep_pairs[:, :HALF].astype(F32) + got[:, :HALF].astype(F32) + col_got.astype(F32)
+    small_got = swap(after(small_send, total), "col", 1)
+    small_sum = (small_keep.astype(F32) + small_got.astype(F32)).astype(BF16)
+    for axis, bit in reversed(steps[2:]):
         half = total.shape[0] // 2
         total = total[:half] + swap(total[half:].astype(BF16), axis, bit).astype(F32)
-    own_total = total[0] + swap(total[1].astype(BF16), "row", 1).astype(F32)
-    grad_pair = turn(
-        total.reshape(2 * HALF, pair_width),
-        jnp.concatenate([cosine[0], cosine[2]], axis=0),
-        -jnp.concatenate([sine[0], sine[2]], axis=0),
-    )
-    grad_keyval = dot(grad_pair.astype(BF16), jnp.concatenate([first_in[0], first_in[2]], axis=0), TN)
-    own_pair = turn(own_total, cosine[0], -sine[0]).astype(BF16)
-    grad_first_kv = dot(own_pair, keyval_full)
-
-    send = jnp.stack(
-        [
-            out_b[1] + ff_out[3],
-            out_a[1] + ff_out[1],
-            dx_b[1] * gain_a + ff_grad[3],
-            dx_a[1] * gain_a + ff_grad[1],
-        ]
-    ).astype(BF16)
-    got = swap(send, "seq", 1).astype(F32)
-    away = jnp.stack(
-        [out_b[0] + ff_out[2] + got[1], dx_b[0] * gain_a + ff_grad[2] + got[3]]
-    ).astype(BF16)
-    back = swap(after(away, col_total), "row", 1).astype(F32)
-    out_one = out_a[0] + ff_out[0] + got[0] + back[0]
-    grad_one = dx_a[0] * gain_a + ff_grad[0] + got[2] + back[1]
-    x_wide = x_own.astype(F32)
-    out_rows = (x_wide + out_one + bias_out).astype(BF16)
-    grad_one = grad_one + grad_first_kv * gain_a
-    normed_own, root_own = norm(x_own)
-    moment_one = jnp.mean(grad_one, axis=1, keepdims=True)
-    moment_two = jnp.mean(grad_one * normed_own, axis=1, keepdims=True)
-    dy_own = dy_all[0]
-    grad_rows = (
-        dy_own.astype(F32) + root_own * (grad_one - moment_one - normed_own * moment_two)
-    ).astype(BF16)
-
-    def give(rows):
-        mine = rows[:, :span]
-        other = swap(rows[:, span:], "col", 1)
-        return jnp.concatenate(
-            [jnp.where(col_me == 0, mine, other), jnp.where(col_me == 0, other, mine)], axis=0
-        )
-
-    layer_out = give(out_rows)
-    grad_tokens = give(grad_rows)
-
-    sum_ff = weights_over_rest(ff_moved)
+    row_got = swap(total[2:].astype(BF16), "row", 2)
+    small_moved = swap_odd_rows(after(small_sum, total))
+    keep_two = total[:2]
+    dy_sum = jnp.sum(cotangent.astype(F32), axis=0)[None]
+    z_send = (keep_two[1] + row_got[1].astype(F32)).astype(BF16)
+    z_got = swap(z_send, "row", 1)
+    extra_mine, extra_send = pair_sums(
+        keep_two, row_got, cosine, sine, first_in, keyval_full, vec_full, stats, ff_stats, dy_sum
+    )
+    extra = extra_mine + swap(extra_send, "col", 1).astype(F32)
+    own_total = (keep_two[0] + row_got[0].astype(F32))[None]
+    mine, away_rows = own_rows(
+        own_total, z_got, cosine, sine, keyval_full, vec_full, x_block, dy_all, stay_a, core_b, back
+    )
+    other = swap(away_rows, "col", 1)
+    first = jnp.where(col_me == 0, mine, other)
+    second = jnp.where(col_me == 0, other, mine)
+    layer_out = jnp.concatenate([first[0], second[0]], axis=0)
+    grad_tokens = jnp.concatenate([first[1], second[1]], axis=0)
+
+    sum_ff = both_halves(ff_part)
     sum_up = jnp.concatenate([sum_ff[:span], sum_ff[span : 2 * span]], axis=1)
     sum_down = sum_ff[2 * span :]
-    bias_query = jnp.pad(dquery_b[:, :head_width], ((0, 0), (0, span - head_width)))
-    bias_part = jnp.concatenate([ff_stats[2].reshape(2, span), bias_query], axis=0)
-    bias_part = lax.reduce_precision(jnp.concatenate([bias_part, bias_part], axis=1), 8, 7)
-    small_part = jnp.concatenate(
-        [
-            dquery_w[:head_width],
-            doutput_w[:head_width],
-            jnp.pad(bias_part, ((0, 29), (0, 0))),
-        ],
-        axis=0,
-    )
-    small_part = after(small_part, first_total)
-    sum_small = weights_over_rest(swap_odd_rows(after(weights_over_col(small_part), col_total)))
+    keep, send = core_halves(small_moved)
+    sum_small = both_halves(over_seq(keep.astype(F32) + swap(send, "seq", 1).astype(F32)))
     sum_query = jnp.transpose(sum_small[:head_width])
     sum_output = sum_small[head_width : 2 * head_width]
     base = 2 * head_width
     sum_bias_up = sum_small[base : base + 2].reshape(-1)
     sum_bias_query = sum_small[base + 2, :head_width]
 
-    query_wide = jnp.concatenate([part[:head_width] for part in small_full], axis=1).astype(F32)
-    keyval_wide = keyval_full.astype(F32)
-    bias_q = dquery_b[0, :head_width][:, None]
-    pair_bias = jnp.sum(grad_pair, axis=0)
-    stat_a = (
-        jnp.sum(query_wide * (dquery_w[:head_width] - bias_q * shift_a), axis=0)
-        + jnp.sum(keyval_wide * (grad_keyval - pair_bias[:, None] * shift_a), axis=0)
-    ) / gain_a[0]
-    stat_as = jnp.sum(query_wide * bias_q, axis=0) + jnp.sum(keyval_wide * pair_bias[:, None], axis=0)
-    stats = jnp.concatenate([stat_a[None], stat_as[None], ff_stats[:2]], axis=0)
-    pair_row = jnp.pad(pair_bias[None], ((0, 0), (0, span - pair_width)))
-    pair_row = lax.reduce_precision(pair_row, 8, 7)
-    dy_sum = jnp.sum(cotangent.astype(F32), axis=0)[None]
-    extra = jnp.concatenate(
-        [
-            grad_keyval,
-            stats,
-            jnp.concatenate([pair_row, pair_row], axis=1),
-            jnp.concatenate([dy_sum, jnp.zeros_like(dy_sum)], axis=1),
-            jnp.zeros((10, width), F32),
-        ],
-        axis=0,
-    )
-    extra = extra[:, :span] + swap(extra[:, span:].astype(BF16), "col", 1).astype(F32)
     bit = 1
     while bit < seq_count:
         extra = swap_add(extra, "seq", bit)

time: 306 us -> 280 us (0.915)
  local copies, waits for them, and re-layouts: 31.3 us -> 14.1 us
  other arithmetic: 33.1 us -> 18.6 us
  Pallas kernels: 60.3 us -> 71.9 us
  starting transfers between devices: 93.7 us -> 82.9 us
  waiting for transfers between devices: 81.1 us -> 90.8 us
  matrix products: 3.14 us -> 0 us
    ppermute x35 -> x33, starting transfers between devices: 88.9 us -> 77 us  [swap(): return lax.ppermute(value, axis, [(i, i ^ bit) for i in range(count)])]
    ppermute x35 -> x33, waiting for transfers between devices: 81.1 us -> 90.8 us  [swap(): return lax.ppermute(value, axis, [(i, i ^ bit) for i in range(count)])]
    pallas_call x0 -> x2, Pallas kernels: none -> 8.13 us  [the longest x1 4.83 us: own_rows(): pl.pallas_call(rows_kernel, in_specs=[vmem] * 11, out_specs=[vmem] * 2, o...]
    another operation x4 -> x0, other arithmetic: 5.9 us -> none
    slice x14 -> x2, local copies, waits for them, and re-layouts: 6.41 us -> 0.74 us  [the longest x1 0.72 us: on_device(): keep_two = total[:2]]
    concatenate x3 -> x0, local copies, waits for them, and re-layouts: 5.66 us -> none  [the longest x1 4.49 us: on_device(): jnp.concatenate([grad_keyval, stats, jnp.concatenate([pair_row, pair_row]...]
    dot_general x2 -> x0, matrix products: 3.14 us -> none  [dot(): return lax.dot_general(left, right, dims, preferred_element_type=F32)]
    unnamed x104 -> x66, local copies, waits for them, and re-layouts: 7.91 us -> 5.79 us
  transfers between devices with their start and end apart: 40 -> 40, of which waited for: 16 -> 15; matrix products, arithmetic and copies ran while one was open for 19% -> 7% of each run, Pallas kernels for 19% -> 25%
where the time goes in v2:
time: 280 us
  waiting for transfers between devices  90.8 us (32%)
  starting transfers between devices  82.9 us (30%)
  Pallas kernels  71.9 us (26%)
  other arithmetic  18.6 us (7%)
  local copies, waits for them, and re-layouts  14.1 us (5%)
    ppermute x33, waiting for transfers between devices, swap(): return lax.ppermute(value, axis, [(i, i ^ bit) for i in range(count)])  90.8 us
    ppermute x33, starting transfers between devices, swap(): return lax.ppermute(value, axis, [(i, i ^ bit) for i in range(count)])  77 us
    pallas_call x2, Pallas kernels, attention(): pl.pallas_call(functools.partial(attention_kernel, shape=shape, second=se...  38.6 us
    pallas_call x1, Pallas kernels, feed_forward(): pl.pallas_call(forward_kernel, grid=(4,), in_specs=[whole(a) for a in arr...  14.9 us
    unnamed x66, local copies, waits for them, and re-layouts  5.79 us
  transfers between devices with their start and end apart: 40, of which 15 were waited for; matrix products, arithmetic and copies ran while one was open for 7% of the time, Pallas kernels for 25%

profile of v2, /device:TPU:0, one launch (start us, length us, event | category | flops | bytes accessed | tf_op | source)
XLA Modules:
  0.0 279.7 jit_solution(11405795025129320107)
XLA Ops:
  2.9 1.3 concatenate.38.where_ref.meta_ref
  4.1 2.6 prologue.1
  6.7 3.0 %collective-permute-start = (bf16[400,384]{1,0:T(8,128)(2,1)}, bf16[400,384]{1,0:T(8,128)(2,1)S(1)}, u32[]{:S(2)}, u32[]{:S(2)}) collective-permute-start(bf16[400,384]{1,0:T(8,128)(2,1)} %get-tuple-element.67.pack_ref), channel_id=1, source_target_pairs={{0,1},{1,0},{2,3},{3,2},{4,5},{5,4},{6,7},{7,6},{8,9},{9,8},{10,11... | collective-permute-start | bytes 921608 | tf_op jit(solution)/shard_map/ppermute | solution.py:34
  11.2 4.1 %tables.1 = (f32[5,256,128]{2,1,0:T(8,128)}, f32[5,256,128]{2,1,0:T(8,128)}) custom-call(s32[22]{0:T(128)} %concatenate.38.where_ref.meta_ref), custom_call_target="tpu_custom_call" | custom-call | tf_op jit(solution)/shard_map/tables/pallas_call | solution.py:488
  16.0 1.2 collective-permute-done.got_ref
  17.9 3.6 %own_pairs.1 = (bf16[1,512,128]{2,1,0:T(8,128)(2,1)}, bf16[2,256,768]{2,1,0:T(8,128)(2,1)}, bf16[128,768]{1,0:T(8,128)(2,1)}, f32[8,768]{1,0:T(8,128)}) custom-call(bf16[512,768]{1,0:T(8,128)(2,1)} %get-tuple-element.65.x_ref, bf16[256,384]{1,0:T(8,128)(2,1)} %get-tuple-element.66.mine_ref, bf16[400,384]{1,0:T(8,128)(2,1)} %get-tuple-element.67.pack_ref, ...), custom_call_target="tpu_custom_call" | custom-call | tf_op jit(solution)/shard_map/own_pairs/pallas_call | solution.py:711
  21.5 1.9 collective-permute-start.1
  23.4 5.7 %collective-permute-done.1 = bf16[1,512,128]{2,1,0:T(8,128)(2,1)S(1)} collective-permute-done((bf16[1,512,128]{2,1,0:T(8,128)(2,1)}, bf16[1,512,128]{2,1,0:T(8,128)(2,1)S(1)}, u32[]{:S(2)}, u32[]{:S(2)}) %collective-permute-start.1) | collective-permute-done | bytes 131104 | tf_op jit(solution)/shard_map/ppermute | solution.py:34
  30.1 1.7 collective-permute-start.5
  33.2 13.8 %collective-permute-start.4 = (bf16[2,256,768]{2,1,0:T(8,128)(2,1)S(1)}, bf16[2,256,768]{2,1,0:T(8,128)(2,1)S(1)}, u32[]{:S(2)}, u32[]{:S(2)}) collective-permute-start(bf16[2,256,768]{2,1,0:T(8,128)(2,1)S(1)} %copy-done.24), channel_id=1, source_target_pairs={{0,8},{8,0},{16,24},{24,16},{1,9},{9,1},{17,25},{25,17},{2,10},{10... | collective-permute-start | bytes 2359304 | tf_op jit(solution)/shard_map/ppermute | solution.py:34
  48.6 1.6 collective-permute-start.6
  50.4 1.6 collective-permute-start.11
  52.0 19.5 %collective-permute-done.2.both1_ref = bf16[2,256,768]{2,1,0:T(8,128)(2,1)S(1)} collective-permute-done((bf16[2,256,768]{2,1,0:T(8,128)(2,1)S(1)}, bf16[2,256,768]{2,1,0:T(8,128)(2,1)S(1)}, u32[]{:S(2)}, u32[]{:S(2)}) %collective-permute-start.2) | collective-permute-done | bytes 786464 | tf_op jit(solution)/shard_map/ppermute | solution.py:34
  73.1 14.4 %collective-permute-done.14.down1_ref = bf16[768,384]{1,0:T(8,128)(2,1)S(1)} collective-permute-done((bf16[768,384]{1,0:T(8,128)(2,1)S(1)}, bf16[768,384]{1,0:T(8,128)(2,1)S(1)}, u32[]{:S(2)}, u32[]{:S(2)}) %collective-permute-start.14) | collective-permute-done | bytes 589856 | tf_op jit(solution)/shard_map/ppermute | solution.py:34
  88.3 14.9 %feed_forward.1 = (bf16[4,256,768]{2,1,0:T(8,128)(2,1)}, bf16[4,256,768]{2,1,0:T(8,128)(2,1)}, f32[4,256,768]{2,1,0:T(8,128)}, f32[4,256,768]{2,1,0:T(8,128)}, b...) custom-call(bf16[2,256,768]{2,1,0:T(8,128)(2,1)} %get-tuple-element.73.both0_ref, ...), custom_call_target="tpu_custom_call" | custom-call | flops 7000000000 | bytes 20000000 | tf_op jit(solution)/shard_map/feed_forward/pallas_call | solution.py:606
  104.1 1.0 copy-done.22
  105.1 18.8 %attention.2 = (f32[2,256,768]{2,1,0:T(8,128)}, bf16[2,256,768]{2,1,0:T(8,128)(2,1)}, f32[256,768]{1,0:T(8,128)}, f32[256,768]{1,0:T(8,128)}, f32[1,256]{1,0:T(1...) custom-call(s32[22]{0:T(128)} %concatenate.38.where_ref.meta_ref, ...), custom_call_target="tpu_custom_call" | custom-call | flops 12000000000 | bytes 15000000 | tf_op jit(solution)/shard_map/attention/pallas_call | solution.py:431
  124.0 7.1 %collective-permute-done.16 = bf16[1536,384]{1,0:T(8,128)(2,1)S(1)} collective-permute-done((bf16[1536,384]{1,0:T(8,128)(2,1)}, bf16[1536,384]{1,0:T(8,128)(2,1)S(1)}, u32[]{:S(2)}, u32[]{:S(2)}) %collective-permute-start.16) | collective-permute-done | bytes 1179680 | tf_op jit(solution)/shard_map/ppermute | solution.py:34
  132.3 3.4 %collective-permute-start.18 = (bf16[2,256,768]{2,1,0:T(8,128)(2,1)}, bf16[2,256,768]{2,1,0:T(8,128)(2,1)}, u32[]{:S(2)}, u32[]{:S(2)}) collective-permute-start(bf16[2,256,768]{2,1,0:T(8,128)(2,1)} %get-tuple-element.85), channel_id=1, source_target_pairs={{0,8},{8,0},{16,24},{24,16},{1,9},{9,1},{17,25},{25,17},{2,10},{10... | collective-permute-start | bytes 2359304 | tf_op jit(solution)/shard_map/ppermute | solution.py:34
  135.7 19.8 %attention.3 = (f32[2,256,768]{2,1,0:T(8,128)}, bf16[2,256,768]{2,1,0:T(8,128)(2,1)}, bf16[416,384]{1,0:T(8,128)(2,1)}, bf16[416,384]{1,0:T(8,128)(2,1)}, f32[8,...) custom-call(s32[22]{0:T(128)} %concatenate.38.where_ref.meta_ref, ...), custom_call_target="tpu_custom_call" | custom-call | flops 12000000000 | bytes 15000000 | tf_op jit(solution)/shard_map/attention/pallas_call | solution.py:431
  155.7 1.0 copy-done.23
  156.7 5.1 %collective-permute-start.19 = (bf16[8,512,128]{2,1,0:T(8,128)(2,1)S(1)}, bf16[8,512,128]{2,1,0:T(8,128)(2,1)S(1)}, u32[]{:S(2)}, u32[]{:S(2)}) collective-permute-start(bf16[8,512,128]{2,1,0:T(8,128)(2,1)S(1)} %copy-done.23), channel_id=1, source_target_pairs={{0,8},{8,0},{16,24},{24,16},{1,9},{9,1},{17,25},{25,17},{2,10},{10... | collective-permute-start | bytes 3145736 | tf_op jit(solution)/shard_map/ppermute | solution.py:34
  161.9 2.3 collective-permute-done.19
  165.8 1.1 convert_reduce_fusion
  167.4 12.4 %collective-permute-done.20 = bf16[8,256,128]{2,1,0:T(8,128)(2,1)} collective-permute-done((bf16[8,256,128]{2,1,0:T(8,128)(2,1)}, bf16[8,256,128]{2,1,0:T(8,128)(2,1)}, u32[]{:S(2)}, u32[]{:S(2)}) %collective-permute-start.20) | collective-permute-done | bytes 524320 | tf_op jit(solution)/shard_map/ppermute | solution.py:34
  179.8 1.3 convert_add_fusion
  181.2 13.7 %collective-permute-start.21 = (bf16[4,256,128]{2,1,0:T(8,128)(2,1)S(1)}, bf16[4,256,128]{2,1,0:T(8,128)(2,1)S(1)}, u32[]{:S(2)}, u32[]{:S(2)}) collective-permute-start(bf16[4,256,128]{2,1,0:T(8,128)(2,1)S(1)} %slice.166), channel_id=1, source_target_pairs={{0,16},{8,24},{16,0},{24,8},{1,17},{9,25},{17,1},{25,9},{2,18},{10... | collective-permute-start | bytes 786440 | tf_op jit(solution)/shard_map/ppermute | solution.py:34
  194.9 1.4 add_convert_fusion.1
  197.8 2.5 collective-permute-start.25
  201.5 8.6 %collective-permute-start.22 = (bf16[2,256,128]{2,1,0:T(8,128)(2,1)S(1)}, bf16[2,256,128]{2,1,0:T(8,128)(2,1)S(1)}, u32[]{:S(2)}, u32[]{:S(2)}) collective-permute-start(bf16[2,256,128]{2,1,0:T(8,128)(2,1)S(1)} %slice.167), channel_id=1, source_target_pairs={{0,4},{2,6},{4,0},{6,2},{1,5},{3,7},{5,1},{7,3},{8,12},{10,14},{12... | collective-permute-start | bytes 393224 | tf_op jit(solution)/shard_map/ppermute | solution.py:34
  210.2 1.4 collective-permute-start.33
  211.6 9.4 %collective-permute-done.22.got_ref = bf16[2,256,128]{2,1,0:T(8,128)(2,1)S(1)} collective-permute-done((bf16[2,256,128]{2,1,0:T(8,128)(2,1)S(1)}, bf16[2,256,128]{2,1,0:T(8,128)(2,1)S(1)}, u32[]{:S(2)}, u32[]{:S(2)}) %collective-permute-start.22) | collective-permute-done | bytes 131104 | tf_op jit(solution)/shard_map/ppermute | solution.py:34
  221.7 3.3 %pair_sums.1 = (f32[144,384]{1,0:T(8,128)}, bf16[144,384]{1,0:T(8,128)(2,1)}) custom-call(f32[2,256,128]{2,1,0:T(8,128)} %slice.133.keep_ref, bf16[2,256,128]{2,1,0:T(8,128)(2,1)} %copy-done.11, f32[5,256,128]{2,1,0:T(8,128)} %get-tuple-element.69.cos_ref, f32[5,256,128]{2,1,0:T(8,128)} %get-tuple-element.70.sin_ref, ...), custom_call_target="tpu_custom_call" | custom-call | tf_op jit(solution)/shard_map/pair_sums/pallas_call | solution.py:768
  225.0 1.4 collective-permute-start.27
  226.4 1.6 fusion.6
  228.0 2.0 collective-permute-done.27
  229.9 9.1 %collective-permute-start.23 = (bf16[256,128]{1,0:T(8,128)(2,1)S(1)}, bf16[256,128]{1,0:T(8,128)(2,1)S(1)}, u32[]{:S(2)}, u32[]{:S(2)}) collective-permute-start(bf16[256,128]{1,0:T(8,128)(2,1)S(1)} %get-tuple-element.126), channel_id=1, source_target_pairs={{0,2},{2,0},{4,6},{6,4},{1,3},{3,1},{5,7},{7,5},{8,10},{10,8},{12,... | collective-permute-start | bytes 196616 | tf_op jit(solution)/shard_map/ppermute | solution.py:34
  239.1 1.6 fusion.3
  240.7 1.0 fusion
  242.3 4.8 %own_rows.1 = (bf16[2,256,384]{2,1,0:T(8,128)(2,1)}, bf16[2,256,384]{2,1,0:T(8,128)(2,1)}) custom-call(f32[1,256,128]{2,1,0:T(8,128)} %get-tuple-element.127.own_ref, bf16[256,128]{1,0:T(8,128)(2,1)} %copy-done.19, f32[5,256,128]{2,1,0:T(8,128)} %get-tuple-element.69.cos_ref, f32[5,256,128]{2,1,0:T(8,128)} %get-tuple-element.70.sin_ref, ...), custom_call_target="tpu_custom_call" | custom-call | tf_op jit(solution)/shard_map/own_rows/pallas_call | solution.py:822
  247.1 1.5 collective-permute-start.26
  249.6 2.1 collective-permute-start.29
  252.4 5.6 %collective-permute-done.38 = bf16[768,384]{1,0:T(8,128)(2,1)S(1)} collective-permute-done((bf16[768,384]{1,0:T(8,128)(2,1)}, bf16[768,384]{1,0:T(8,128)(2,1)S(1)}, u32[]{:S(2)}, u32[]{:S(2)}) %collective-permute-start.38) | collective-permute-done | bytes 589856 | tf_op jit(solution)/shard_map/ppermute | solution.py:34
  258.3 1.6 collective-permute-done.29
  260.5 4.3 %collective-permute-done.30 = bf16[144,384]{1,0:T(8,128)(2,1)S(1)} collective-permute-done((bf16[144,384]{1,0:T(8,128)(2,1)S(1)}, bf16[144,384]{1,0:T(8,128)(2,1)S(1)}, u32[]{:S(2)}, u32[]{:S(2)}) %collective-permute-start.30) | collective-permute-done | bytes 110624 | tf_op jit(solution)/shard_map/ppermute | solution.py:34
  266.7 5.0 %collective-permute-done.31 = bf16[144,384]{1,0:T(8,128)(2,1)S(1)} collective-permute-done((bf16[144,384]{1,0:T(8,128)(2,1)S(1)}, bf16[144,384]{1,0:T(8,128)(2,1)S(1)}, u32[]{:S(2)}, u32[]{:S(2)}) %collective-permute-start.31) | collective-permute-done | bytes 110624 | tf_op jit(solution)/shard_map/ppermute | solution.py:34
  276.8 1.1 fusion.1
  278.0 1.1 pad_maximum_fusion
  (164 shorter events, 30.3 us)
Async XLA Ops:
  6.7 10.4 %collective-permute-start = (bf16[400,384]{1,0:T(8,128)(2,1)}, bf16[400,384]{1,0:T(8,128)(2,1)S(1)}, u32[]{:S(2)}, u32[]{:S(2)}) collective-permute-start(bf16[400,384]{1,0:T(8,128)(2,1)} %get-tuple-element.67.pack_ref), channel_id=1, source_target_pairs={{0,1},{1,0},{2,3},{3,2},{4,5},{5,4},{6,7},{7,6},{8,9},{9,8},{10,11... | collective-permute-start | bytes 921608 | tf_op jit(solution)/shard_map/ppermute | solution.py:34
  9.7 13.7 %collective-permute-start.7 = (bf16[400,384]{1,0:T(8,128)(2,1)}, bf16[400,384]{1,0:T(8,128)(2,1)S(1)}, u32[]{:S(2)}, u32[]{:S(2)}) collective-permute-start(bf16[400,384]{1,0:T(8,128)(2,1)} %get-tuple-element.75), channel_id=1, source_target_pairs={{8,12},{10,14},{12,8},{14,10},{24,28},{26,30},{28,24},{30,26},{9,1... | collective-permute-start | bytes 921608 | tf_op jit(solution)/shard_map/ppermute | solution.py:43
  10.5 4.8 %collective-permute-start.9 = (bf16[192,768]{1,0:T(8,128)(2,1)S(1)}, bf16[192,768]{1,0:T(8,128)(2,1)S(1)}, u32[]{:S(2)}, u32[]{:S(2)}) collective-permute-start(bf16[192,768]{1,0:T(8,128)(2,1)S(1)} %constant_dynamic-slice_fusion.4), channel_id=1, source_target_pairs={{8,12},{10,14},{12,8},{14,10},{24,28},{26,30},{28,24},{30,26},{9,1... | collective-permute-start | bytes 884744 | tf_op jit(solution)/shard_map/ppermute | solution.py:55
  15.3 31.7 %collective-permute-start.10 = (bf16[192,768]{1,0:T(8,128)(2,1)S(1)}, bf16[192,768]{1,0:T(8,128)(2,1)S(1)}, u32[]{:S(2)}, u32[]{:S(2)}) collective-permute-start(bf16[192,768]{1,0:T(8,128)(2,1)S(1)} %collective-permute-done.9), channel_id=1, source_target_pairs={{8,24},{24,8},{9,25},{25,9},{10,26},{26,10},{11,27},{27,11},{12,28... | collective-permute-start | bytes 884744 | tf_op jit(solution)/shard_map/ppermute | solution.py:56
  21.5 7.6 %collective-permute-start.1 = (bf16[1,512,128]{2,1,0:T(8,128)(2,1)}, bf16[1,512,128]{2,1,0:T(8,128)(2,1)S(1)}, u32[]{:S(2)}, u32[]{:S(2)}) collective-permute-start(bf16[1,512,128]{2,1,0:T(8,128)(2,1)} %get-tuple-element.72), channel_id=1, source_target_pairs={{0,2},{2,0},{4,6},{6,4},{1,3},{3,1},{5,7},{7,5},{8,10},{10,8},{12,... | collective-permute-start | bytes 393224 | tf_op jit(solution)/shard_map/ppermute | solution.py:34
  23.4 24.3 %copy-start.16 = (bf16[400,384]{1,0:T(8,128)(2,1)}, bf16[400,384]{1,0:T(8,128)(2,1)S(1)}, u32[]{:S(2)}) copy-start(bf16[400,384]{1,0:T(8,128)(2,1)S(1)} %broadcast_select_fusion.6.small_ref.small0_ref) | copy-start | bytes 921604
  30.1 18.5 %collective-permute-start.5 = (bf16[2,512,128]{2,1,0:T(8,128)(2,1)S(1)}, bf16[2,512,128]{2,1,0:T(8,128)(2,1)S(1)}, u32[]{:S(2)}, u32[]{:S(2)}) collective-permute-start(bf16[2,512,128]{2,1,0:T(8,128)(2,1)S(1)} %pad_maximum_fusion.5), channel_id=1, source_target_pairs={{0,4},{2,6},{4,0},{6,2},{1,5},{3,7},{5,1},{7,3},{8,12},{10,14},{12... | collective-permute-start | bytes 786440 | tf_op jit(solution)/shard_map/ppermute | solution.py:34
  31.9 15.8 %collective-permute-start.12 = (bf16[384,384]{1,0:T(8,128)(2,1)S(1)}, bf16[384,384]{1,0:T(8,128)(2,1)S(1)}, u32[]{:S(2)}, u32[]{:S(2)}) collective-permute-start(bf16[384,384]{1,0:T(8,128)(2,1)S(1)} %constant_dynamic-slice_fusion.3), channel_id=1, source_target_pairs={{8,12},{10,14},{12,8},{14,10},{24,28},{26,30},{28,24},{30,26},{9,1... | collective-permute-start | bytes 884744 | tf_op jit(solution)/shard_map/ppermute | solution.py:55
  32.6 40.2 %collective-permute-start.8 = (bf16[400,384]{1,0:T(8,128)(2,1)S(1)}, bf16[400,384]{1,0:T(8,128)(2,1)S(1)}, u32[]{:S(2)}, u32[]{:S(2)}) collective-permute-start(bf16[400,384]{1,0:T(8,128)(2,1)S(1)} %broadcast_select_fusion.6.small_ref.small0_ref), channel_id=1, source_target_pairs={{0,1},{1,0},{2,3},{3,2},{4,5},{5,4},{6,7},{7,6},{8,9},{9,8},{10,11... | collective-permute-start | bytes 921608 | tf_op jit(solution)/shard_map/ppermute | solution.py:34
  33.2 39.9 %collective-permute-start.4 = (bf16[2,256,768]{2,1,0:T(8,128)(2,1)S(1)}, bf16[2,256,768]{2,1,0:T(8,128)(2,1)S(1)}, u32[]{:S(2)}, u32[]{:S(2)}) collective-permute-start(bf16[2,256,768]{2,1,0:T(8,128)(2,1)S(1)} %copy-done.24), channel_id=1, source_target_pairs={{0,8},{8,0},{16,24},{24,16},{1,9},{9,1},{17,25},{25,17},{2,10},{10... | collective-permute-start | bytes 2359304 | tf_op jit(solution)/shard_map/ppermute | solution.py:34
  47.0 24.5 %collective-permute-start.2 = (bf16[2,256,768]{2,1,0:T(8,128)(2,1)S(1)}, bf16[2,256,768]{2,1,0:T(8,128)(2,1)S(1)}, u32[]{:S(2)}, u32[]{:S(2)}) collective-permute-start(bf16[2,256,768]{2,1,0:T(8,128)(2,1)S(1)} %copy-done.24), channel_id=1, source_target_pairs={{0,2},{2,0},{4,6},{6,4},{1,3},{3,1},{5,7},{7,5},{8,10},{10,8},{12,... | collective-permute-start | bytes 2359304 | tf_op jit(solution)/shard_map/ppermute | solution.py:34
  47.7 2.6 collective-permute-start.13
  48.6 23.0 %collective-permute-start.6 = (bf16[4,512,128]{2,1,0:T(8,128)(2,1)S(1)}, bf16[4,512,128]{2,1,0:T(8,128)(2,1)S(1)}, u32[]{:S(2)}, u32[]{:S(2)}) collective-permute-start(bf16[4,512,128]{2,1,0:T(8,128)(2,1)S(1)} %pad_maximum_fusion.2), channel_id=1, source_target_pairs={{0,16},{8,24},{16,0},{24,8},{1,17},{9,25},{17,1},{25,9},{2,18},{10... | collective-permute-start | bytes 1572872 | tf_op jit(solution)/shard_map/ppermute | solution.py:34
  50.3 21.3 %copy-start.9 = (bf16[384,768]{1,0:T(8,128)(2,1)}, bf16[384,768]{1,0:T(8,128)(2,1)S(1)}, u32[]{:S(2)}) copy-start(bf16[384,768]{1,0:T(8,128)(2,1)S(1)} %maximum_select_fusion.up0_ref) | copy-start | bytes 1769476
  50.4 22.7 %collective-permute-start.11 = (bf16[384,768]{1,0:T(8,128)(2,1)S(1)}, bf16[384,768]{1,0:T(8,128)(2,1)S(1)}, u32[]{:S(2)}, u32[]{:S(2)}) collective-permute-start(bf16[384,768]{1,0:T(8,128)(2,1)S(1)} %maximum_select_fusion.up0_ref), channel_id=1, source_target_pairs={{0,1},{1,0},{2,3},{3,2},{4,5},{5,4},{6,7},{7,6},{8,9},{9,8},{10,11... | collective-permute-start | bytes 1769480 | tf_op jit(solution)/shard_map/ppermute | solution.py:34
  71.5 16.8 %collective-permute-start.3 = (bf16[2,256,768]{2,1,0:T(8,128)(2,1)S(1)}, bf16[2,256,768]{2,1,0:T(8,128)(2,1)}, u32[]{:S(2)}, u32[]{:S(2)}) collective-permute-start(bf16[2,256,768]{2,1,0:T(8,128)(2,1)S(1)} %collective-permute-done.2.both1_ref), channel_id=1, source_target_pairs={{0,8},{8,0},{16,24},{24,16},{1,9},{9,1},{17,25},{25,17},{2,10},{10... | collective-permute-start | bytes 2359304 | tf_op jit(solution)/shard_map/ppermute | solution.py:34
  71.6 16.7 %copy-start.10 = (bf16[768,384]{1,0:T(8,128)(2,1)}, bf16[768,384]{1,0:T(8,128)(2,1)S(1)}, u32[]{:S(2)}) copy-start(bf16[768,384]{1,0:T(8,128)(2,1)S(1)} %maximum_select_fusion.1.down0_ref) | copy-start | bytes 1769476
  71.7 15.8 %collective-permute-start.14 = (bf16[768,384]{1,0:T(8,128)(2,1)S(1)}, bf16[768,384]{1,0:T(8,128)(2,1)S(1)}, u32[]{:S(2)}, u32[]{:S(2)}) collective-permute-start(bf16[768,384]{1,0:T(8,128)(2,1)S(1)} %maximum_select_fusion.1.down0_ref), channel_id=1, source_target_pairs={{0,1},{1,0},{2,3},{3,2},{4,5},{5,4},{6,7},{7,6},{8,9},{9,8},{10,11... | collective-permute-start | bytes 1769480 | tf_op jit(solution)/shard_map/ppermute | solution.py:34
  72.8 30.4 %copy-start.20 = (bf16[8,512,128]{2,1,0:T(8,128)(2,1)}, bf16[8,512,128]{2,1,0:T(8,128)(2,1)S(1)}, u32[]{:S(2)}) copy-start(bf16[8,512,128]{2,1,0:T(8,128)(2,1)S(1)} %constant_dynamic-update-slice_fusion.kv0_ref) | copy-start | bytes 3145732
  72.8 31.3 %collective-permute-start.15 = (bf16[8,512,128]{2,1,0:T(8,128)(2,1)S(1)}, bf16[8,512,128]{2,1,0:T(8,128)(2,1)S(1)}, u32[]{:S(2)}, u32[]{:S(2)}) collective-permute-start(bf16[8,512,128]{2,1,0:T(8,128)(2,1)S(1)} %constant_dynamic-update-slice_fusion.kv0_ref), channel_id=1, source_target_pairs={{0,8},{8,0},{16,24},{24,16},{1,9},{9,1},{17,25},{25,17},{2,10},{10... | collective-permute-start | bytes 3145736 | tf_op jit(solution)/shard_map/ppermute | solution.py:34
  73.1 15.2 %copy-start.27 = (bf16[384,768]{1,0:T(8,128)(2,1)}, bf16[384,768]{1,0:T(8,128)(2,1)S(1)}, u32[]{:S(2)}) copy-start(bf16[384,768]{1,0:T(8,128)(2,1)S(1)} %collective-permute-done.11.up1_ref) | copy-start | bytes 1769476
  103.2 27.9 %collective-permute-start.16 = (bf16[1536,384]{1,0:T(8,128)(2,1)}, bf16[1536,384]{1,0:T(8,128)(2,1)S(1)}, u32[]{:S(2)}, u32[]{:S(2)}) collective-permute-start(bf16[1536,384]{1,0:T(8,128)(2,1)} %get-tuple-element.79), channel_id=1, source_target_pairs={{0,1},{1,0},{2,3},{3,2},{4,5},{5,4},{6,7},{7,6},{8,9},{9,8},{10,11... | collective-permute-start | bytes 3538952 | tf_op jit(solution)/shard_map/ppermute | solution.py:34
  105.1 26.0 %copy-start.5 = (bf16[1536,384]{1,0:T(8,128)(2,1)S(1)}, bf16[1536,384]{1,0:T(8,128)(2,1)}, u32[]{:S(2)}) copy-start(bf16[1536,384]{1,0:T(8,128)(2,1)} %get-tuple-element.86) | copy-start | bytes 3538948
  131.4 24.2 %collective-permute-start.17 = (bf16[1536,384]{1,0:T(8,128)(2,1)S(1)}, bf16[1536,384]{1,0:T(8,128)(2,1)S(1)}, u32[]{:S(2)}, u32[]{:S(2)}) collective-permute-start(bf16[1536,384]{1,0:T(8,128)(2,1)S(1)} %add_convert_fusion), channel_id=1, source_target_pairs={{8,12},{10,14},{12,8},{14,10},{24,28},{26,30},{28,24},{30,26},{9,1... | collective-permute-start | bytes 3538952 | tf_op jit(solution)/shard_map/ppermute | solution.py:43
  132.3 23.3 %collective-permute-start.18 = (bf16[2,256,768]{2,1,0:T(8,128)(2,1)}, bf16[2,256,768]{2,1,0:T(8,128)(2,1)}, u32[]{:S(2)}, u32[]{:S(2)}) collective-permute-start(bf16[2,256,768]{2,1,0:T(8,128)(2,1)} %get-tuple-element.85), channel_id=1, source_target_pairs={{0,8},{8,0},{16,24},{24,16},{1,9},{9,1},{17,25},{25,17},{2,10},{10... | collective-permute-start | bytes 2359304 | tf_op jit(solution)/shard_map/ppermute | solution.py:34
  156.7 7.4 %collective-permute-start.19 = (bf16[8,512,128]{2,1,0:T(8,128)(2,1)S(1)}, bf16[8,512,128]{2,1,0:T(8,128)(2,1)S(1)}, u32[]{:S(2)}, u32[]{:S(2)}) collective-permute-start(bf16[8,512,128]{2,1,0:T(8,128)(2,1)S(1)} %copy-done.23), channel_id=1, source_target_pairs={{0,8},{8,0},{16,24},{24,16},{1,9},{9,1},{17,25},{25,17},{2,10},{10... | collective-permute-start | bytes 3145736 | tf_op jit(solution)/shard_map/ppermute | solution.py:34
  164.2 15.7 %copy-start.1 = (f32[8,512,128]{2,1,0:T(8,128)S(1)}, f32[8,512,128]{2,1,0:T(8,128)}, u32[]{:S(2)}) copy-start(f32[8,512,128]{2,1,0:T(8,128)} %get-tuple-element.93) | copy-start | bytes 6291460
  165.3 14.5 %collective-permute-start.20 = (bf16[8,256,128]{2,1,0:T(8,128)(2,1)}, bf16[8,256,128]{2,1,0:T(8,128)(2,1)}, u32[]{:S(2)}, u32[]{:S(2)}) collective-permute-start(bf16[8,256,128]{2,1,0:T(8,128)(2,1)} %add_convert_fusion.3), channel_id=1, source_target_pairs={{0,1},{1,0},{2,3},{3,2},{4,5},{5,4},{6,7},{7,6},{8,9},{9,8},{10,11... | collective-permute-start | bytes 1572872 | tf_op jit(solution)/shard_map/ppermute | solution.py:34
  167.4 27.5 %copy-start.2 = (f32[2,256,768]{2,1,0:T(8,128)S(1)}, f32[2,256,768]{2,1,0:T(8,128)}, u32[]{:S(2)}) copy-start(f32[2,256,768]{2,1,0:T(8,128)} %get-tuple-element.100) | copy-start | bytes 4718596
  181.2 19.5 %collective-permute-start.21 = (bf16[4,256,128]{2,1,0:T(8,128)(2,1)S(1)}, bf16[4,256,128]{2,1,0:T(8,128)(2,1)S(1)}, u32[]{:S(2)}, u32[]{:S(2)}) collective-permute-start(bf16[4,256,128]{2,1,0:T(8,128)(2,1)S(1)} %slice.166), channel_id=1, source_target_pairs={{0,16},{8,24},{16,0},{24,8},{1,17},{9,25},{17,1},{25,9},{2,18},{10... | collective-permute-start | bytes 786440 | tf_op jit(solution)/shard_map/ppermute | solution.py:34
  196.3 13.8 %collective-permute-start.32 = (bf16[416,384]{1,0:T(8,128)(2,1)S(1)}, bf16[416,384]{1,0:T(8,128)(2,1)S(1)}, u32[]{:S(2)}, u32[]{:S(2)}) collective-permute-start(bf16[416,384]{1,0:T(8,128)(2,1)S(1)} %copy-done.29), channel_id=1, source_target_pairs={{0,1},{1,0},{2,3},{3,2},{4,5},{5,4},{6,7},{7,6},{8,9},{9,8},{10,11... | collective-permute-start | bytes 958472 | tf_op jit(solution)/shard_map/ppermute | solution.py:34
  197.8 42.9 %collective-permute-start.37 = (bf16[768,384]{1,0:T(8,128)(2,1)}, bf16[768,384]{1,0:T(8,128)(2,1)S(1)}, u32[]{:S(2)}, u32[]{:S(2)}) collective-permute-start(bf16[768,384]{1,0:T(8,128)(2,1)} %constant_dynamic-slice_fusion), channel_id=1, source_target_pairs={{0,8},{8,0},{16,24},{24,16},{1,9},{9,1},{17,25},{25,17},{2,10},{10... | collective-permute-start | bytes 1769480 | tf_op jit(solution)/shard_map/ppermute | solution.py:34
  197.8 43.9 %collective-permute-start.25 = (bf16[2,256,768]{2,1,0:T(8,128)(2,1)S(1)}, bf16[2,256,768]{2,1,0:T(8,128)(2,1)}, u32[]{:S(2)}, u32[]{:S(2)}) collective-permute-start(bf16[2,256,768]{2,1,0:T(8,128)(2,1)S(1)} %add_convert_fusion.1), channel_id=1, source_target_pairs={{0,2},{2,0},{4,6},{6,4},{1,3},{3,1},{5,7},{7,5},{8,10},{10,8},{12,... | collective-permute-start | bytes 2359304 | tf_op jit(solution)/shard_map/ppermute | solution.py:34
  200.3 41.4 %collective-permute-start.24 = (bf16[2,256,768]{2,1,0:T(8,128)(2,1)}, bf16[2,256,768]{2,1,0:T(8,128)(2,1)}, u32[]{:S(2)}, u32[]{:S(2)}) collective-permute-start(bf16[2,256,768]{2,1,0:T(8,128)(2,1)} %get-tuple-element.99), channel_id=1, source_target_pairs={{0,8},{8,0},{16,24},{24,16},{1,9},{9,1},{17,25},{25,17},{2,10},{10... | collective-permute-start | bytes 2359304 | tf_op jit(solution)/shard_map/ppermute | solution.py:34
  201.5 19.5 %collective-permute-start.22 = (bf16[2,256,128]{2,1,0:T(8,128)(2,1)S(1)}, bf16[2,256,128]{2,1,0:T(8,128)(2,1)S(1)}, u32[]{:S(2)}, u32[]{:S(2)}) collective-permute-start(bf16[2,256,128]{2,1,0:T(8,128)(2,1)S(1)} %slice.167), channel_id=1, source_target_pairs={{0,4},{2,6},{4,0},{6,2},{1,5},{3,7},{5,1},{7,3},{8,12},{10,14},{12... | collective-permute-start | bytes 393224 | tf_op jit(solution)/shard_map/ppermute | solution.py:34
  210.2 41.4 %collective-permute-start.33 = (bf16[416,384]{1,0:T(8,128)(2,1)S(1)}, bf16[416,384]{1,0:T(8,128)(2,1)}, u32[]{:S(2)}, u32[]{:S(2)}) collective-permute-start(bf16[416,384]{1,0:T(8,128)(2,1)S(1)} %add_convert_fusion.4), channel_id=1, source_target_pairs={{8,12},{10,14},{12,8},{14,10},{24,28},{26,30},{28,24},{30,26},{9,1... | collective-permute-start | bytes 958472 | tf_op jit(solution)/shard_map/ppermute | solution.py:43
  225.0 5.0 %collective-permute-start.27 = (bf16[144,384]{1,0:T(8,128)(2,1)}, bf16[144,384]{1,0:T(8,128)(2,1)S(1)}, u32[]{:S(2)}, u32[]{:S(2)}) collective-permute-start(bf16[144,384]{1,0:T(8,128)(2,1)} %get-tuple-element.107), channel_id=1, source_target_pairs={{0,1},{1,0},{2,3},{3,2},{4,5},{5,4},{6,7},{7,6},{8,9},{9,8},{10,11... | collective-permute-start | bytes 331784 | tf_op jit(solution)/shard_map/ppermute | solution.py:34
  229.9 11.8 %collective-permute-start.23 = (bf16[256,128]{1,0:T(8,128)(2,1)S(1)}, bf16[256,128]{1,0:T(8,128)(2,1)S(1)}, u32[]{:S(2)}, u32[]{:S(2)}) collective-permute-start(bf16[256,128]{1,0:T(8,128)(2,1)S(1)} %get-tuple-element.126), channel_id=1, source_target_pairs={{0,2},{2,0},{4,6},{6,4},{1,3},{3,1},{5,7},{7,5},{8,10},{10,8},{12,... | collective-permute-start | bytes 196616 | tf_op jit(solution)/shard_map/ppermute | solution.py:34
  240.7 8.0 %collective-permute-start.28 = (bf16[144,384]{1,0:T(8,128)(2,1)}, bf16[144,384]{1,0:T(8,128)(2,1)}, u32[]{:S(2)}, u32[]{:S(2)}) collective-permute-start(bf16[144,384]{1,0:T(8,128)(2,1)} %fusion.3), channel_id=1, source_target_pairs={{0,8},{8,0},{16,24},{24,16},{1,9},{9,1},{17,25},{25,17},{2,10},{10... | collective-permute-start | bytes 331784 | tf_op jit(solution)/shard_map/ppermute | solution.py:34
  241.6 16.3 %collective-permute-start.38 = (bf16[768,384]{1,0:T(8,128)(2,1)}, bf16[768,384]{1,0:T(8,128)(2,1)S(1)}, u32[]{:S(2)}, u32[]{:S(2)}) collective-permute-start(bf16[768,384]{1,0:T(8,128)(2,1)} %fusion), channel_id=1, source_target_pairs={{0,16},{8,24},{16,0},{24,8},{1,17},{9,25},{17,1},{25,9},{2,18},{10... | collective-permute-start | bytes 1769480 | tf_op jit(solution)/shard_map/ppermute | solution.py:34
  247.1 17.8 %collective-permute-start.26 = (bf16[2,256,384]{2,1,0:T(8,128)(2,1)}, bf16[2,256,384]{2,1,0:T(8,128)(2,1)S(1)}, u32[]{:S(2)}, u32[]{:S(2)}) collective-permute-start(bf16[2,256,384]{2,1,0:T(8,128)(2,1)} %get-tuple-element.103), channel_id=1, source_target_pairs={{0,1},{1,0},{2,3},{3,2},{4,5},{5,4},{6,7},{7,6},{8,9},{9,8},{10,11... | collective-permute-start | bytes 1179656 | tf_op jit(solution)/shard_map/ppermute | solution.py:34
  249.6 10.4 %collective-permute-start.29 = (bf16[144,384]{1,0:T(8,128)(2,1)S(1)}, bf16[144,384]{1,0:T(8,128)(2,1)S(1)}, u32[]{:S(2)}, u32[]{:S(2)}) collective-permute-start(bf16[144,384]{1,0:T(8,128)(2,1)S(1)} %get-tuple-element.118), channel_id=1, source_target_pairs={{0,16},{8,24},{16,0},{24,8},{1,17},{9,25},{17,1},{25,9},{2,18},{10... | collective-permute-start | bytes 331784 | tf_op jit(solution)/shard_map/ppermute | solution.py:34
  251.7 8.4 %collective-permute-start.34 = (bf16[208,384]{1,0:T(8,128)(2,1)S(1)}, bf16[208,384]{1,0:T(8,128)(2,1)S(1)}, u32[]{:S(2)}, u32[]{:S(2)}) collective-permute-start(bf16[208,384]{1,0:T(8,128)(2,1)S(1)} %constant_dynamic-slice_fusion.2), channel_id=1, source_target_pairs={{0,8},{8,0},{16,24},{24,16},{1,9},{9,1},{17,25},{25,17},{2,10},{10... | collective-permute-start | bytes 479240 | tf_op jit(solution)/shard_map/ppermute | solution.py:34
  258.3 18.4 %collective-permute-start.39 = (bf16[768,384]{1,0:T(8,128)(2,1)S(1)}, bf16[768,384]{1,0:T(8,128)(2,1)S(1)}, u32[]{:S(2)}, u32[]{:S(2)}) collective-permute-start(bf16[768,384]{1,0:T(8,128)(2,1)S(1)} %add_convert_fusion.2), channel_id=1, source_target_pairs={{0,8},{8,0},{16,24},{24,16},{1,9},{9,1},{17,25},{25,17},{2,10},{10... | collective-permute-start | bytes 1769480 | tf_op jit(solution)/shard_map/ppermute | solution.py:34
  260.0 4.8 %collective-permute-start.30 = (bf16[144,384]{1,0:T(8,128)(2,1)S(1)}, bf16[144,384]{1,0:T(8,128)(2,1)S(1)}, u32[]{:S(2)}, u32[]{:S(2)}) collective-permute-start(bf16[144,384]{1,0:T(8,128)(2,1)S(1)} %fusion.4), channel_id=1, source_target_pairs={{0,2},{2,0},{4,6},{6,4},{1,3},{3,1},{5,7},{7,5},{8,10},{10,8},{12,... | collective-permute-start | bytes 331784 | tf_op jit(solution)/shard_map/ppermute | solution.py:34
  260.1 12.3 %collective-permute-start.35 = (bf16[208,384]{1,0:T(8,128)(2,1)S(1)}, bf16[208,384]{1,0:T(8,128)(2,1)S(1)}, u32[]{:S(2)}, u32[]{:S(2)}) collective-permute-start(bf16[208,384]{1,0:T(8,128)(2,1)S(1)} %fusion.2), channel_id=1, source_target_pairs={{0,16},{8,24},{16,0},{24,8},{1,17},{9,25},{17,1},{25,9},{2,18},{10... | collective-permute-start | bytes 479240 | tf_op jit(solution)/shard_map/ppermute | solution.py:34
  264.8 6.9 %collective-permute-start.31 = (bf16[144,384]{1,0:T(8,128)(2,1)S(1)}, bf16[144,384]{1,0:T(8,128)(2,1)S(1)}, u32[]{:S(2)}, u32[]{:S(2)}) collective-permute-start(bf16[144,384]{1,0:T(8,128)(2,1)S(1)} %fusion.7), channel_id=1, source_target_pairs={{0,4},{2,6},{4,0},{6,2},{1,5},{3,7},{5,1},{7,3},{8,12},{10,14},{12... | collective-permute-start | bytes 331784 | tf_op jit(solution)/shard_map/ppermute | solution.py:34
  272.5 1.5 collective-permute-start.36
  (23 other events, 143.8 us)

commit v3 on v2

--- a/solution.py
+++ b/solution.py
@@ -44,20 +44,17 @@
     return jnp.where(lax.rem(lax.axis_index("seq"), 2) == 0, value, moved)
 
 
-def fetch_quarter(value):
-    seq_count, row_count = lax.axis_size("seq"), lax.axis_size("row")
-    seq_me = lax.axis_index("seq")
-    odd = range(1, seq_count, 2)
-    over_z = [(s * row_count + r, s * row_count + (r ^ 2)) for s in odd for r in range(row_count)]
-    over_x = [(s, s ^ 2) for s in odd]
-    side = lax.rem(seq_me // 2, 2)
-    half = value.shape[0] // 2
-    got = lax.ppermute(lax.dynamic_slice_in_dim(value, side * half, half, 0), ("seq", "row"), over_z)
-    other = lax.ppermute(got, "seq", over_x)
-    low = jnp.where(side == 0, got, other)
-    high = jnp.where(side == 0, other, got)
-    moved = jnp.concatenate([low, high], axis=0)
-    return jnp.where(lax.rem(seq_me, 2) == 0, value, moved)
+def swap_some(value, axis, bit, parity):
+    sizes = [lax.axis_size(name) for name in ("seq", "row", "col")]
+    pairs = []
+    for s in range(parity, sizes[0], 2):
+        for r in range(sizes[1]):
+            for c in range(sizes[2]):
+                index = {"seq": s, "row": r, "col": c}
+                source = (s * sizes[1] + r) * sizes[2] + c
+                index[axis] ^= bit
+                pairs.append((source, (index["seq"] * sizes[1] + index["row"]) * sizes[2] + index["col"]))
+    return lax.ppermute(value, ("seq", "row", "col"), pairs)
 
 
 def swap_add(value, axis, bit):
@@ -90,25 +87,18 @@
     vec_ref,
     small0_ref,
     small1_ref,
+    stats_ref,
     kv0_ref,
     kv1_ref,
     *rest,
     shape,
-    second,
 ):
     heads = shape.heads
-    rest = list(rest)
-    if second:
-        stats_ref, dqw_in_ref, dow_in_ref, dqb_in_ref, dkv_in_ref = rest[:5]
-        rest = rest[5:]
-        stay_ref, go_ref, keep_ref, send_ref, stat_ref, dkv_out_ref, last_ref = rest[:7]
-        dqw_ref, dow_ref, dqb_ref = rest[7:10]
-        rest = rest[10:]
-    else:
-        stay_ref, go_ref, dqw_ref, dow_ref, dqb_ref, dkv_out_ref, last_ref = rest[:7]
-        rest = rest[7:]
+    stay_ref, go_ref, keep_ref, send_ref, stat_ref, dkv_out_ref, dkv_low_ref, cache_ref = rest[:8]
+    dqw_ref, dow_ref, dqb_ref = rest[8:11]
+    rest = rest[11:]
     (
-    qd_ref,
+        qd_ref,
         probs_ref,
         high_ref,
         sums_ref,
@@ -118,6 +108,7 @@
         dkv_ref,
         kv_ref,
         low_ref,
+        zero_ref,
         qw_ref,
         ow_ref,
         copy_sem,
@@ -129,9 +120,7 @@
     lanes = 2 * HD
     rows = heads * HALF
     seq, row, second_half = meta_ref[0], meta_ref[1], meta_ref[2]
-    own_block = lax.bitwise_xor(seq, slot) * shape.row_count + lax.bitwise_xor(
-        row, 1 - slot if second else slot
-    )
+    own_block = lax.bitwise_xor(seq, slot // 2) * shape.row_count + lax.bitwise_xor(row, slot % 2)
     first_block = first_of(meta_ref, own_block, shape)
     before = own_block - first_block
 
@@ -143,44 +132,45 @@
         )
 
     def put(index, rows):
-        @pl.when(slot == 0)
+        @pl.when(slot < 2)
         def _():
-            stay_ref[index] = rows
-
-        @pl.when(slot == 1)
+            stay_ref[slot, index] = rows
+
+        @pl.when(slot >= 2)
         def _():
-            go_ref[index] = rows.astype(BF16)
+            go_ref[slot - 2, index] = rows.astype(BF16)
+
+    def cache_copies(dealt, group):
+        copies = []
+        for i in range(dealt):
+            owner = meta_ref[3 + shape.sequences + group * dealt + i]
+            for part in (0, 1):
+                take = jnp.where(second_half > 0, 1 - part, part) * HALF
+                copies.append(
+                    pltpu.make_async_copy(
+                        kv_ref.at[slot_of(owner), pl.ds(take, HALF), :],
+                        cache_ref.at[i, part * HALF : (part + 1) * HALF, :],
+                        copy_sem.at[2 + 2 * i + part],
+                    )
+                )
+        return copies
 
     pieces = [
         pltpu.make_async_copy(piece, kv_ref.at[i * half : (i + 1) * half], copy_sem.at[i])
         for i, piece in enumerate((kv0_ref, kv1_ref))
     ]
-    if second:
-        late = [
-            pltpu.make_async_copy(source, target, late_sem.at[i])
-            for i, (source, target) in enumerate(
-                (
-                    (dkv_in_ref, dkv_ref),
-                    (dqw_in_ref, dqw_ref),
-                    (dow_in_ref, dow_ref),
-                    (dqb_in_ref, dqb_ref),
-                )
-            )
-        ]
-    else:
-        late = [
-            pltpu.make_async_copy(low_ref, dkv_ref.at[i : i + 1], late_sem.at[i]) for i in range(blocks)
-        ]
+    late = [
+        pltpu.make_async_copy(zero_ref, dkv_ref.at[i : i + 1], late_sem.at[i]) for i in range(blocks)
+    ]
 
     @pl.when(slot == 0)
     def _():
         for copy in pieces:
             copy.start()
-        if not second:
-            low_ref[...] = jnp.zeros_like(low_ref)
-            dqw_ref[...] = jnp.zeros_like(dqw_ref)
-            dow_ref[...] = jnp.zeros_like(dow_ref)
-            dqb_ref[...] = jnp.zeros_like(dqb_ref)
+        zero_ref[...] = jnp.zeros_like(zero_ref)
+        dqw_ref[...] = jnp.zeros_like(dqw_ref)
+        dow_ref[...] = jnp.zeros_like(dow_ref)
+        dqb_ref[...] = jnp.zeros_like(dqb_ref)
         for copy in late:
             copy.start()
         span = small0_ref.shape[1]
@@ -321,68 +311,57 @@
     put(1, ff_grad_ref[0] + dot(joined, qw_ref[...]) * vec_ref[0:1, :])
     dqw_ref[...] += dot(joined, first_ref[0], TN)
 
-    @pl.when(slot == 1)
+    @pl.when(slot == 0)
     def _():
-        if not second:
-            copies = [pltpu.make_async_copy(dkv_ref, dkv_out_ref, copy_sem.at[0])]
-            dealt = last_ref.shape[0]
-            group = seq * 2 + second_half
-            for i in range(dealt):
-                owner = meta_ref[3 + shape.sequences + group * dealt + i]
-                for part in (0, 1):
-                    take = jnp.where(second_half > 0, 1 - part, part) * HALF
-                    copies.append(
-                        pltpu.make_async_copy(
-                            kv_ref.at[slot_of(owner), pl.ds(take, HALF), :],
-                            last_ref.at[i, part * HALF : (part + 1) * HALF, :],
-                            copy_sem.at[1 + 2 * i + part],
-                        )
-                    )
-            for copy in copies:
-                copy.start()
+        dealt = cache_ref.shape[0]
+        group = seq * 2 + second_half
+        for copy in cache_copies(dealt, group):
+            copy.start()
+
+    @pl.when(slot == 3)
+    def _():
+        copies = [pltpu.make_async_copy(dkv_ref.at[:half], dkv_out_ref, copy_sem.at[0])]
+        copies[0].start()
+        if dkv_ref.dtype == BF16:
+            copies.append(pltpu.make_async_copy(dkv_ref.at[half:], dkv_low_ref, copy_sem.at[1]))
         else:
-            copies = [pltpu.make_async_copy(dkv_ref.at[:half], dkv_out_ref, copy_sem.at[0])]
-            copies[0].start()
-            if dkv_ref.dtype == BF16:
-                copies.append(pltpu.make_async_copy(dkv_ref.at[half:], last_ref, copy_sem.at[1]))
-            else:
-                low_ref[...] = dkv_ref[half:].astype(BF16)
-                copies.append(pltpu.make_async_copy(low_ref, last_ref, copy_sem.at[1]))
-            copies[1].start()
-            count = heads * HD
-            span = small0_ref.shape[1]
-            bias_up = stats_ref[2:3, :]
-            bias_q = dqb_ref[...]
-            for i, target in enumerate((keep_ref, send_ref)):
-                part = slice(i * span, (i + 1) * span)
-                target[:count, :] = dqw_ref[:count, part].astype(BF16)
-                target[count : 2 * count, :] = dow_ref[:count, part].astype(BF16)
-                rows_of = jnp.concatenate(
-                    [
-                        bias_up[:, :span],
-                        bias_up[:, span:],
-                        jnp.concatenate([bias_q, jnp.zeros((1, span - padded), F32)], axis=1),
-                        jnp.zeros((5, span), F32),
-                    ],
-                    axis=0,
-                )
-                target[2 * count :, :] = jnp.concatenate(
-                    [rows_of, jnp.zeros((target.shape[0] - 2 * count - 8, span), F32)], axis=0
-                ).astype(BF16)
-            weight = qw_ref[...].astype(F32)
-            column = jnp.transpose(jnp.broadcast_to(bias_q, (8, padded)))[:, 0:1]
-            plain = jnp.sum(weight * column, axis=0, keepdims=True)
-            stat_ref[0:1, :] = (
-                jnp.sum(weight * dqw_ref[...], axis=0, keepdims=True) - vec_ref[1:2, :] * plain
-            ) / vec_ref[0:1, :]
-            stat_ref[1:2, :] = plain
-            stat_ref[2:8, :] = jnp.zeros((6, 2 * span), F32)
+            low_ref[...] = dkv_ref[half:].astype(BF16)
+            copies.append(pltpu.make_async_copy(low_ref, dkv_low_ref, copy_sem.at[1]))
+        copies[1].start()
+        copies += cache_copies(cache_ref.shape[0], seq * 2 + second_half)
+        count = heads * HD
+        span = small0_ref.shape[1]
+        bias_up = stats_ref[2:3, :]
+        bias_q = dqb_ref[...]
+        for i, target in enumerate((keep_ref, send_ref)):
+            part = slice(i * span, (i + 1) * span)
+            target[:count, :] = dqw_ref[:count, part].astype(BF16)
+            target[count : 2 * count, :] = dow_ref[:count, part].astype(BF16)
+            rows_of = jnp.concatenate(
+                [
+                    bias_up[:, :span],
+                    bias_up[:, span:],
+                    jnp.concatenate([bias_q, jnp.zeros((1, span - padded), F32)], axis=1),
+                    jnp.zeros((5, span), F32),
+                ],
+                axis=0,
+            )
+            target[2 * count :, :] = jnp.concatenate(
+                [rows_of, jnp.zeros((target.shape[0] - 2 * count - 8, span), F32)], axis=0
+            ).astype(BF16)
+        weight = qw_ref[...].astype(F32)
+        column = jnp.transpose(jnp.broadcast_to(bias_q, (8, padded)))[:, 0:1]
+        plain = jnp.sum(weight * column, axis=0, keepdims=True)
+        stat_ref[0:1, :] = (
+            jnp.sum(weight * dqw_ref[...], axis=0, keepdims=True) - vec_ref[1:2, :] * plain
+        ) / vec_ref[0:1, :]
+        stat_ref[1:2, :] = plain
+        stat_ref[2:8, :] = jnp.zeros((6, 2 * span), F32)
         for copy in copies:
             copy.wait()
 
 
-def attention(meta, first_in, dy, cosine, sine, ff, vectors, small, pieces, so_far, shape):
-    second = so_far is not None
+def attention(meta, first_in, dy, cosine, sine, ff, vectors, small, stats, pieces, shape):
     _, _, width = first_in.shape
     half = pieces[0].shape[0]
     blocks = 2 * half
@@ -393,10 +372,9 @@
     longest = min(LONGEST, blocks // 2)
     total_type = F32 if blocks <= 32 else BF16
     dealt = blocks // (2 * shape.seq_count)
-    offset = 2 if second else 0
 
     def per_slot(lanes):
-        return pl.BlockSpec((1, HALF, lanes), lambda i, m: (i + offset, 0, 0))
+        return pl.BlockSpec((1, HALF, lanes), lambda i, m: (i, 0, 0))
 
     def whole(array):
         return pl.BlockSpec(
@@ -404,39 +382,35 @@
         )
 
     far = pl.BlockSpec(memory_space=pltpu.MemorySpace.HBM)
-    arrays = [first_in, dy, cosine, sine, *ff, vectors, *small, *pieces]
+    arrays = [first_in, dy, cosine, sine, *ff, vectors, *small, stats, *pieces]
     in_specs = [per_slot(width), per_slot(width), per_slot(lanes), per_slot(lanes)]
-    in_specs += [per_slot(width)] * 2 + [whole(vectors)] + [whole(a) for a in small] + [far] * 2
-    weight = jax.ShapeDtypeStruct((padded, width), F32)
-    bias = jax.ShapeDtypeStruct((1, padded), F32)
-    tokens = jax.ShapeDtypeStruct((2, HALF, width), F32)
-    if second:
-        arrays += list(so_far)
-        in_specs += [whole(so_far[0])] + [far] * 4
-        part = jax.ShapeDtypeStruct((2 * heads * HD + 32, width // 2), BF16)
-        sums = [part, part, jax.ShapeDtypeStruct((8, width), F32)]
-        kept = [pltpu.VMEM(a.shape, F32) for a in (weight, weight, bias)]
-    else:
-        sums = [weight, weight, bias]
-        kept = []
+    in_specs += [per_slot(width)] * 2 + [whole(a) for a in (vectors, *small, stats)] + [far] * 2
+    part = jax.ShapeDtypeStruct((2 * heads * HD + 32, width // 2), BF16)
+    results = [
+        jax.ShapeDtypeStruct((2, 2, HALF, width), F32),
+        jax.ShapeDtypeStruct((2, 2, HALF, width), BF16),
+        part,
+        part,
+        jax.ShapeDtypeStruct((8, width), F32),
+    ]
     out_shape = [
-        tokens,
-        jax.ShapeDtypeStruct(tokens.shape, BF16),
-        *sums,
-        jax.ShapeDtypeStruct((half if second else blocks, BLOCK, lanes), total_type),
-        jax.ShapeDtypeStruct((half if second else dealt, BLOCK, lanes), BF16),
+        *results,
+        jax.ShapeDtypeStruct((half, BLOCK, lanes), total_type),
+        jax.ShapeDtypeStruct((half, BLOCK, lanes), BF16),
+        jax.ShapeDtypeStruct((dealt, BLOCK, lanes), BF16),
     ]
-    out_specs = [whole(tokens)] * 2 + [whole(a) for a in sums] + [far, far]
-    low = BF16 if second else total_type
+    out_specs = [whole(a) for a in results] + [far] * 3
     return pl.pallas_call(
-        functools.partial(attention_kernel, shape=shape, second=second),
+        functools.partial(attention_kernel, shape=shape),
         grid_spec=pltpu.PrefetchScalarGridSpec(
             num_scalar_prefetch=1,
-            grid=(2,),
+            grid=(4,),
             in_specs=in_specs,
             out_specs=out_specs,
-            scratch_shapes=kept
-            + [
+            scratch_shapes=[
+                pltpu.VMEM((padded, width), F32),
+                pltpu.VMEM((padded, width), F32),
+                pltpu.VMEM((1, padded), F32),
                 pltpu.VMEM((2 * rows, lanes), BF16),
                 pltpu.VMEM((longest, BLOCK, rows), BF16),
                 pltpu.VMEM((longest, rows), F32),
@@ -446,16 +420,17 @@
                 pltpu.VMEM((rows, lanes), F32),
                 pltpu.VMEM((blocks, BLOCK, lanes), total_type),
                 pltpu.VMEM((blocks, BLOCK, lanes), BF16),
-                pltpu.VMEM((half if second and blocks <= 32 else 1, BLOCK, lanes), low),
+                pltpu.VMEM((half if blocks <= 32 else 1, BLOCK, lanes), BF16),
+                pltpu.VMEM((1, BLOCK, lanes), total_type),
                 pltpu.VMEM((padded, width), BF16),
                 pltpu.VMEM((padded, width), BF16),
                 pltpu.SemaphoreType.DMA((2 + 2 * dealt,)),
-                pltpu.SemaphoreType.DMA((4 if second else blocks,)),
+                pltpu.SemaphoreType.DMA((blocks,)),
             ],
         ),
         out_shape=out_shape,
         cost_estimate=pl.CostEstimate(
-            flops=12_000_000_000, bytes_accessed=15_000_000, transcendentals=15_000_000
+            flops=24_000_000_000, bytes_accessed=30_000_000, transcendentals=30_000_000
         ),
         compiler_params=pltpu.CompilerParams(
             vmem_limit_bytes=67_043_328 if blocks > 32 else VMEM
@@ -464,7 +439,7 @@
     )(meta, *arrays)
 
 
-ORDER = (0, 3, 1, 2)
+ORDER = (0, 1, 2, 3)
 
 
 def tables_kernel(meta_ref, cos_ref, sin_ref, *, shape):
@@ -495,24 +470,29 @@
 
 
 def forward_kernel(
+    meta_ref,
     both0_ref,
-    both3_ref,
     both1_ref,
     both2_ref,
+    both3_ref,
     vec_ref,
-    small_ref,
-    up0_ref,
-    up1_ref,
-    down0_ref,
-    down1_ref,
+    pack_ref,
+    even_ref,
+    z_ref,
+    x_got_ref,
+    odd0_ref,
+    odd1_ref,
     first_ref,
     dy_ref,
     out_ref,
     dx_ref,
-    keep_ref,
-    send_ref,
+    grads_ref,
     stat_ref,
+    small0_ref,
+    small1_ref,
     x_ref,
+    own_ref,
+    other_ref,
     up_ref,
     down_ref,
     second_ref,
@@ -520,28 +500,64 @@
     grad_ref,
     dys_ref,
     bias_ref,
+    sem,
 ):
     step = pl.program_id(0)
-    span = up0_ref.shape[0]
+    span = pack_ref.shape[1]
+    total = pack_ref.shape[0]
     here = pl.ds(pl.multiple_of(step * HALF, HALF), HALF)
+    core = lax.rem(meta_ref[0], 2)
+    side = lax.rem(meta_ref[0] // 2, 2)
+
+    def run(copies):
+        for copy in copies:
+            copy.start()
+        for copy in copies:
+            copy.wait()
+
+    @pl.when((step == 0) & (core == 0))
+    def _():
+        run(
+            [
+                pltpu.make_async_copy(pack_ref, own_ref, sem.at[0]),
+                pltpu.make_async_copy(even_ref, other_ref, sem.at[1]),
+            ]
+        )
+
+    @pl.when((step == 0) & (core == 1))
+    def _():
+        half = total // 2
+        near = pl.ds(pl.multiple_of(side * half, half), half)
+        far = pl.ds(pl.multiple_of((1 - side) * half, half), half)
+        run(
+            [
+                pltpu.make_async_copy(z_ref, own_ref.at[near, :], sem.at[0]),
+                pltpu.make_async_copy(x_got_ref, own_ref.at[far, :], sem.at[1]),
+                pltpu.make_async_copy(odd0_ref, other_ref.at[near, :], sem.at[2]),
+                pltpu.make_async_copy(odd1_ref, other_ref.at[far, :], sem.at[3]),
+            ]
+        )
 
     @pl.when(step == 0)
     def _():
-        up_ref[:span, :] = up0_ref[...]
-        up_ref[span:, :] = up1_ref[...]
-        down_ref[:, :span] = down0_ref[...]
-        down_ref[:, span:] = down1_ref[...]
+        base = small0_ref.shape[0]
+        for i, held in enumerate((own_ref, other_ref)):
+            part = slice(i * span, (i + 1) * span)
+            (small0_ref, small1_ref)[i][...] = held[:base, :]
+            up_ref[part, :span] = held[base : base + span, :]
+            up_ref[part, span:] = held[base + span : base + 2 * span, :]
+            down_ref[:, part] = held[base + 2 * span : base + 4 * span, :]
         bias_ref[...] = jnp.zeros_like(bias_ref)
 
-    for i, piece in enumerate((both0_ref, both3_ref, both1_ref, both2_ref)):
+    for i, piece in enumerate((both0_ref, both1_ref, both2_ref, both3_ref)):
 
         @pl.when(step == i)
         def _():
             x_ref[...] = piece[0]
             dys_ref[here, :] = piece[1]
 
-    base = small_ref.shape[0] - 16
-    bias = small_ref[base : base + 8, :].astype(F32) + small_ref[base + 8 :, :].astype(F32)
+    base = small0_ref.shape[0] - 32
+    bias = own_ref[base : base + 8, :].astype(F32) + own_ref[base + 8 : base + 16, :].astype(F32)
     upward_b = jnp.concatenate([bias[5:6], bias[6:7]], axis=1)
     wide = x_ref[...].astype(F32)
     mean = jnp.mean(wide, axis=1, keepdims=True)
@@ -567,13 +583,13 @@
     @pl.when(step == 3)
     def _():
         down_grad = dot(hidden_ref[...], dys_ref[...], TN)
-        keep_ref[2 * span :, :] = down_grad[:, :span].astype(BF16)
-        send_ref[2 * span :, :] = down_grad[:, span:].astype(BF16)
+        grads_ref[0, 2 * span :, :] = down_grad[:, :span].astype(BF16)
+        grads_ref[1, 2 * span :, :] = down_grad[:, span:].astype(BF16)
         up_grad = dot(second_ref[...], grad_ref[...], TN)
         for i in (0, 1):
             part = slice(i * span, (i + 1) * span)
-            keep_ref[part, :] = up_grad[:span, part].astype(BF16)
-            send_ref[part, :] = up_grad[span:, part].astype(BF16)
+            grads_ref[0, part, :] = up_grad[:span, part].astype(BF16)
+            grads_ref[1, part, :] = up_grad[span:, part].astype(BF16)
         weight = up_ref[...].astype(F32)
         bias_grad = bias_ref[0:1, :]
 
@@ -588,10 +604,10 @@
         stat_ref[3:8, :] = jnp.zeros((5, 2 * span), F32)
 
 
-def feed_forward(both, vectors, small, up, down):
+def feed_forward(meta, both, vectors, weights, small_rows):
     width = vectors.shape[1]
     span = width // 2
-    hidden = up[0].shape[1]
+    total = weights[0].shape[0]
 
     def whole(array):
         return pl.BlockSpec(
@@ -599,36 +615,42 @@
         )
 
     slot = pl.BlockSpec((1, HALF, width), lambda i: (i, 0, 0))
-    arrays = [*both, vectors, small, *up, *down]
-    half = jax.ShapeDtypeStruct((2 * span + hidden, span), BF16)
+    arrays = [*both, vectors]
+    grads = jax.ShapeDtypeStruct((2, 4 * span, span), BF16)
     stat = jax.ShapeDtypeStruct((8, width), F32)
+    small = jax.ShapeDtypeStruct((small_rows, span), BF16)
     tokens = lambda kind: jax.ShapeDtypeStruct((4, HALF, width), kind)
     return pl.pallas_call(
         forward_kernel,
         grid=(4,),
-        in_specs=[whole(a) for a in arrays],
-        out_specs=[slot] * 4 + [whole(half), whole(half), whole(stat)],
-        out_shape=[tokens(BF16), tokens(BF16), tokens(F32), tokens(F32), half, half, stat],
+        in_specs=[pl.BlockSpec(memory_space=pltpu.SMEM)]
+        + [whole(a) for a in arrays]
+        + [pl.BlockSpec(memory_space=pltpu.MemorySpace.HBM)] * len(weights),
+        out_specs=[slot] * 4 + [whole(grads), whole(stat), whole(small), whole(small)],
+        out_shape=[tokens(BF16), tokens(BF16), tokens(F32), tokens(F32), grads, stat, small, small],
         scratch_shapes=[
             pltpu.VMEM((HALF, width), BF16),
-            pltpu.VMEM((width, hidden), BF16),
-            pltpu.VMEM((hidden, width), BF16),
+            pltpu.VMEM((total, span), BF16),
+            pltpu.VMEM((total, span), BF16),
+            pltpu.VMEM((width, width), BF16),
+            pltpu.VMEM((width, width), BF16),
             pltpu.VMEM((4 * HALF, width), BF16),
-            pltpu.VMEM((4 * HALF, hidden), BF16),
-            pltpu.VMEM((4 * HALF, hidden), BF16),
             pltpu.VMEM((4 * HALF, width), BF16),
-            pltpu.VMEM((8, hidden), F32),
+            pltpu.VMEM((4 * HALF, width), BF16),
+            pltpu.VMEM((4 * HALF, width), BF16),
+            pltpu.VMEM((8, width), F32),
+            pltpu.SemaphoreType.DMA((4,)),
         ],
         cost_estimate=pl.CostEstimate(
             flops=7_000_000_000, bytes_accessed=20_000_000, transcendentals=3_000_000
         ),
         compiler_params=pltpu.CompilerParams(vmem_limit_bytes=VMEM),
         name="feed_forward",
-    )(*arrays)
+    )(meta, *arrays, *weights)
 
 
 def prologue_kernel(
-    where_ref, tokens_ref, dy_ref, kvw_ref, qw_ref, ow_ref, vec_ref, pack_ref, x_ref, mine_ref, small_ref
+    where_ref, tokens_ref, dy_ref, kvw_ref, vec_ref, pack_ref, x_ref, mine_ref
 ):
     col = where_ref[2]
     span = dy_ref.shape[1]
@@ -647,30 +669,59 @@
         x_ref[part, :span] = tokens_ref[rows, pl.ds(pl.multiple_of(col * span, 128), span)]
         x_ref[part, span:] = tokens_ref[rows, pl.ds(pl.multiple_of((1 - col) * span, 128), span)]
     mine_ref[...] = dy_ref[here, :]
-    count = qw_ref.shape[0]
-    small_ref[:count, :] = qw_ref[...]
-    small_ref[count : 2 * count, :] = ow_ref[...]
-    small_ref[2 * count :, :] = both
-
-
-def prologue(col, tokens, cotangent, keyval_weight, query_weight, output_weight, vectors):
+
+
+def prologue(meta, tokens, cotangent, keyval_weight, vectors):
     width = tokens.shape[1]
     span = width // 2
     rows = vectors.shape[0]
-    count = query_weight.shape[0]
     vmem = pl.BlockSpec(memory_space=pltpu.VMEM)
     return pl.pallas_call(
         prologue_kernel,
-        in_specs=[pl.BlockSpec(memory_space=pltpu.SMEM)] + [vmem] * 6,
-        out_specs=[vmem] * 4,
+        in_specs=[pl.BlockSpec(memory_space=pltpu.SMEM)] + [vmem] * 4,
+        out_specs=[vmem] * 3,
         out_shape=[
             jax.ShapeDtypeStruct((HALF + 2 * HD + 2 * rows, span), BF16),
             jax.ShapeDtypeStruct((2 * HALF, width), BF16),
             jax.ShapeDtypeStruct((HALF, span), BF16),
-            jax.ShapeDtypeStruct((2 * count + 2 * rows, span), BF16),
         ],
         name="prologue",
-    )(col, tokens, cotangent, keyval_weight, query_weight, output_weight, vectors)
+    )(meta, tokens, cotangent, keyval_weight, vectors)
+
+
+def weights_kernel(where_ref, qw_ref, ow_ref, up_ref, down_ref, vec_ref, pack_ref, part_ref):
+    count = qw_ref.shape[0]
+    span = pack_ref.shape[1]
+    total = pack_ref.shape[0]
+    vectors = vec_ref[...]
+    high = vectors.astype(BF16).astype(F32)
+    both = jnp.concatenate([high, vectors - high], axis=0).astype(BF16)
+    pack_ref[:count, :] = qw_ref[...]
+    pack_ref[count : 2 * count, :] = ow_ref[...]
+    pack_ref[2 * count : 2 * count + 16, :] = both
+    pack_ref[2 * count + 16 : 2 * count + 32, :] = jnp.zeros((16, span), BF16)
+    base = 2 * count + 32
+    pack_ref[base : base + span, :] = up_ref[:, :span]
+    pack_ref[base + span : base + 2 * span, :] = up_ref[:, span:]
+    pack_ref[base + 2 * span :, :] = down_ref[...]
+    side = lax.rem(where_ref[0] // 2, 2)
+    part_ref[...] = pack_ref[pl.ds(pl.multiple_of(side * (total // 2), 16), total // 2), :]
+
+
+def pack_weights(meta, query_t, output_weight, upward_weight, down_weight, vectors):
+    span = output_weight.shape[1]
+    total = 2 * query_t.shape[0] + 32 + 2 * upward_weight.shape[0] + down_weight.shape[0]
+    vmem = pl.BlockSpec(memory_space=pltpu.VMEM)
+    return pl.pallas_call(
+        weights_kernel,
+        in_specs=[pl.BlockSpec(memory_space=pltpu.SMEM)] + [vmem] * 5,
+        out_specs=[vmem] * 2,
+        out_shape=[
+            jax.ShapeDtypeStruct((total, span), BF16),
+            jax.ShapeDtypeStruct((total // 2, span), BF16),
+        ],
+        name="pack_weights",
+    )(meta, query_t, output_weight, upward_weight, down_weight, vectors)
 
 
 def own_kernel(
@@ -736,9 +787,9 @@
         rolled = jnp.where(
             lane < ROT // 2, pltpu.roll(part, lanes - ROT // 2, 1), pltpu.roll(part, ROT // 2, 1)
         )
-        turned = part * cos_ref[2 * i] - rolled * sin_ref[2 * i]
+        turned = part * cos_ref[i] - rolled * sin_ref[i]
         bias = bias + jnp.sum(turned, axis=0, keepdims=True)
-        weight = weight + dot(turned.astype(BF16), first_ref[2 * i], TN)
+        weight = weight + dot(turned.astype(BF16), first_ref[i], TN)
     kvw = kvw_ref[...].astype(F32)
     column = jnp.transpose(jnp.broadcast_to(bias, (8, lanes)))[:, 0:1]
     plain = jnp.sum(kvw * column, axis=0, keepdims=True)
@@ -805,11 +856,11 @@
     spread = jnp.mean(wide * wide, axis=1, keepdims=True) - mean * mean
     root = lax.rsqrt(spread + EPS)
     normed = (wide - mean) * root
-    grad = keep_ref[1] + core_ref[1].astype(F32) + back_ref[1].astype(F32) + dot(turned, kvw_ref[...]) * vec_ref[0:1, :]
+    grad = keep_ref[0, 1] + core_ref[0, 1].astype(F32) + back_ref[1].astype(F32) + dot(turned, kvw_ref[...]) * vec_ref[0:1, :]
     one = jnp.mean(grad, axis=1, keepdims=True)
     two = jnp.mean(grad * normed, axis=1, keepdims=True)
     grad = dy_ref[0].astype(F32) + root * (grad - one - normed * two)
-    out = wide + keep_ref[0] + core_ref[0].astype(F32) + back_ref[0].astype(F32) + vec_ref[4:5, :]
+    out = wide + keep_ref[0, 0] + core_ref[0, 0].astype(F32) + back_ref[0].astype(F32) + vec_ref[4:5, :]
     for i, rows in enumerate((out.astype(BF16), grad.astype(BF16))):
         mine_ref[i] = rows[:, :span]
         send_ref[i] = rows[:, span:]
@@ -882,14 +933,15 @@
             jnp.zeros((span - head_width,), F32),
         ]
     ).reshape(8, span)
-    pack, x_block, dy_mine, small = prologue(
-        meta, tokens, cotangent, keyval_weight, jnp.transpose(query_weight), output_weight, vectors
-    )
+    pack, x_block, dy_mine = prologue(meta, tokens, cotangent, keyval_weight, vectors)
     received = swap(pack, "col", 1)
-    cosine, sine = tables(after(meta, pack), shape)
-
-    small_own = swap_odd_rows(small)
-    up_own = fetch_quarter(upward_weight)
+    weights, weights_half = pack_weights(
+        after(meta, pack), jnp.transpose(query_weight), output_weight, upward_weight, down_weight, vectors
+    )
+    weights_z = swap_some(weights_half, "row", 2, 1)
+    weights_even = swap_some(after(weights, received), "col", 1, 0)
+    cosine, sine = tables(after(meta, weights), shape)
+
     pairs, both, keyval_full, vec_full = own_pairs(
         x_block, dy_mine, pack, received, vectors, cosine, sine, keyval_bias[None]
     )
@@ -898,59 +950,59 @@
     while bit < seq_count:
         steps.append(("seq", bit))
         bit = bit * 2
-    small_full = (small_own, swap(small_own, "col", 1))
-    for i, (axis, bit) in enumerate(steps):
+    got = swap(pairs, "row", 1)
+    weights_x = swap_some(after(weights_z, got), "seq", 2, 1)
+    weights_odd0 = swap_some(after(weights_z, got), "col", 1, 1)
+    both_got = swap(after(both, got), "row", 1)
+    pairs = jnp.concatenate([pairs, got], axis=0)
+    got = swap(pairs, "row", 2)
+    weights_odd1 = swap_some(after(weights_x, got), "col", 1, 1)
+    got = after(got, weights_x, weights_odd0, weights_even)
+    for axis, bit in steps[2:]:
+        pairs = jnp.concatenate([pairs, got], axis=0)
         got = swap(pairs, axis, bit)
-        if i == 0:
-            both_got = swap(after(both, got), "row", 1)
-            down_own = fetch_quarter(after(down_weight, got))
-        pairs = jnp.concatenate([pairs, got], axis=0)
+    got = after(got, weights_odd1, both_got)
+    both_two = swap(after(both, got), "seq", 1)
+    both_three = swap(after(both_got, got), "seq", 1)
+    pairs = jnp.concatenate([pairs, got], axis=0)
     pieces = (pairs, swap(pairs, "seq", 1))
-    up_full = (up_own, swap(up_own, "col", 1))
-
-    first_in, dy_all, ff_out, ff_grad, ff_keep, ff_send, ff_stats = feed_forward(
-        (both, swap(both_got, "seq", 1), both_got, swap(both, "seq", 1)),
-        after(vec_full, got, small_full[1]),
-        small_own,
-        up_full,
-        (down_own, swap(down_own, "col", 1)),
-    )
-
-    ff_got = swap(ff_send, "col", 1)
-    ff = (ff_out, ff_grad)
-    stay_a, go_a, dquery_w, doutput_w, dquery_b, dpairs, cache_rows = attention(
-        after(meta, ff_send), first_in, dy_all, cosine, sine, ff, vec_full, small_full, pieces, None, shape
-    )
-    ff_sum = (after(ff_keep, go_a).astype(F32) + ff_got.astype(F32)).astype(BF16)
-    ff_moved = swap_odd_rows(ff_sum)
-    core_a = swap(go_a, "seq", 1)
-    stay_b, go_b, small_keep, small_send, stats, keep_pairs, send_pairs = attention(
-        after(meta, ff_sum),
+
+    first_in, dy_all, ff_out, ff_grad, ff_grads, ff_stats, small0, small1 = feed_forward(
+        meta,
+        (both, both_got, both_two, both_three),
+        vec_full,
+        (weights, weights_even, weights_z, weights_x, weights_odd0, weights_odd1),
+        2 * head_width + 32,
+    )
+
+    ff_z = swap_some(ff_grads, "row", 2, 1)
+    stay, go, small_keep, small_send, stats, keep_pairs, send_pairs, cache_rows = attention(
+        after(meta, ff_grads),
         first_in,
         dy_all,
         cosine,
         sine,
-        ff,
+        (ff_out, ff_grad),
         vec_full,
-        small_full,
+        (small0, small1),
+        ff_stats,
         pieces,
-        (ff_stats, dquery_w, doutput_w, dquery_b, dpairs),
         shape,
     )
 
-    send_pairs = after(send_pairs, ff_moved, core_a)
-    got = swap(send_pairs, "seq", 1)
+    got = swap(after(send_pairs, ff_z), "seq", 1)
     col_send = (keep_pairs[:, HALF:].astype(F32) + got[:, HALF:].astype(F32)).astype(BF16)
     col_got = swap(col_send, "col", 1)
-    away = (stay_b + core_a.astype(F32)).astype(BF16)
-    back = swap(after(away, got), "row", 1)
-    core_b = swap(after(go_b, col_send), "seq", 1)
+    core_got = swap(after(go, col_send), "seq", 1)
+    away = (stay[1] + core_got[1].astype(F32)).astype(BF16)
+    back = swap(away, "row", 1)
+    col_got = after(col_got, away)
     core = lax.rem(seq_me, 2)
 
-    def core_halves(moved):
-        half = moved.shape[0] // 2
-        keep = lax.dynamic_slice_in_dim(moved, core * half, half, 0)
-        return keep, lax.dynamic_slice_in_dim(moved, (1 - core) * half, half, 0)
+    def core_halves(moved, axis=0):
+        half = moved.shape[axis] // 2
+        keep = lax.dynamic_slice_in_dim(moved, core * half, half, axis)
+        return keep, lax.dynamic_slice_in_dim(moved, (1 - core) * half, half, axis)
 
     def over_seq(value):
         bit = 2
@@ -965,16 +1017,21 @@
         second = jnp.where(core == 0, other, value)
         return jnp.concatenate([first, second], axis=0).astype(F32)
 
-    ff_keep, ff_away = core_halves(after(ff_moved, col_send))
-    ff_part = over_seq(ff_keep.astype(F32) + swap(ff_away, "seq", 1).astype(F32))
+    ff_keep, ff_away = core_halves(jnp.where(core == 0, after(ff_grads, col_send), ff_z), 1)
+    ff_core = swap(ff_away, "seq", 1)
+    ff_col = swap(
+        after((ff_keep[1].astype(F32) + ff_core[1].astype(F32)).astype(BF16), col_got), "col", 1
+    )
+    ff_sum = ff_keep[0].astype(F32) + ff_core[0].astype(F32) + ff_col.astype(F32)
     total = keep_pairs[:, :HALF].astype(F32) + got[:, :HALF].astype(F32) + col_got.astype(F32)
-    small_got = swap(after(small_send, total), "col", 1)
+    small_got = swap(after(small_send, ff_col), "col", 1)
     small_sum = (small_keep.astype(F32) + small_got.astype(F32)).astype(BF16)
     for axis, bit in reversed(steps[2:]):
         half = total.shape[0] // 2
         total = total[:half] + swap(total[half:].astype(BF16), axis, bit).astype(F32)
-    row_got = swap(total[2:].astype(BF16), "row", 2)
-    small_moved = swap_odd_rows(after(small_sum, total))
+    total = after(total, back)
+    row_got = after(swap(total[2:].astype(BF16), "row", 2), ff_sum)
+    small_moved = swap_odd_rows(after(small_sum, row_got))
     keep_two = total[:2]
     dy_sum = jnp.sum(cotangent.astype(F32), axis=0)[None]
     z_send = (keep_two[1] + row_got[1].astype(F32)).astype(BF16)
@@ -985,7 +1042,7 @@
     extra = extra_mine + swap(extra_send, "col", 1).astype(F32)
     own_total = (keep_two[0] + row_got[0].astype(F32))[None]
     mine, away_rows = own_rows(
-        own_total, z_got, cosine, sine, keyval_full, vec_full, x_block, dy_all, stay_a, core_b, back
+        own_total, z_got, cosine, sine, keyval_full, vec_full, x_block, dy_all, stay, core_got, back
     )
     other = swap(away_rows, "col", 1)
     first = jnp.where(col_me == 0, mine, other)
@@ -993,7 +1050,7 @@
     layer_out = jnp.concatenate([first[0], second[0]], axis=0)
     grad_tokens = jnp.concatenate([first[1], second[1]], axis=0)
 
-    sum_ff = both_halves(ff_part)
+    sum_ff = both_halves(over_seq(ff_sum))
     sum_up = jnp.concatenate([sum_ff[:span], sum_ff[span : 2 * span]], axis=1)
     sum_down = sum_ff[2 * span :]
     keep, send = core_halves(small_moved)

time: 280 us -> 253 us (0.904)
  starting transfers between devices: 82.9 us -> 53.1 us
  waiting for transfers between devices: 90.8 us -> 74.3 us
  Pallas kernels: 71.9 us -> 85 us
  other arithmetic: 18.6 us -> 25.2 us
    ppermute x33 -> x29, starting transfers between devices: 77 us -> 43.2 us  [swap(): return lax.ppermute(value, axis, [(i, i ^ bit) for i in range(count)])]
    ppermute x33 -> x29, waiting for transfers between devices: 90.8 us -> 74.3 us  [swap(): return lax.ppermute(value, axis, [(i, i ^ bit) for i in range(count)])]
    pallas_call x3, Pallas kernels: 53.5 us -> 66 us  [the longest x1 46.9 us: attention(): pl.pallas_call(functools.partial(attention_kernel, shape=shape), grid_spe...]
    ppermute x4 -> x6, starting transfers between devices: 2.89 us -> 8.5 us  [swap_some(): return lax.ppermute(value, ('seq', 'row', 'col'), pairs)]
    convert_element_type x2, other arithmetic: 1.68 us -> 4.84 us  [the longest x1 2.79 us: on_device(): away = (stay[1] + core_got[1].astype(F32)).astype(BF16)]
    unnamed x66 -> x54, local copies, waits for them, and re-layouts: 5.79 us -> 4.79 us
  transfers between devices with their start and end apart: 40 -> 36, of which waited for: 15 -> 19; matrix products, arithmetic and copies ran while one was open for 7% -> 10% of each run, Pallas kernels for 25% -> 33%
where the time goes in v3:
time: 253 us; the launch traced here: 252 us
  Pallas kernels  85 us (34%)
  waiting for transfers between devices  74.3 us (29%)
  starting transfers between devices  53.1 us (21%)
  other arithmetic  25.2 us (10%)
  local copies, waits for them, and re-layouts  13 us (5%)
    ppermute x29, waiting for transfers between devices, swap(): return lax.ppermute(value, axis, [(i, i ^ bit) for i in range(count)])  74.3 us
    pallas_call x1, Pallas kernels, attention(): pl.pallas_call(functools.partial(attention_kernel, shape=shape), grid_spe...  46.9 us
    ppermute x29, starting transfers between devices, swap(): return lax.ppermute(value, axis, [(i, i ^ bit) for i in range(count)])  43.2 us
    pallas_call x1, Pallas kernels, feed_forward(): pl.pallas_call(forward_kernel, grid=(4,), in_specs=[pl.BlockSpec(memory_s...  16.2 us
    ppermute x6, starting transfers between devices, swap_some(): return lax.ppermute(value, ('seq', 'row', 'col'), pairs)  8.5 us
    pallas_call x1, Pallas kernels, own_rows(): pl.pallas_call(rows_kernel, in_specs=[vmem] * 11, out_specs=[vmem] * 2, o...  5.5 us
  transfers between devices with their start and end apart: 36, of which 19 were waited for; matrix products, arithmetic and copies ran while one was open for 10% of the time, Pallas kernels for 33%

profile of v3, /device:TPU:0, one launch (start us, length us, event | category | flops | bytes accessed | tf_op | source)
XLA Modules:
  0.0 251.6 jit_solution(2495811917475136800)
XLA Ops:
  2.8 1.3 concatenate.32.where_ref.meta_ref
  4.1 2.4 prologue.1
  6.5 3.0 %collective-permute-start = (bf16[400,384]{1,0:T(8,128)(2,1)}, bf16[400,384]{1,0:T(8,128)(2,1)S(1)}, u32[]{:S(2)}, u32[]{:S(2)}) collective-permute-start(bf16[400,384]{1,0:T(8,128)(2,1)} %get-tuple-element.70.pack_ref), channel_id=1, source_target_pairs={{0,1},{1,0},{2,3},{3,2},{4,5},{5,4},{6,7},{7,6},{8,9},{9,8},{10,11... | collective-permute-start | bytes 921608 | tf_op jit(solution)/shard_map/ppermute | solution.py:34
  9.4 2.9 %pack_weights.1 = (bf16[1952,384]{1,0:T(8,128)(2,1)}, bf16[976,384]{1,0:T(8,128)(2,1)}) custom-call(s32[22]{0:T(128)} %concatenate.32.where_ref.meta_ref, bf16[192,384]{1,0:T(8,128)(2,1)} %bitcast.30, bf16[192,384]{1,0:T(8,128)(2,1)} %ow_ref.1, bf16[384,768]{1,0:T(8,128)(2,1)} %up_ref.1, bf16[768,384]{1,0:T(8,128)(2,1)} %down_ref.1, f32[8,384]{1,0:T(8,128)} %reshape.57.vec_ref), custom_call_target="tpu_custom_call" | custom-call | tf_op jit(solution)/shard_map/pack_weights/pallas_call | solution.py:715
  13.0 3.9 %collective-permute-done.got_ref = bf16[400,384]{1,0:T(8,128)(2,1)S(1)} collective-permute-done((bf16[400,384]{1,0:T(8,128)(2,1)}, bf16[400,384]{1,0:T(8,128)(2,1)S(1)}, u32[]{:S(2)}, u32[]{:S(2)}) %collective-permute-start) | collective-permute-done | bytes 307232 | tf_op jit(solution)/shard_map/ppermute | solution.py:34
  16.9 3.6 %collective-permute-start.7 = (bf16[1952,384]{1,0:T(8,128)(2,1)}, bf16[1952,384]{1,0:T(8,128)(2,1)S(1)}, u32[]{:S(2)}, u32[]{:S(2)}) collective-permute-start(bf16[1952,384]{1,0:T(8,128)(2,1)} %get-tuple-element.81.pack_ref), channel_id=1, source_target_pairs={{0,1},{1,0},{2,3},{3,2},{4,5},{5,4},{6,7},{7,6},{16,17},{17,16},{1... | collective-permute-start | bytes 4497416 | tf_op jit(solution)/shard_map/ppermute | solution.py:57
  20.6 4.2 %tables.1 = (f32[5,256,128]{2,1,0:T(8,128)}, f32[5,256,128]{2,1,0:T(8,128)}) custom-call(s32[22]{0:T(128)} %concatenate.32.where_ref.meta_ref), custom_call_target="tpu_custom_call" | custom-call | tf_op jit(solution)/shard_map/tables/pallas_call | solution.py:463
  24.7 3.5 %own_pairs.1 = (bf16[1,512,128]{2,1,0:T(8,128)(2,1)}, bf16[2,256,768]{2,1,0:T(8,128)(2,1)}, bf16[128,768]{1,0:T(8,128)(2,1)}, f32[8,768]{1,0:T(8,128)}) custom-call(bf16[512,768]{1,0:T(8,128)(2,1)} %get-tuple-element.68.x_ref, bf16[256,384]{1,0:T(8,128)(2,1)} %get-tuple-element.69.mine_ref, bf16[400,384]{1,0:T(8,128)(2,1)} %get-tuple-element.70.pack_ref, ...), custom_call_target="tpu_custom_call" | custom-call | tf_op jit(solution)/shard_map/own_pairs/pallas_call | solution.py:762
  28.3 1.6 collective-permute-start.1
  29.9 6.4 %collective-permute-done.1 = bf16[1,512,128]{2,1,0:T(8,128)(2,1)S(1)} collective-permute-done((bf16[1,512,128]{2,1,0:T(8,128)(2,1)}, bf16[1,512,128]{2,1,0:T(8,128)(2,1)S(1)}, u32[]{:S(2)}, u32[]{:S(2)}) %collective-permute-start.1) | collective-permute-done | bytes 131104 | tf_op jit(solution)/shard_map/ppermute | solution.py:34
  38.7 1.7 collective-permute-start.3
  40.4 2.4 collective-permute-start.2
  42.8 11.0 %collective-permute-done.3 = bf16[2,512,128]{2,1,0:T(8,128)(2,1)S(1)} collective-permute-done((bf16[2,512,128]{2,1,0:T(8,128)(2,1)S(1)}, bf16[2,512,128]{2,1,0:T(8,128)(2,1)S(1)}, u32[]{:S(2)}, u32[]{:S(2)}) %collective-permute-start.3) | collective-permute-done | bytes 262176 | tf_op jit(solution)/shard_map/ppermute | solution.py:34
  56.5 1.6 collective-permute-start.8
  58.1 5.9 %collective-permute-done.2.both1_ref = bf16[2,256,768]{2,1,0:T(8,128)(2,1)S(1)} collective-permute-done((bf16[2,256,768]{2,1,0:T(8,128)(2,1)}, bf16[2,256,768]{2,1,0:T(8,128)(2,1)S(1)}, u32[]{:S(2)}, u32[]{:S(2)}) %collective-permute-start.2) | collective-permute-done | bytes 786464 | tf_op jit(solution)/shard_map/ppermute | solution.py:34
  63.9 6.4 %collective-permute-done.8 = bf16[4,512,128]{2,1,0:T(8,128)(2,1)S(1)} collective-permute-done((bf16[4,512,128]{2,1,0:T(8,128)(2,1)S(1)}, bf16[4,512,128]{2,1,0:T(8,128)(2,1)S(1)}, u32[]{:S(2)}, u32[]{:S(2)}) %collective-permute-start.8) | collective-permute-done | bytes 524320 | tf_op jit(solution)/shard_map/ppermute | solution.py:34
  72.0 1.1 collective-permute-done.10.both2_ref
  73.1 1.1 collective-permute-done.11.both3_ref
  75.2 16.2 %feed_forward.1 = (bf16[4,256,768]{2,1,0:T(8,128)(2,1)}, bf16[4,256,768]{2,1,0:T(8,128)(2,1)}, f32[4,256,768]{2,1,0:T(8,128)}, f32[4,256,768]{2,1,0:T(8,128)}, b...) custom-call(s32[22]{0:T(128)} %concatenate.32.where_ref.meta_ref, ...), custom_call_target="tpu_custom_call" | custom-call | flops 7000000000 | bytes 20000000 | tf_op jit(solution)/shard_map/feed_forward/pallas_call | solution.py:623
  91.4 2.1 collective-permute-start.13
  94.5 46.9 %attention.1 = (f32[2,2,256,768]{3,2,1,0:T(8,128)}, bf16[2,2,256,768]{3,2,1,0:T(8,128)(2,1)}, bf16[416,384]{1,0:T(8,128)(2,1)}, bf16[416,384]{1,0:T(8,128)(2,1)}...) custom-call(s32[22]{0:T(128)} %concatenate.32.where_ref.meta_ref, ...), custom_call_target="tpu_custom_call" | custom-call | flops 24000000000 | bytes 30000000 | tf_op jit(solution)/shard_map/attention/pallas_call | solution.py:403
  141.4 6.4 %collective-permute-start.14 = (bf16[8,512,128]{2,1,0:T(8,128)(2,1)}, bf16[8,512,128]{2,1,0:T(8,128)(2,1)S(1)}, u32[]{:S(2)}, u32[]{:S(2)}) collective-permute-start(bf16[8,512,128]{2,1,0:T(8,128)(2,1)} %get-tuple-element.99), channel_id=1, source_target_pairs={{0,8},{8,0},{16,24},{24,16},{1,9},{9,1},{17,25},{25,17},{2,10},{10... | collective-permute-start | bytes 3145736 | tf_op jit(solution)/shard_map/ppermute | solution.py:34
  147.9 2.5 collective-permute-done.14
  150.4 2.5 add_convert_fusion.3
  153.3 1.9 broadcast_select_fusion
  155.5 2.8 %collective-permute-done.20 = bf16[2,768,384]{2,1,0:T(8,128)(2,1)} collective-permute-done((bf16[2,768,384]{2,1,0:T(8,128)(2,1)S(1)}, bf16[2,768,384]{2,1,0:T(8,128)(2,1)}, u32[]{:S(2)}, u32[]{:S(2)}) %collective-permute-start.20) | collective-permute-done | bytes 1179680 | tf_op jit(solution)/shard_map/ppermute | solution.py:34
  158.4 2.0 fusion.1
  160.4 2.8 %fusion = bf16[2,256,768]{2,1,0:T(8,128)(2,1)} fusion(f32[2,2,256,768]{3,2,1,0:T(8,128)} %get-tuple-element.100.keep_ref, bf16[2,2,256,768]{3,2,1,0:T(8,128)(2,1)} %collective-permute-done.16.core_ref), kind=kLoop, calls=%fused_computation.9 | loop fusion | flops 1179648 | bytes 3145728 | tf_op jit(solution)/shard_map/convert_element_type | solution.py:997
  163.2 6.7 %collective-permute-done.15 = bf16[8,256,128]{2,1,0:T(8,128)(2,1)S(1)} collective-permute-done((bf16[8,256,128]{2,1,0:T(8,128)(2,1)}, bf16[8,256,128]{2,1,0:T(8,128)(2,1)S(1)}, u32[]{:S(2)}, u32[]{:S(2)}) %collective-permute-start.15) | collective-permute-done | bytes 524320 | tf_op jit(solution)/shard_map/ppermute | solution.py:34
  171.1 1.7 collective-permute-start.17
  174.5 4.8 %collective-permute-done.17 = bf16[4,256,128]{2,1,0:T(8,128)(2,1)} collective-permute-done((bf16[4,256,128]{2,1,0:T(8,128)(2,1)}, bf16[4,256,128]{2,1,0:T(8,128)(2,1)}, u32[]{:S(2)}, u32[]{:S(2)}) %collective-permute-start.17) | collective-permute-done | bytes 262176 | tf_op jit(solution)/shard_map/ppermute | solution.py:34
  180.3 4.9 %collective-permute-done.21 = bf16[768,384]{1,0:T(8,128)(2,1)} collective-permute-done((bf16[768,384]{1,0:T(8,128)(2,1)}, bf16[768,384]{1,0:T(8,128)(2,1)}, u32[]{:S(2)}, u32[]{:S(2)}) %collective-permute-start.21) | collective-permute-done | bytes 589856 | tf_op jit(solution)/shard_map/ppermute | solution.py:34
  185.7 13.5 %collective-permute-start.19 = (bf16[2,256,128]{2,1,0:T(8,128)(2,1)S(1)}, bf16[2,256,128]{2,1,0:T(8,128)(2,1)S(1)}, u32[]{:S(2)}, u32[]{:S(2)}) collective-permute-start(bf16[2,256,128]{2,1,0:T(8,128)(2,1)S(1)} %slice.193), channel_id=1, source_target_pairs={{0,4},{2,6},{4,0},{6,2},{1,5},{3,7},{5,1},{7,3},{8,12},{10,14},{12... | collective-permute-start | bytes 393224 | tf_op jit(solution)/shard_map/ppermute | solution.py:34
  199.2 2.3 reduce-precision_convert_fusion
  202.2 2.2 collective-permute-done.19.got_ref
  205.1 3.4 %pair_sums.1 = (f32[144,384]{1,0:T(8,128)}, bf16[144,384]{1,0:T(8,128)(2,1)}) custom-call(f32[2,256,128]{2,1,0:T(8,128)} %slice.130.keep_ref, bf16[2,256,128]{2,1,0:T(8,128)(2,1)} %copy-done.7, f32[5,256,128]{2,1,0:T(8,128)} %get-tuple-element.74.cos_ref, f32[5,256,128]{2,1,0:T(8,128)} %get-tuple-element.75.sin_ref, ...), custom_call_target="tpu_custom_call" | custom-call | tf_op jit(solution)/shard_map/pair_sums/pallas_call | solution.py:819
  208.4 1.2 collective-permute-start.24
  210.4 3.0 %collective-permute-done.24 = bf16[144,384]{1,0:T(8,128)(2,1)S(1)} collective-permute-done((bf16[144,384]{1,0:T(8,128)(2,1)}, bf16[144,384]{1,0:T(8,128)(2,1)S(1)}, u32[]{:S(2)}, u32[]{:S(2)}) %collective-permute-start.24) | collective-permute-done | bytes 110624 | tf_op jit(solution)/shard_map/ppermute | solution.py:34
  215.5 1.4 collective-permute-start.30
  217.6 5.5 %own_rows.1 = (bf16[2,256,384]{2,1,0:T(8,128)(2,1)}, bf16[2,256,384]{2,1,0:T(8,128)(2,1)}) custom-call(f32[1,256,128]{2,1,0:T(8,128)} %get-tuple-element.135.own_ref, bf16[256,128]{1,0:T(8,128)(2,1)} %copy-done.12, f32[5,256,128]{2,1,0:T(8,128)} %get-tuple-element.74.cos_ref, f32[5,256,128]{2,1,0:T(8,128)} %get-tuple-element.75.sin_ref, ...), custom_call_target="tpu_custom_call" | custom-call | tf_op jit(solution)/shard_map/own_rows/pallas_call | solution.py:873
  223.1 1.2 collective-permute-start.23
  224.7 1.7 collective-permute-start.35
  226.4 3.3 %collective-permute-done.26 = bf16[144,384]{1,0:T(8,128)(2,1)S(1)} collective-permute-done((bf16[144,384]{1,0:T(8,128)(2,1)S(1)}, bf16[144,384]{1,0:T(8,128)(2,1)S(1)}, u32[]{:S(2)}, u32[]{:S(2)}) %collective-permute-start.26) | collective-permute-done | bytes 110624 | tf_op jit(solution)/shard_map/ppermute | solution.py:34
  229.8 2.0 collective-permute-start.31
  231.9 3.7 %collective-permute-done.27 = bf16[144,384]{1,0:T(8,128)(2,1)S(1)} collective-permute-done((bf16[144,384]{1,0:T(8,128)(2,1)S(1)}, bf16[144,384]{1,0:T(8,128)(2,1)S(1)}, u32[]{:S(2)}, u32[]{:S(2)}) %collective-permute-start.27) | collective-permute-done | bytes 110624 | tf_op jit(solution)/shard_map/ppermute | solution.py:34
  235.6 1.6 collective-permute-start.28
  239.2 4.2 %collective-permute-done.28 = bf16[144,384]{1,0:T(8,128)(2,1)S(1)} collective-permute-done((bf16[144,384]{1,0:T(8,128)(2,1)S(1)}, bf16[144,384]{1,0:T(8,128)(2,1)S(1)}, u32[]{:S(2)}, u32[]{:S(2)}) %collective-permute-start.28) | collective-permute-done | bytes 110624 | tf_op jit(solution)/shard_map/ppermute | solution.py:34
  249.9 1.1 pad_maximum_fusion
  (137 shorter events, 31.0 us)
Async XLA Ops:
  6.5 10.4 %collective-permute-start = (bf16[400,384]{1,0:T(8,128)(2,1)}, bf16[400,384]{1,0:T(8,128)(2,1)S(1)}, u32[]{:S(2)}, u32[]{:S(2)}) collective-permute-start(bf16[400,384]{1,0:T(8,128)(2,1)} %get-tuple-element.70.pack_ref), channel_id=1, source_target_pairs={{0,1},{1,0},{2,3},{3,2},{4,5},{5,4},{6,7},{7,6},{8,9},{9,8},{10,11... | collective-permute-start | bytes 921608 | tf_op jit(solution)/shard_map/ppermute | solution.py:34
  12.3 24.0 %collective-permute-start.4 = (bf16[976,384]{1,0:T(8,128)(2,1)}, bf16[976,384]{1,0:T(8,128)(2,1)S(1)}, u32[]{:S(2)}, u32[]{:S(2)}) collective-permute-start(bf16[976,384]{1,0:T(8,128)(2,1)} %get-tuple-element.79), channel_id=1, source_target_pairs={{8,12},{9,13},{10,14},{11,15},{12,8},{13,9},{14,10},{15,11},{24,28... | collective-permute-start | bytes 2248712 | tf_op jit(solution)/shard_map/ppermute | solution.py:57
  16.9 7.8 %copy-start.11 = (bf16[400,384]{1,0:T(8,128)(2,1)}, bf16[400,384]{1,0:T(8,128)(2,1)S(1)}, u32[]{:S(2)}) copy-start(bf16[400,384]{1,0:T(8,128)(2,1)S(1)} %collective-permute-done.got_ref) | copy-start | bytes 921604
  16.9 38.5 %collective-permute-start.7 = (bf16[1952,384]{1,0:T(8,128)(2,1)}, bf16[1952,384]{1,0:T(8,128)(2,1)S(1)}, u32[]{:S(2)}, u32[]{:S(2)}) collective-permute-start(bf16[1952,384]{1,0:T(8,128)(2,1)} %get-tuple-element.81.pack_ref), channel_id=1, source_target_pairs={{0,1},{1,0},{2,3},{3,2},{4,5},{5,4},{6,7},{7,6},{16,17},{17,16},{1... | collective-permute-start | bytes 4497416 | tf_op jit(solution)/shard_map/ppermute | solution.py:57
  28.3 42.0 %copy-start.17 = (bf16[2,256,768]{2,1,0:T(8,128)(2,1)S(1)}, bf16[2,256,768]{2,1,0:T(8,128)(2,1)}, u32[]{:S(2)}) copy-start(bf16[2,256,768]{2,1,0:T(8,128)(2,1)} %get-tuple-element.85.both0_ref) | copy-start | bytes 2359300
  28.3 43.0 %copy-start.3 = (bf16[1,512,128]{2,1,0:T(8,128)(2,1)S(1)}, bf16[1,512,128]{2,1,0:T(8,128)(2,1)}, u32[]{:S(2)}) copy-start(bf16[1,512,128]{2,1,0:T(8,128)(2,1)} %get-tuple-element.77) | copy-start | bytes 393220
  28.3 8.0 %collective-permute-start.1 = (bf16[1,512,128]{2,1,0:T(8,128)(2,1)}, bf16[1,512,128]{2,1,0:T(8,128)(2,1)S(1)}, u32[]{:S(2)}, u32[]{:S(2)}) collective-permute-start(bf16[1,512,128]{2,1,0:T(8,128)(2,1)} %get-tuple-element.77), channel_id=1, source_target_pairs={{0,2},{2,0},{4,6},{6,4},{1,3},{3,1},{5,7},{7,5},{8,10},{10,8},{12,... | collective-permute-start | bytes 393224 | tf_op jit(solution)/shard_map/ppermute | solution.py:34
  36.3 35.1 %copy-start.21 = (bf16[976,384]{1,0:T(8,128)(2,1)}, bf16[976,384]{1,0:T(8,128)(2,1)S(1)}, u32[]{:S(2)}) copy-start(bf16[976,384]{1,0:T(8,128)(2,1)S(1)} %collective-permute-done.4.z_ref) | copy-start | bytes 2248708
  36.3 17.4 %collective-permute-start.5 = (bf16[976,384]{1,0:T(8,128)(2,1)S(1)}, bf16[976,384]{1,0:T(8,128)(2,1)S(1)}, u32[]{:S(2)}, u32[]{:S(2)}) collective-permute-start(bf16[976,384]{1,0:T(8,128)(2,1)S(1)} %collective-permute-done.4.z_ref), channel_id=1, source_target_pairs={{8,24},{9,25},{10,26},{11,27},{12,28},{13,29},{14,30},{15,31},{24,... | collective-permute-start | bytes 2248712 | tf_op jit(solution)/shard_map/ppermute | solution.py:57
  37.0 17.4 %collective-permute-start.6 = (bf16[976,384]{1,0:T(8,128)(2,1)S(1)}, bf16[976,384]{1,0:T(8,128)(2,1)S(1)}, u32[]{:S(2)}, u32[]{:S(2)}) collective-permute-start(bf16[976,384]{1,0:T(8,128)(2,1)S(1)} %collective-permute-done.4.z_ref), channel_id=1, source_target_pairs={{8,9},{9,8},{10,11},{11,10},{12,13},{13,12},{14,15},{15,14},{24,25... | collective-permute-start | bytes 2248712 | tf_op jit(solution)/shard_map/ppermute | solution.py:57
  38.7 15.1 %collective-permute-start.3 = (bf16[2,512,128]{2,1,0:T(8,128)(2,1)S(1)}, bf16[2,512,128]{2,1,0:T(8,128)(2,1)S(1)}, u32[]{:S(2)}, u32[]{:S(2)}) collective-permute-start(bf16[2,512,128]{2,1,0:T(8,128)(2,1)S(1)} %pad_maximum_fusion.5), channel_id=1, source_target_pairs={{0,4},{2,6},{4,0},{6,2},{1,5},{3,7},{5,1},{7,3},{8,12},{10,14},{12... | collective-permute-start | bytes 786440 | tf_op jit(solution)/shard_map/ppermute | solution.py:34
  40.4 23.5 %collective-permute-start.2 = (bf16[2,256,768]{2,1,0:T(8,128)(2,1)}, bf16[2,256,768]{2,1,0:T(8,128)(2,1)S(1)}, u32[]{:S(2)}, u32[]{:S(2)}) collective-permute-start(bf16[2,256,768]{2,1,0:T(8,128)(2,1)} %get-tuple-element.85.both0_ref), channel_id=1, source_target_pairs={{0,2},{2,0},{4,6},{6,4},{1,3},{3,1},{5,7},{7,5},{8,10},{10,8},{12,... | collective-permute-start | bytes 2359304 | tf_op jit(solution)/shard_map/ppermute | solution.py:34
  53.8 16.5 %copy-start.22 = (bf16[976,384]{1,0:T(8,128)(2,1)}, bf16[976,384]{1,0:T(8,128)(2,1)S(1)}, u32[]{:S(2)}) copy-start(bf16[976,384]{1,0:T(8,128)(2,1)S(1)} %collective-permute-done.5.x_got_ref) | copy-start | bytes 2248708
  53.8 10.2 %collective-permute-start.9 = (bf16[976,384]{1,0:T(8,128)(2,1)S(1)}, bf16[976,384]{1,0:T(8,128)(2,1)S(1)}, u32[]{:S(2)}, u32[]{:S(2)}) collective-permute-start(bf16[976,384]{1,0:T(8,128)(2,1)S(1)} %collective-permute-done.5.x_got_ref), channel_id=1, source_target_pairs={{8,9},{9,8},{10,11},{11,10},{12,13},{13,12},{14,15},{15,14},{24,25... | collective-permute-start | bytes 2248712 | tf_op jit(solution)/shard_map/ppermute | solution.py:57
  55.4 16.1 %copy-start.15 = (bf16[1952,384]{1,0:T(8,128)(2,1)}, bf16[1952,384]{1,0:T(8,128)(2,1)S(1)}, u32[]{:S(2)}) copy-start(bf16[1952,384]{1,0:T(8,128)(2,1)S(1)} %collective-permute-done.7.even_ref) | copy-start | bytes 4497412
  56.5 13.8 %collective-permute-start.8 = (bf16[4,512,128]{2,1,0:T(8,128)(2,1)S(1)}, bf16[4,512,128]{2,1,0:T(8,128)(2,1)S(1)}, u32[]{:S(2)}, u32[]{:S(2)}) collective-permute-start(bf16[4,512,128]{2,1,0:T(8,128)(2,1)S(1)} %pad_maximum_fusion.2), channel_id=1, source_target_pairs={{0,16},{8,24},{16,0},{24,8},{1,17},{9,25},{17,1},{25,9},{2,18},{10... | collective-permute-start | bytes 1572872 | tf_op jit(solution)/shard_map/ppermute | solution.py:34
  63.9 9.2 %copy-start.18 = (bf16[2,256,768]{2,1,0:T(8,128)(2,1)}, bf16[2,256,768]{2,1,0:T(8,128)(2,1)S(1)}, u32[]{:S(2)}) copy-start(bf16[2,256,768]{2,1,0:T(8,128)(2,1)S(1)} %collective-permute-done.2.both1_ref) | copy-start | bytes 2359300
  70.3 2.8 %collective-permute-start.10 = (bf16[2,256,768]{2,1,0:T(8,128)(2,1)S(1)}, bf16[2,256,768]{2,1,0:T(8,128)(2,1)S(1)}, u32[]{:S(2)}, u32[]{:S(2)}) collective-permute-start(bf16[2,256,768]{2,1,0:T(8,128)(2,1)S(1)} %copy-done.17), channel_id=1, source_target_pairs={{0,8},{8,0},{16,24},{24,16},{1,9},{9,1},{17,25},{25,17},{2,10},{10... | collective-permute-start | bytes 2359304 | tf_op jit(solution)/shard_map/ppermute | solution.py:34
  71.2 3.0 %collective-permute-start.11 = (bf16[2,256,768]{2,1,0:T(8,128)(2,1)S(1)}, bf16[2,256,768]{2,1,0:T(8,128)(2,1)S(1)}, u32[]{:S(2)}, u32[]{:S(2)}) collective-permute-start(bf16[2,256,768]{2,1,0:T(8,128)(2,1)S(1)} %collective-permute-done.2.both1_ref), channel_id=1, source_target_pairs={{0,8},{8,0},{16,24},{24,16},{1,9},{9,1},{17,25},{25,17},{2,10},{10... | collective-permute-start | bytes 2359304 | tf_op jit(solution)/shard_map/ppermute | solution.py:34
  71.5 19.9 %copy-start.13 = (bf16[8,512,128]{2,1,0:T(8,128)(2,1)}, bf16[8,512,128]{2,1,0:T(8,128)(2,1)S(1)}, u32[]{:S(2)}) copy-start(bf16[8,512,128]{2,1,0:T(8,128)(2,1)S(1)} %constant_dynamic-update-slice_fusion.kv0_ref) | copy-start | bytes 3145732
  71.5 22.0 %collective-permute-start.12 = (bf16[8,512,128]{2,1,0:T(8,128)(2,1)S(1)}, bf16[8,512,128]{2,1,0:T(8,128)(2,1)S(1)}, u32[]{:S(2)}, u32[]{:S(2)}) collective-permute-start(bf16[8,512,128]{2,1,0:T(8,128)(2,1)S(1)} %constant_dynamic-update-slice_fusion.kv0_ref), channel_id=1, source_target_pairs={{0,8},{8,0},{16,24},{24,16},{1,9},{9,1},{17,25},{25,17},{2,10},{10... | collective-permute-start | bytes 3145736 | tf_op jit(solution)/shard_map/ppermute | solution.py:34
  91.4 50.0 %collective-permute-start.13 = (bf16[2,1536,384]{2,1,0:T(8,128)(2,1)}, bf16[2,1536,384]{2,1,0:T(8,128)(2,1)}, u32[]{:S(2)}, u32[]{:S(2)}) collective-permute-start(bf16[2,1536,384]{2,1,0:T(8,128)(2,1)} %get-tuple-element.105), channel_id=1, source_target_pairs={{8,12},{9,13},{10,14},{11,15},{12,8},{13,9},{14,10},{15,11},{24,28... | collective-permute-start | bytes 7077896 | tf_op jit(solution)/shard_map/ppermute | solution.py:57
  141.4 8.9 %collective-permute-start.14 = (bf16[8,512,128]{2,1,0:T(8,128)(2,1)}, bf16[8,512,128]{2,1,0:T(8,128)(2,1)S(1)}, u32[]{:S(2)}, u32[]{:S(2)}) collective-permute-start(bf16[8,512,128]{2,1,0:T(8,128)(2,1)} %get-tuple-element.99), channel_id=1, source_target_pairs={{0,8},{8,0},{16,24},{24,16},{1,9},{9,1},{17,25},{25,17},{2,10},{10... | collective-permute-start | bytes 3145736 | tf_op jit(solution)/shard_map/ppermute | solution.py:34
  152.9 7.5 %collective-permute-start.16 = (bf16[2,2,256,768]{3,2,1,0:T(8,128)(2,1)}, bf16[2,2,256,768]{3,2,1,0:T(8,128)(2,1)}, u32[]{:S(2)}, u32[]{:S(2)}) collective-permute-start(bf16[2,2,256,768]{3,2,1,0:T(8,128)(2,1)} %get-tuple-element.102), channel_id=1, source_target_pairs={{0,8},{8,0},{16,24},{24,16},{1,9},{9,1},{17,25},{25,17},{2,10},{10... | collective-permute-start | bytes 4718600 | tf_op jit(solution)/shard_map/ppermute | solution.py:34
  155.3 3.0 %collective-permute-start.20 = (bf16[2,768,384]{2,1,0:T(8,128)(2,1)S(1)}, bf16[2,768,384]{2,1,0:T(8,128)(2,1)}, u32[]{:S(2)}, u32[]{:S(2)}) collective-permute-start(bf16[2,768,384]{2,1,0:T(8,128)(2,1)S(1)} %constant_dynamic-slice_fusion.2), channel_id=1, source_target_pairs={{0,8},{8,0},{16,24},{24,16},{1,9},{9,1},{17,25},{25,17},{2,10},{10... | collective-permute-start | bytes 3538952 | tf_op jit(solution)/shard_map/ppermute | solution.py:34
  155.5 14.4 %collective-permute-start.15 = (bf16[8,256,128]{2,1,0:T(8,128)(2,1)}, bf16[8,256,128]{2,1,0:T(8,128)(2,1)S(1)}, u32[]{:S(2)}, u32[]{:S(2)}) collective-permute-start(bf16[8,256,128]{2,1,0:T(8,128)(2,1)} %add_convert_fusion.3), channel_id=1, source_target_pairs={{0,1},{1,0},{2,3},{3,2},{4,5},{5,4},{6,7},{7,6},{8,9},{9,8},{10,11... | collective-permute-start | bytes 1572872 | tf_op jit(solution)/shard_map/ppermute | solution.py:34
  160.4 9.8 %copy-start.2 = (f32[8,512,128]{2,1,0:T(8,128)S(1)}, f32[8,512,128]{2,1,0:T(8,128)}, u32[]{:S(2)}) copy-start(f32[8,512,128]{2,1,0:T(8,128)} %get-tuple-element.97) | copy-start | bytes 6291460
  160.4 9.8 %copy-start.5 = (bf16[8,512,128]{2,1,0:T(8,128)(2,1)S(1)}, bf16[8,512,128]{2,1,0:T(8,128)(2,1)}, u32[]{:S(2)}) copy-start(bf16[8,512,128]{2,1,0:T(8,128)(2,1)} %copy-done.4) | copy-start | bytes 3145732
  163.2 22.5 %collective-permute-start.18 = (bf16[2,256,768]{2,1,0:T(8,128)(2,1)}, bf16[2,256,768]{2,1,0:T(8,128)(2,1)}, u32[]{:S(2)}, u32[]{:S(2)}) collective-permute-start(bf16[2,256,768]{2,1,0:T(8,128)(2,1)} %fusion), channel_id=1, source_target_pairs={{0,2},{2,0},{4,6},{6,4},{1,3},{3,1},{5,7},{7,5},{8,10},{10,8},{12,... | collective-permute-start | bytes 2359304 | tf_op jit(solution)/shard_map/ppermute | solution.py:34
  170.0 15.2 %collective-permute-start.21 = (bf16[768,384]{1,0:T(8,128)(2,1)}, bf16[768,384]{1,0:T(8,128)(2,1)}, u32[]{:S(2)}, u32[]{:S(2)}) collective-permute-start(bf16[768,384]{1,0:T(8,128)(2,1)} %fusion.1), channel_id=1, source_target_pairs={{0,1},{1,0},{2,3},{3,2},{4,5},{5,4},{6,7},{7,6},{8,9},{9,8},{10,11... | collective-permute-start | bytes 1769480 | tf_op jit(solution)/shard_map/ppermute | solution.py:34
  171.1 8.1 %collective-permute-start.17 = (bf16[4,256,128]{2,1,0:T(8,128)(2,1)}, bf16[4,256,128]{2,1,0:T(8,128)(2,1)}, u32[]{:S(2)}, u32[]{:S(2)}) collective-permute-start(bf16[4,256,128]{2,1,0:T(8,128)(2,1)} %slice.192), channel_id=1, source_target_pairs={{0,16},{8,24},{16,0},{24,8},{1,17},{9,25},{17,1},{25,9},{2,18},{10... | collective-permute-start | bytes 786440 | tf_op jit(solution)/shard_map/ppermute | solution.py:34
  180.3 21.2 %copy-start = (f32[4,256,128]{2,1,0:T(8,128)}, f32[4,256,128]{2,1,0:T(8,128)S(1)}, u32[]{:S(2)}) copy-start(f32[4,256,128]{2,1,0:T(8,128)S(1)} %slice_add_fusion) | copy-start | bytes 1572868
  185.2 29.3 %collective-permute-start.29 = (bf16[416,384]{1,0:T(8,128)(2,1)}, bf16[416,384]{1,0:T(8,128)(2,1)}, u32[]{:S(2)}, u32[]{:S(2)}) collective-permute-start(bf16[416,384]{1,0:T(8,128)(2,1)} %get-tuple-element.117), channel_id=1, source_target_pairs={{0,1},{1,0},{2,3},{3,2},{4,5},{5,4},{6,7},{7,6},{8,9},{9,8},{10,11... | collective-permute-start | bytes 958472 | tf_op jit(solution)/shard_map/ppermute | solution.py:34
  185.7 18.7 %collective-permute-start.19 = (bf16[2,256,128]{2,1,0:T(8,128)(2,1)S(1)}, bf16[2,256,128]{2,1,0:T(8,128)(2,1)S(1)}, u32[]{:S(2)}, u32[]{:S(2)}) collective-permute-start(bf16[2,256,128]{2,1,0:T(8,128)(2,1)S(1)} %slice.193), channel_id=1, source_target_pairs={{0,4},{2,6},{4,0},{6,2},{1,5},{3,7},{5,1},{7,3},{8,12},{10,14},{12... | collective-permute-start | bytes 393224 | tf_op jit(solution)/shard_map/ppermute | solution.py:34
  201.5 23.0 %collective-permute-start.34 = (bf16[768,384]{1,0:T(8,128)(2,1)}, bf16[768,384]{1,0:T(8,128)(2,1)S(1)}, u32[]{:S(2)}, u32[]{:S(2)}) collective-permute-start(bf16[768,384]{1,0:T(8,128)(2,1)} %get-tuple-element.124), channel_id=1, source_target_pairs={{0,16},{8,24},{16,0},{24,8},{1,17},{9,25},{17,1},{25,9},{2,18},{10... | collective-permute-start | bytes 1769480 | tf_op jit(solution)/shard_map/ppermute | solution.py:34
  208.4 5.0 %collective-permute-start.24 = (bf16[144,384]{1,0:T(8,128)(2,1)}, bf16[144,384]{1,0:T(8,128)(2,1)S(1)}, u32[]{:S(2)}, u32[]{:S(2)}) collective-permute-start(bf16[144,384]{1,0:T(8,128)(2,1)} %get-tuple-element.114), channel_id=1, source_target_pairs={{0,1},{1,0},{2,3},{3,2},{4,5},{5,4},{6,7},{7,6},{8,9},{9,8},{10,11... | collective-permute-start | bytes 331784 | tf_op jit(solution)/shard_map/ppermute | solution.py:34
  210.4 6.6 %collective-permute-start.22 = (bf16[256,128]{1,0:T(8,128)(2,1)S(1)}, bf16[256,128]{1,0:T(8,128)(2,1)S(1)}, u32[]{:S(2)}, u32[]{:S(2)}) collective-permute-start(bf16[256,128]{1,0:T(8,128)(2,1)S(1)} %get-tuple-element.134), channel_id=1, source_target_pairs={{0,2},{2,0},{4,6},{6,4},{1,3},{3,1},{5,7},{7,5},{8,10},{10,8},{12,... | collective-permute-start | bytes 196616 | tf_op jit(solution)/shard_map/ppermute | solution.py:34
  214.4 9.9 %collective-permute-start.25 = (bf16[144,384]{1,0:T(8,128)(2,1)S(1)}, bf16[144,384]{1,0:T(8,128)(2,1)S(1)}, u32[]{:S(2)}, u32[]{:S(2)}) collective-permute-start(bf16[144,384]{1,0:T(8,128)(2,1)S(1)} %fusion.4), channel_id=1, source_target_pairs={{0,8},{8,0},{16,24},{24,16},{1,9},{9,1},{17,25},{25,17},{2,10},{10... | collective-permute-start | bytes 331784 | tf_op jit(solution)/shard_map/ppermute | solution.py:34
  215.5 10.8 %collective-permute-start.30 = (bf16[416,384]{1,0:T(8,128)(2,1)S(1)}, bf16[416,384]{1,0:T(8,128)(2,1)}, u32[]{:S(2)}, u32[]{:S(2)}) collective-permute-start(bf16[416,384]{1,0:T(8,128)(2,1)S(1)} %add_convert_fusion.4), channel_id=1, source_target_pairs={{8,12},{10,14},{12,8},{14,10},{24,28},{26,30},{28,24},{30,26},{9,1... | collective-permute-start | bytes 958472 | tf_op jit(solution)/shard_map/ppermute | solution.py:43
  223.1 14.1 %collective-permute-start.23 = (bf16[2,256,384]{2,1,0:T(8,128)(2,1)}, bf16[2,256,384]{2,1,0:T(8,128)(2,1)S(1)}, u32[]{:S(2)}, u32[]{:S(2)}) collective-permute-start(bf16[2,256,384]{2,1,0:T(8,128)(2,1)} %get-tuple-element.110), channel_id=1, source_target_pairs={{0,1},{1,0},{2,3},{3,2},{4,5},{5,4},{6,7},{7,6},{8,9},{9,8},{10,11... | collective-permute-start | bytes 1179656 | tf_op jit(solution)/shard_map/ppermute | solution.py:34
  224.4 5.3 %collective-permute-start.26 = (bf16[144,384]{1,0:T(8,128)(2,1)S(1)}, bf16[144,384]{1,0:T(8,128)(2,1)S(1)}, u32[]{:S(2)}, u32[]{:S(2)}) collective-permute-start(bf16[144,384]{1,0:T(8,128)(2,1)S(1)} %get-tuple-element.126), channel_id=1, source_target_pairs={{0,16},{8,24},{16,0},{24,8},{1,17},{9,25},{17,1},{25,9},{2,18},{10... | collective-permute-start | bytes 331784 | tf_op jit(solution)/shard_map/ppermute | solution.py:34
  224.6 12.5 %copy-start.9 = (bf16[2,256,384]{2,1,0:T(8,128)(2,1)S(1)}, bf16[2,256,384]{2,1,0:T(8,128)(2,1)}, u32[]{:S(2)}) copy-start(bf16[2,256,384]{2,1,0:T(8,128)(2,1)} %get-tuple-element.109) | copy-start | bytes 1179652
  224.7 24.0 %collective-permute-start.35 = (bf16[768,384]{1,0:T(8,128)(2,1)S(1)}, bf16[768,384]{1,0:T(8,128)(2,1)S(1)}, u32[]{:S(2)}, u32[]{:S(2)}) collective-permute-start(bf16[768,384]{1,0:T(8,128)(2,1)S(1)} %add_convert_fusion.1), channel_id=1, source_target_pairs={{0,8},{8,0},{16,24},{24,16},{1,9},{9,1},{17,25},{25,17},{2,10},{10... | collective-permute-start | bytes 1769480 | tf_op jit(solution)/shard_map/ppermute | solution.py:34
  229.7 5.8 %collective-permute-start.27 = (bf16[144,384]{1,0:T(8,128)(2,1)S(1)}, bf16[144,384]{1,0:T(8,128)(2,1)S(1)}, u32[]{:S(2)}, u32[]{:S(2)}) collective-permute-start(bf16[144,384]{1,0:T(8,128)(2,1)S(1)} %fusion.5), channel_id=1, source_target_pairs={{0,2},{2,0},{4,6},{6,4},{1,3},{3,1},{5,7},{7,5},{8,10},{10,8},{12,... | collective-permute-start | bytes 331784 | tf_op jit(solution)/shard_map/ppermute | solution.py:34
  229.8 9.1 %collective-permute-start.31 = (bf16[208,384]{1,0:T(8,128)(2,1)S(1)}, bf16[208,384]{1,0:T(8,128)(2,1)S(1)}, u32[]{:S(2)}, u32[]{:S(2)}) collective-permute-start(bf16[208,384]{1,0:T(8,128)(2,1)S(1)} %constant_dynamic-slice_fusion.1), channel_id=1, source_target_pairs={{0,8},{8,0},{16,24},{24,16},{1,9},{9,1},{17,25},{25,17},{2,10},{10... | collective-permute-start | bytes 479240 | tf_op jit(solution)/shard_map/ppermute | solution.py:34
  235.6 7.9 %collective-permute-start.28 = (bf16[144,384]{1,0:T(8,128)(2,1)S(1)}, bf16[144,384]{1,0:T(8,128)(2,1)S(1)}, u32[]{:S(2)}, u32[]{:S(2)}) collective-permute-start(bf16[144,384]{1,0:T(8,128)(2,1)S(1)} %fusion.7), channel_id=1, source_target_pairs={{0,4},{2,6},{4,0},{6,2},{1,5},{3,7},{5,1},{7,3},{8,12},{10,14},{12... | collective-permute-start | bytes 331784 | tf_op jit(solution)/shard_map/ppermute | solution.py:34
  239.0 5.4 %collective-permute-start.32 = (bf16[208,384]{1,0:T(8,128)(2,1)S(1)}, bf16[208,384]{1,0:T(8,128)(2,1)S(1)}, u32[]{:S(2)}, u32[]{:S(2)}) collective-permute-start(bf16[208,384]{1,0:T(8,128)(2,1)S(1)} %fusion.3), channel_id=1, source_target_pairs={{0,16},{8,24},{16,0},{24,8},{1,17},{9,25},{17,1},{25,9},{2,18},{10... | collective-permute-start | bytes 479240 | tf_op jit(solution)/shard_map/ppermute | solution.py:34
  244.4 1.5 collective-permute-start.33
  (13 other events, 42.9 us)

commit v4 on v3

--- a/solution.py
+++ b/solution.py
@@ -818,7 +818,8 @@
     vmem = pl.BlockSpec(memory_space=pltpu.VMEM)
     return pl.pallas_call(
         pairs_kernel,
-        in_specs=[vmem] * 10,
+        grid=(1,),
+        in_specs=[vmem, vmem, head(cosine, 2), head(sine, 2), head(first_in, 2)] + [vmem] * 5,
         out_specs=[vmem] * 2,
         out_shape=[
             jax.ShapeDtypeStruct((2 * HD + 16, width // 2), F32),
@@ -866,13 +867,20 @@
         send_ref[i] = rows[:, span:]
 
 
+def head(array, count):
+    rank = len(array.shape)
+    return pl.BlockSpec((count,) + array.shape[1:], lambda i: (0,) * rank)
+
+
 def own_rows(own, got, cosine, sine, keyval, vectors, x_block, dy, keep, core, back):
     width = keyval.shape[1]
     vmem = pl.BlockSpec(memory_space=pltpu.VMEM)
     half = jax.ShapeDtypeStruct((2, HALF, width // 2), BF16)
     return pl.pallas_call(
         rows_kernel,
-        in_specs=[vmem] * 11,
+        grid=(1,),
+        in_specs=[vmem, vmem, head(cosine, 1), head(sine, 1), vmem, vmem, head(x_block, HALF)]
+        + [head(dy, 1), head(keep, 1), head(core, 1), vmem],
         out_specs=[vmem] * 2,
         out_shape=[half, half],
         name="own_rows",

time: 253 us -> 251 us (level)
  transfers between devices with their start and end apart: 36 -> 36, of which waited for: 19 -> 19; matrix products, arithmetic and copies ran while one was open for 10% -> 10% of each run, Pallas kernels for 33% -> 32%
where the time goes in v4:
time: 251 us; the launch traced here: 250 us
  Pallas kernels  83.1 us (33%)
  waiting for transfers between devices  74.4 us (30%)
  starting transfers between devices  53 us (21%)
  other arithmetic  25.2 us (10%)
  local copies, waits for them, and re-layouts  13 us (5%)
    ppermute x29, waiting for transfers between devices, swap(): return lax.ppermute(value, axis, [(i, i ^ bit) for i in range(count)])  74.4 us
    pallas_call x1, Pallas kernels, attention(): pl.pallas_call(functools.partial(attention_kernel, shape=shape), grid_spe...  46.9 us
    ppermute x29, starting transfers between devices, swap(): return lax.ppermute(value, axis, [(i, i ^ bit) for i in range(count)])  43 us
    pallas_call x1, Pallas kernels, feed_forward(): pl.pallas_call(forward_kernel, grid=(4,), in_specs=[pl.BlockSpec(memory_s...  16.2 us
    ppermute x6, starting transfers between devices, swap_some(): return lax.ppermute(value, ('seq', 'row', 'col'), pairs)  8.5 us
  transfers between devices with their start and end apart: 36, of which 19 were waited for; matrix products, arithmetic and copies ran while one was open for 10% of the time, Pallas kernels for 32%

profile of v4, /device:TPU:0, one launch (start us, length us, event | category | flops | bytes accessed | tf_op | source)
XLA Modules:
  0.0 249.7 jit_solution(42256877984971358)
XLA Ops:
  2.8 1.3 concatenate.32.where_ref.meta_ref
  4.1 2.4 prologue.1
  6.5 3.0 %collective-permute-start = (bf16[400,384]{1,0:T(8,128)(2,1)}, bf16[400,384]{1,0:T(8,128)(2,1)S(1)}, u32[]{:S(2)}, u32[]{:S(2)}) collective-permute-start(bf16[400,384]{1,0:T(8,128)(2,1)} %get-tuple-element.70.pack_ref), channel_id=1, source_target_pairs={{0,1},{1,0},{2,3},{3,2},{4,5},{5,4},{6,7},{7,6},{8,9},{9,8},{10,11... | collective-permute-start | bytes 921608 | tf_op jit(solution)/shard_map/ppermute | solution.py:34
  9.4 2.9 %pack_weights.1 = (bf16[1952,384]{1,0:T(8,128)(2,1)}, bf16[976,384]{1,0:T(8,128)(2,1)}) custom-call(s32[22]{0:T(128)} %concatenate.32.where_ref.meta_ref, bf16[192,384]{1,0:T(8,128)(2,1)} %bitcast.30, bf16[192,384]{1,0:T(8,128)(2,1)} %ow_ref.1, bf16[384,768]{1,0:T(8,128)(2,1)} %up_ref.1, bf16[768,384]{1,0:T(8,128)(2,1)} %down_ref.1, f32[8,384]{1,0:T(8,128)} %reshape.57.vec_ref), custom_call_target="tpu_custom_call" | custom-call | tf_op jit(solution)/shard_map/pack_weights/pallas_call | solution.py:715
  13.0 3.9 %collective-permute-done.got_ref = bf16[400,384]{1,0:T(8,128)(2,1)S(1)} collective-permute-done((bf16[400,384]{1,0:T(8,128)(2,1)}, bf16[400,384]{1,0:T(8,128)(2,1)S(1)}, u32[]{:S(2)}, u32[]{:S(2)}) %collective-permute-start) | collective-permute-done | bytes 307232 | tf_op jit(solution)/shard_map/ppermute | solution.py:34
  16.9 3.6 %collective-permute-start.7 = (bf16[1952,384]{1,0:T(8,128)(2,1)}, bf16[1952,384]{1,0:T(8,128)(2,1)S(1)}, u32[]{:S(2)}, u32[]{:S(2)}) collective-permute-start(bf16[1952,384]{1,0:T(8,128)(2,1)} %get-tuple-element.81.pack_ref), channel_id=1, source_target_pairs={{0,1},{1,0},{2,3},{3,2},{4,5},{5,4},{6,7},{7,6},{16,17},{17,16},{1... | collective-permute-start | bytes 4497416 | tf_op jit(solution)/shard_map/ppermute | solution.py:57
  20.6 4.2 %tables.1 = (f32[5,256,128]{2,1,0:T(8,128)}, f32[5,256,128]{2,1,0:T(8,128)}) custom-call(s32[22]{0:T(128)} %concatenate.32.where_ref.meta_ref), custom_call_target="tpu_custom_call" | custom-call | tf_op jit(solution)/shard_map/tables/pallas_call | solution.py:463
  24.7 3.5 %own_pairs.1 = (bf16[1,512,128]{2,1,0:T(8,128)(2,1)}, bf16[2,256,768]{2,1,0:T(8,128)(2,1)}, bf16[128,768]{1,0:T(8,128)(2,1)}, f32[8,768]{1,0:T(8,128)}) custom-call(bf16[512,768]{1,0:T(8,128)(2,1)} %get-tuple-element.68.x_ref, bf16[256,384]{1,0:T(8,128)(2,1)} %get-tuple-element.69.mine_ref, bf16[400,384]{1,0:T(8,128)(2,1)} %get-tuple-element.70.pack_ref, ...), custom_call_target="tpu_custom_call" | custom-call | tf_op jit(solution)/shard_map/own_pairs/pallas_call | solution.py:762
  28.3 1.6 collective-permute-start.1
  29.9 6.4 %collective-permute-done.1 = bf16[1,512,128]{2,1,0:T(8,128)(2,1)S(1)} collective-permute-done((bf16[1,512,128]{2,1,0:T(8,128)(2,1)}, bf16[1,512,128]{2,1,0:T(8,128)(2,1)S(1)}, u32[]{:S(2)}, u32[]{:S(2)}) %collective-permute-start.1) | collective-permute-done | bytes 131104 | tf_op jit(solution)/shard_map/ppermute | solution.py:34
  38.7 1.7 collective-permute-start.3
  40.4 2.4 collective-permute-start.2
  42.8 11.0 %collective-permute-done.3 = bf16[2,512,128]{2,1,0:T(8,128)(2,1)S(1)} collective-permute-done((bf16[2,512,128]{2,1,0:T(8,128)(2,1)S(1)}, bf16[2,512,128]{2,1,0:T(8,128)(2,1)S(1)}, u32[]{:S(2)}, u32[]{:S(2)}) %collective-permute-start.3) | collective-permute-done | bytes 262176 | tf_op jit(solution)/shard_map/ppermute | solution.py:34
  56.5 1.6 collective-permute-start.8
  58.1 5.9 %collective-permute-done.2.both1_ref = bf16[2,256,768]{2,1,0:T(8,128)(2,1)S(1)} collective-permute-done((bf16[2,256,768]{2,1,0:T(8,128)(2,1)}, bf16[2,256,768]{2,1,0:T(8,128)(2,1)S(1)}, u32[]{:S(2)}, u32[]{:S(2)}) %collective-permute-start.2) | collective-permute-done | bytes 786464 | tf_op jit(solution)/shard_map/ppermute | solution.py:34
  63.9 6.4 %collective-permute-done.8 = bf16[4,512,128]{2,1,0:T(8,128)(2,1)S(1)} collective-permute-done((bf16[4,512,128]{2,1,0:T(8,128)(2,1)S(1)}, bf16[4,512,128]{2,1,0:T(8,128)(2,1)S(1)}, u32[]{:S(2)}, u32[]{:S(2)}) %collective-permute-start.8) | collective-permute-done | bytes 524320 | tf_op jit(solution)/shard_map/ppermute | solution.py:34
  72.0 1.1 collective-permute-done.10.both2_ref
  73.1 1.1 collective-permute-done.11.both3_ref
  75.2 16.2 %feed_forward.1 = (bf16[4,256,768]{2,1,0:T(8,128)(2,1)}, bf16[4,256,768]{2,1,0:T(8,128)(2,1)}, f32[4,256,768]{2,1,0:T(8,128)}, f32[4,256,768]{2,1,0:T(8,128)}, b...) custom-call(s32[22]{0:T(128)} %concatenate.32.where_ref.meta_ref, ...), custom_call_target="tpu_custom_call" | custom-call | flops 7000000000 | bytes 20000000 | tf_op jit(solution)/shard_map/feed_forward/pallas_call | solution.py:623
  91.4 2.1 collective-permute-start.13
  94.5 46.9 %attention.1 = (f32[2,2,256,768]{3,2,1,0:T(8,128)}, bf16[2,2,256,768]{3,2,1,0:T(8,128)(2,1)}, bf16[416,384]{1,0:T(8,128)(2,1)}, bf16[416,384]{1,0:T(8,128)(2,1)}...) custom-call(s32[22]{0:T(128)} %concatenate.32.where_ref.meta_ref, ...), custom_call_target="tpu_custom_call" | custom-call | flops 24000000000 | bytes 30000000 | tf_op jit(solution)/shard_map/attention/pallas_call | solution.py:403
  141.4 6.4 %collective-permute-start.14 = (bf16[8,512,128]{2,1,0:T(8,128)(2,1)}, bf16[8,512,128]{2,1,0:T(8,128)(2,1)S(1)}, u32[]{:S(2)}, u32[]{:S(2)}) collective-permute-start(bf16[8,512,128]{2,1,0:T(8,128)(2,1)} %get-tuple-element.99), channel_id=1, source_target_pairs={{0,8},{8,0},{16,24},{24,16},{1,9},{9,1},{17,25},{25,17},{2,10},{10... | collective-permute-start | bytes 3145736 | tf_op jit(solution)/shard_map/ppermute | solution.py:34
  147.9 2.5 %collective-permute-done.14 = bf16[8,512,128]{2,1,0:T(8,128)(2,1)S(1)} collective-permute-done((bf16[8,512,128]{2,1,0:T(8,128)(2,1)}, bf16[8,512,128]{2,1,0:T(8,128)(2,1)S(1)}, u32[]{:S(2)}, u32[]{:S(2)}) %collective-permute-start.14) | collective-permute-done | bytes 1048608 | tf_op jit(solution)/shard_map/ppermute | solution.py:34
  150.4 2.5 %add_convert_fusion.3 = bf16[8,256,128]{2,1,0:T(8,128)(2,1)} fusion(f32[8,512,128]{2,1,0:T(8,128)} %get-tuple-element.97, bf16[8,512,128]{2,1,0:T(8,128)(2,1)S(1)} %collective-permute-done.14), kind=kLoop, calls=%fused_computation.8 | loop fusion | flops 786432 | bytes 2097152 | tf_op jit(solution)/shard_map/convert_element_type | solution.py:1002
  153.3 1.9 broadcast_select_fusion
  155.5 2.8 %collective-permute-done.20 = bf16[2,768,384]{2,1,0:T(8,128)(2,1)} collective-permute-done((bf16[2,768,384]{2,1,0:T(8,128)(2,1)S(1)}, bf16[2,768,384]{2,1,0:T(8,128)(2,1)}, u32[]{:S(2)}, u32[]{:S(2)}) %collective-permute-start.20) | collective-permute-done | bytes 1179680 | tf_op jit(solution)/shard_map/ppermute | solution.py:34
  158.4 2.0 fusion.1
  160.4 2.8 %fusion = bf16[2,256,768]{2,1,0:T(8,128)(2,1)} fusion(f32[2,2,256,768]{3,2,1,0:T(8,128)} %get-tuple-element.100.keep_ref, bf16[2,2,256,768]{3,2,1,0:T(8,128)(2,1)} %collective-permute-done.16.core_ref), kind=kLoop, calls=%fused_computation.9 | loop fusion | flops 1179648 | bytes 3145728 | tf_op jit(solution)/shard_map/convert_element_type | solution.py:1005
  163.2 6.7 %collective-permute-done.15 = bf16[8,256,128]{2,1,0:T(8,128)(2,1)S(1)} collective-permute-done((bf16[8,256,128]{2,1,0:T(8,128)(2,1)}, bf16[8,256,128]{2,1,0:T(8,128)(2,1)S(1)}, u32[]{:S(2)}, u32[]{:S(2)}) %collective-permute-start.15) | collective-permute-done | bytes 524320 | tf_op jit(solution)/shard_map/ppermute | solution.py:34
  171.1 1.7 collective-permute-start.17
  174.5 4.8 %collective-permute-done.17 = bf16[4,256,128]{2,1,0:T(8,128)(2,1)} collective-permute-done((bf16[4,256,128]{2,1,0:T(8,128)(2,1)}, bf16[4,256,128]{2,1,0:T(8,128)(2,1)}, u32[]{:S(2)}, u32[]{:S(2)}) %collective-permute-start.17) | collective-permute-done | bytes 262176 | tf_op jit(solution)/shard_map/ppermute | solution.py:34
  180.3 4.9 %collective-permute-done.21 = bf16[768,384]{1,0:T(8,128)(2,1)} collective-permute-done((bf16[768,384]{1,0:T(8,128)(2,1)}, bf16[768,384]{1,0:T(8,128)(2,1)}, u32[]{:S(2)}, u32[]{:S(2)}) %collective-permute-start.21) | collective-permute-done | bytes 589856 | tf_op jit(solution)/shard_map/ppermute | solution.py:34
  185.7 13.5 %collective-permute-start.19 = (bf16[2,256,128]{2,1,0:T(8,128)(2,1)S(1)}, bf16[2,256,128]{2,1,0:T(8,128)(2,1)S(1)}, u32[]{:S(2)}, u32[]{:S(2)}) collective-permute-start(bf16[2,256,128]{2,1,0:T(8,128)(2,1)S(1)} %slice.193), channel_id=1, source_target_pairs={{0,4},{2,6},{4,0},{6,2},{1,5},{3,7},{5,1},{7,3},{8,12},{10,14},{12... | collective-permute-start | bytes 393224 | tf_op jit(solution)/shard_map/ppermute | solution.py:34
  199.2 2.3 reduce-precision_convert_fusion
  202.2 2.2 collective-permute-done.19.got_ref
  205.1 2.9 %pair_sums.1 = (f32[144,384]{1,0:T(8,128)}, bf16[144,384]{1,0:T(8,128)(2,1)}) custom-call(f32[2,256,128]{2,1,0:T(8,128)} %slice.130.keep_ref, bf16[2,256,128]{2,1,0:T(8,128)(2,1)} %copy-done.7, f32[5,256,128]{2,1,0:T(8,128)} %get-tuple-element.74.cos_ref, f32[5,256,128]{2,1,0:T(8,128)} %get-tuple-element.75.sin_ref, ...), custom_call_target="tpu_custom_call" | custom-call | tf_op jit(solution)/shard_map/pair_sums/pallas_call | solution.py:819
  208.0 1.2 collective-permute-start.24
  209.9 3.0 %collective-permute-done.24 = bf16[144,384]{1,0:T(8,128)(2,1)S(1)} collective-permute-done((bf16[144,384]{1,0:T(8,128)(2,1)}, bf16[144,384]{1,0:T(8,128)(2,1)S(1)}, u32[]{:S(2)}, u32[]{:S(2)}) %collective-permute-start.24) | collective-permute-done | bytes 110624 | tf_op jit(solution)/shard_map/ppermute | solution.py:34
  215.0 1.4 collective-permute-start.30
  217.1 4.1 %own_rows.1 = (bf16[2,256,384]{2,1,0:T(8,128)(2,1)}, bf16[2,256,384]{2,1,0:T(8,128)(2,1)}) custom-call(f32[1,256,128]{2,1,0:T(8,128)} %get-tuple-element.135.own_ref, bf16[256,128]{1,0:T(8,128)(2,1)} %copy-done.12, f32[5,256,128]{2,1,0:T(8,128)} %get-tuple-element.74.cos_ref, f32[5,256,128]{2,1,0:T(8,128)} %get-tuple-element.75.sin_ref, ...), custom_call_target="tpu_custom_call" | custom-call | tf_op jit(solution)/shard_map/own_rows/pallas_call | solution.py:879
  221.2 1.2 collective-permute-start.23
  222.8 1.7 collective-permute-start.35
  224.5 3.3 %collective-permute-done.26 = bf16[144,384]{1,0:T(8,128)(2,1)S(1)} collective-permute-done((bf16[144,384]{1,0:T(8,128)(2,1)S(1)}, bf16[144,384]{1,0:T(8,128)(2,1)S(1)}, u32[]{:S(2)}, u32[]{:S(2)}) %collective-permute-start.26) | collective-permute-done | bytes 110624 | tf_op jit(solution)/shard_map/ppermute | solution.py:34
  227.9 2.0 collective-permute-start.31
  230.0 3.8 %collective-permute-done.27 = bf16[144,384]{1,0:T(8,128)(2,1)S(1)} collective-permute-done((bf16[144,384]{1,0:T(8,128)(2,1)S(1)}, bf16[144,384]{1,0:T(8,128)(2,1)S(1)}, u32[]{:S(2)}, u32[]{:S(2)}) %collective-permute-start.27) | collective-permute-done | bytes 110624 | tf_op jit(solution)/shard_map/ppermute | solution.py:34
  233.8 1.4 collective-permute-start.28
  237.3 4.2 %collective-permute-done.28 = bf16[144,384]{1,0:T(8,128)(2,1)S(1)} collective-permute-done((bf16[144,384]{1,0:T(8,128)(2,1)S(1)}, bf16[144,384]{1,0:T(8,128)(2,1)S(1)}, u32[]{:S(2)}, u32[]{:S(2)}) %collective-permute-start.28) | collective-permute-done | bytes 110624 | tf_op jit(solution)/shard_map/ppermute | solution.py:34
  248.0 1.1 pad_maximum_fusion
  (137 shorter events, 30.9 us)
Async XLA Ops:
  6.5 10.4 %collective-permute-start = (bf16[400,384]{1,0:T(8,128)(2,1)}, bf16[400,384]{1,0:T(8,128)(2,1)S(1)}, u32[]{:S(2)}, u32[]{:S(2)}) collective-permute-start(bf16[400,384]{1,0:T(8,128)(2,1)} %get-tuple-element.70.pack_ref), channel_id=1, source_target_pairs={{0,1},{1,0},{2,3},{3,2},{4,5},{5,4},{6,7},{7,6},{8,9},{9,8},{10,11... | collective-permute-start | bytes 921608 | tf_op jit(solution)/shard_map/ppermute | solution.py:34
  12.3 24.0 %collective-permute-start.4 = (bf16[976,384]{1,0:T(8,128)(2,1)}, bf16[976,384]{1,0:T(8,128)(2,1)S(1)}, u32[]{:S(2)}, u32[]{:S(2)}) collective-permute-start(bf16[976,384]{1,0:T(8,128)(2,1)} %get-tuple-element.79), channel_id=1, source_target_pairs={{8,12},{9,13},{10,14},{11,15},{12,8},{13,9},{14,10},{15,11},{24,28... | collective-permute-start | bytes 2248712 | tf_op jit(solution)/shard_map/ppermute | solution.py:57
  16.9 7.8 %copy-start.11 = (bf16[400,384]{1,0:T(8,128)(2,1)}, bf16[400,384]{1,0:T(8,128)(2,1)S(1)}, u32[]{:S(2)}) copy-start(bf16[400,384]{1,0:T(8,128)(2,1)S(1)} %collective-permute-done.got_ref) | copy-start | bytes 921604
  16.9 38.5 %collective-permute-start.7 = (bf16[1952,384]{1,0:T(8,128)(2,1)}, bf16[1952,384]{1,0:T(8,128)(2,1)S(1)}, u32[]{:S(2)}, u32[]{:S(2)}) collective-permute-start(bf16[1952,384]{1,0:T(8,128)(2,1)} %get-tuple-element.81.pack_ref), channel_id=1, source_target_pairs={{0,1},{1,0},{2,3},{3,2},{4,5},{5,4},{6,7},{7,6},{16,17},{17,16},{1... | collective-permute-start | bytes 4497416 | tf_op jit(solution)/shard_map/ppermute | solution.py:57
  28.3 42.0 %copy-start.17 = (bf16[2,256,768]{2,1,0:T(8,128)(2,1)S(1)}, bf16[2,256,768]{2,1,0:T(8,128)(2,1)}, u32[]{:S(2)}) copy-start(bf16[2,256,768]{2,1,0:T(8,128)(2,1)} %get-tuple-element.85.both0_ref) | copy-start | bytes 2359300
  28.3 43.0 %copy-start.3 = (bf16[1,512,128]{2,1,0:T(8,128)(2,1)S(1)}, bf16[1,512,128]{2,1,0:T(8,128)(2,1)}, u32[]{:S(2)}) copy-start(bf16[1,512,128]{2,1,0:T(8,128)(2,1)} %get-tuple-element.77) | copy-start | bytes 393220
  28.3 8.0 %collective-permute-start.1 = (bf16[1,512,128]{2,1,0:T(8,128)(2,1)}, bf16[1,512,128]{2,1,0:T(8,128)(2,1)S(1)}, u32[]{:S(2)}, u32[]{:S(2)}) collective-permute-start(bf16[1,512,128]{2,1,0:T(8,128)(2,1)} %get-tuple-element.77), channel_id=1, source_target_pairs={{0,2},{2,0},{4,6},{6,4},{1,3},{3,1},{5,7},{7,5},{8,10},{10,8},{12,... | collective-permute-start | bytes 393224 | tf_op jit(solution)/shard_map/ppermute | solution.py:34
  36.3 35.1 %copy-start.21 = (bf16[976,384]{1,0:T(8,128)(2,1)}, bf16[976,384]{1,0:T(8,128)(2,1)S(1)}, u32[]{:S(2)}) copy-start(bf16[976,384]{1,0:T(8,128)(2,1)S(1)} %collective-permute-done.4.z_ref) | copy-start | bytes 2248708
  36.3 17.4 %collective-permute-start.5 = (bf16[976,384]{1,0:T(8,128)(2,1)S(1)}, bf16[976,384]{1,0:T(8,128)(2,1)S(1)}, u32[]{:S(2)}, u32[]{:S(2)}) collective-permute-start(bf16[976,384]{1,0:T(8,128)(2,1)S(1)} %collective-permute-done.4.z_ref), channel_id=1, source_target_pairs={{8,24},{9,25},{10,26},{11,27},{12,28},{13,29},{14,30},{15,31},{24,... | collective-permute-start | bytes 2248712 | tf_op jit(solution)/shard_map/ppermute | solution.py:57
  37.0 17.4 %collective-permute-start.6 = (bf16[976,384]{1,0:T(8,128)(2,1)S(1)}, bf16[976,384]{1,0:T(8,128)(2,1)S(1)}, u32[]{:S(2)}, u32[]{:S(2)}) collective-permute-start(bf16[976,384]{1,0:T(8,128)(2,1)S(1)} %collective-permute-done.4.z_ref), channel_id=1, source_target_pairs={{8,9},{9,8},{10,11},{11,10},{12,13},{13,12},{14,15},{15,14},{24,25... | collective-permute-start | bytes 2248712 | tf_op jit(solution)/shard_map/ppermute | solution.py:57
  38.7 15.1 %collective-permute-start.3 = (bf16[2,512,128]{2,1,0:T(8,128)(2,1)S(1)}, bf16[2,512,128]{2,1,0:T(8,128)(2,1)S(1)}, u32[]{:S(2)}, u32[]{:S(2)}) collective-permute-start(bf16[2,512,128]{2,1,0:T(8,128)(2,1)S(1)} %pad_maximum_fusion.5), channel_id=1, source_target_pairs={{0,4},{2,6},{4,0},{6,2},{1,5},{3,7},{5,1},{7,3},{8,12},{10,14},{12... | collective-permute-start | bytes 786440 | tf_op jit(solution)/shard_map/ppermute | solution.py:34
  40.4 23.5 %collective-permute-start.2 = (bf16[2,256,768]{2,1,0:T(8,128)(2,1)}, bf16[2,256,768]{2,1,0:T(8,128)(2,1)S(1)}, u32[]{:S(2)}, u32[]{:S(2)}) collective-permute-start(bf16[2,256,768]{2,1,0:T(8,128)(2,1)} %get-tuple-element.85.both0_ref), channel_id=1, source_target_pairs={{0,2},{2,0},{4,6},{6,4},{1,3},{3,1},{5,7},{7,5},{8,10},{10,8},{12,... | collective-permute-start | bytes 2359304 | tf_op jit(solution)/shard_map/ppermute | solution.py:34
  53.8 16.5 %copy-start.22 = (bf16[976,384]{1,0:T(8,128)(2,1)}, bf16[976,384]{1,0:T(8,128)(2,1)S(1)}, u32[]{:S(2)}) copy-start(bf16[976,384]{1,0:T(8,128)(2,1)S(1)} %collective-permute-done.5.x_got_ref) | copy-start | bytes 2248708
  53.8 10.2 %collective-permute-start.9 = (bf16[976,384]{1,0:T(8,128)(2,1)S(1)}, bf16[976,384]{1,0:T(8,128)(2,1)S(1)}, u32[]{:S(2)}, u32[]{:S(2)}) collective-permute-start(bf16[976,384]{1,0:T(8,128)(2,1)S(1)} %collective-permute-done.5.x_got_ref), channel_id=1, source_target_pairs={{8,9},{9,8},{10,11},{11,10},{12,13},{13,12},{14,15},{15,14},{24,25... | collective-permute-start | bytes 2248712 | tf_op jit(solution)/shard_map/ppermute | solution.py:57
  55.4 16.1 %copy-start.15 = (bf16[1952,384]{1,0:T(8,128)(2,1)}, bf16[1952,384]{1,0:T(8,128)(2,1)S(1)}, u32[]{:S(2)}) copy-start(bf16[1952,384]{1,0:T(8,128)(2,1)S(1)} %collective-permute-done.7.even_ref) | copy-start | bytes 4497412
  56.5 13.8 %collective-permute-start.8 = (bf16[4,512,128]{2,1,0:T(8,128)(2,1)S(1)}, bf16[4,512,128]{2,1,0:T(8,128)(2,1)S(1)}, u32[]{:S(2)}, u32[]{:S(2)}) collective-permute-start(bf16[4,512,128]{2,1,0:T(8,128)(2,1)S(1)} %pad_maximum_fusion.2), channel_id=1, source_target_pairs={{0,16},{8,24},{16,0},{24,8},{1,17},{9,25},{17,1},{25,9},{2,18},{10... | collective-permute-start | bytes 1572872 | tf_op jit(solution)/shard_map/ppermute | solution.py:34
  63.9 9.2 %copy-start.18 = (bf16[2,256,768]{2,1,0:T(8,128)(2,1)}, bf16[2,256,768]{2,1,0:T(8,128)(2,1)S(1)}, u32[]{:S(2)}) copy-start(bf16[2,256,768]{2,1,0:T(8,128)(2,1)S(1)} %collective-permute-done.2.both1_ref) | copy-start | bytes 2359300
  70.3 2.8 %collective-permute-start.10 = (bf16[2,256,768]{2,1,0:T(8,128)(2,1)S(1)}, bf16[2,256,768]{2,1,0:T(8,128)(2,1)S(1)}, u32[]{:S(2)}, u32[]{:S(2)}) collective-permute-start(bf16[2,256,768]{2,1,0:T(8,128)(2,1)S(1)} %copy-done.17), channel_id=1, source_target_pairs={{0,8},{8,0},{16,24},{24,16},{1,9},{9,1},{17,25},{25,17},{2,10},{10... | collective-permute-start | bytes 2359304 | tf_op jit(solution)/shard_map/ppermute | solution.py:34
  71.2 3.0 %collective-permute-start.11 = (bf16[2,256,768]{2,1,0:T(8,128)(2,1)S(1)}, bf16[2,256,768]{2,1,0:T(8,128)(2,1)S(1)}, u32[]{:S(2)}, u32[]{:S(2)}) collective-permute-start(bf16[2,256,768]{2,1,0:T(8,128)(2,1)S(1)} %collective-permute-done.2.both1_ref), channel_id=1, source_target_pairs={{0,8},{8,0},{16,24},{24,16},{1,9},{9,1},{17,25},{25,17},{2,10},{10... | collective-permute-start | bytes 2359304 | tf_op jit(solution)/shard_map/ppermute | solution.py:34
  71.5 19.9 %copy-start.13 = (bf16[8,512,128]{2,1,0:T(8,128)(2,1)}, bf16[8,512,128]{2,1,0:T(8,128)(2,1)S(1)}, u32[]{:S(2)}) copy-start(bf16[8,512,128]{2,1,0:T(8,128)(2,1)S(1)} %constant_dynamic-update-slice_fusion.kv0_ref) | copy-start | bytes 3145732
  71.5 22.0 %collective-permute-start.12 = (bf16[8,512,128]{2,1,0:T(8,128)(2,1)S(1)}, bf16[8,512,128]{2,1,0:T(8,128)(2,1)S(1)}, u32[]{:S(2)}, u32[]{:S(2)}) collective-permute-start(bf16[8,512,128]{2,1,0:T(8,128)(2,1)S(1)} %constant_dynamic-update-slice_fusion.kv0_ref), channel_id=1, source_target_pairs={{0,8},{8,0},{16,24},{24,16},{1,9},{9,1},{17,25},{25,17},{2,10},{10... | collective-permute-start | bytes 3145736 | tf_op jit(solution)/shard_map/ppermute | solution.py:34
  91.4 50.0 %collective-permute-start.13 = (bf16[2,1536,384]{2,1,0:T(8,128)(2,1)}, bf16[2,1536,384]{2,1,0:T(8,128)(2,1)}, u32[]{:S(2)}, u32[]{:S(2)}) collective-permute-start(bf16[2,1536,384]{2,1,0:T(8,128)(2,1)} %get-tuple-element.105), channel_id=1, source_target_pairs={{8,12},{9,13},{10,14},{11,15},{12,8},{13,9},{14,10},{15,11},{24,28... | collective-permute-start | bytes 7077896 | tf_op jit(solution)/shard_map/ppermute | solution.py:57
  141.4 8.9 %collective-permute-start.14 = (bf16[8,512,128]{2,1,0:T(8,128)(2,1)}, bf16[8,512,128]{2,1,0:T(8,128)(2,1)S(1)}, u32[]{:S(2)}, u32[]{:S(2)}) collective-permute-start(bf16[8,512,128]{2,1,0:T(8,128)(2,1)} %get-tuple-element.99), channel_id=1, source_target_pairs={{0,8},{8,0},{16,24},{24,16},{1,9},{9,1},{17,25},{25,17},{2,10},{10... | collective-permute-start | bytes 3145736 | tf_op jit(solution)/shard_map/ppermute | solution.py:34
  152.9 7.5 %collective-permute-start.16 = (bf16[2,2,256,768]{3,2,1,0:T(8,128)(2,1)}, bf16[2,2,256,768]{3,2,1,0:T(8,128)(2,1)}, u32[]{:S(2)}, u32[]{:S(2)}) collective-permute-start(bf16[2,2,256,768]{3,2,1,0:T(8,128)(2,1)} %get-tuple-element.102), channel_id=1, source_target_pairs={{0,8},{8,0},{16,24},{24,16},{1,9},{9,1},{17,25},{25,17},{2,10},{10... | collective-permute-start | bytes 4718600 | tf_op jit(solution)/shard_map/ppermute | solution.py:34
  155.3 3.0 %collective-permute-start.20 = (bf16[2,768,384]{2,1,0:T(8,128)(2,1)S(1)}, bf16[2,768,384]{2,1,0:T(8,128)(2,1)}, u32[]{:S(2)}, u32[]{:S(2)}) collective-permute-start(bf16[2,768,384]{2,1,0:T(8,128)(2,1)S(1)} %constant_dynamic-slice_fusion.2), channel_id=1, source_target_pairs={{0,8},{8,0},{16,24},{24,16},{1,9},{9,1},{17,25},{25,17},{2,10},{10... | collective-permute-start | bytes 3538952 | tf_op jit(solution)/shard_map/ppermute | solution.py:34
  155.5 14.4 %collective-permute-start.15 = (bf16[8,256,128]{2,1,0:T(8,128)(2,1)}, bf16[8,256,128]{2,1,0:T(8,128)(2,1)S(1)}, u32[]{:S(2)}, u32[]{:S(2)}) collective-permute-start(bf16[8,256,128]{2,1,0:T(8,128)(2,1)} %add_convert_fusion.3), channel_id=1, source_target_pairs={{0,1},{1,0},{2,3},{3,2},{4,5},{5,4},{6,7},{7,6},{8,9},{9,8},{10,11... | collective-permute-start | bytes 1572872 | tf_op jit(solution)/shard_map/ppermute | solution.py:34
  160.4 9.8 %copy-start.2 = (f32[8,512,128]{2,1,0:T(8,128)S(1)}, f32[8,512,128]{2,1,0:T(8,128)}, u32[]{:S(2)}) copy-start(f32[8,512,128]{2,1,0:T(8,128)} %get-tuple-element.97) | copy-start | bytes 6291460
  160.4 9.8 %copy-start.5 = (bf16[8,512,128]{2,1,0:T(8,128)(2,1)S(1)}, bf16[8,512,128]{2,1,0:T(8,128)(2,1)}, u32[]{:S(2)}) copy-start(bf16[8,512,128]{2,1,0:T(8,128)(2,1)} %copy-done.4) | copy-start | bytes 3145732
  163.2 22.5 %collective-permute-start.18 = (bf16[2,256,768]{2,1,0:T(8,128)(2,1)}, bf16[2,256,768]{2,1,0:T(8,128)(2,1)}, u32[]{:S(2)}, u32[]{:S(2)}) collective-permute-start(bf16[2,256,768]{2,1,0:T(8,128)(2,1)} %fusion), channel_id=1, source_target_pairs={{0,2},{2,0},{4,6},{6,4},{1,3},{3,1},{5,7},{7,5},{8,10},{10,8},{12,... | collective-permute-start | bytes 2359304 | tf_op jit(solution)/shard_map/ppermute | solution.py:34
  170.0 15.2 %collective-permute-start.21 = (bf16[768,384]{1,0:T(8,128)(2,1)}, bf16[768,384]{1,0:T(8,128)(2,1)}, u32[]{:S(2)}, u32[]{:S(2)}) collective-permute-start(bf16[768,384]{1,0:T(8,128)(2,1)} %fusion.1), channel_id=1, source_target_pairs={{0,1},{1,0},{2,3},{3,2},{4,5},{5,4},{6,7},{7,6},{8,9},{9,8},{10,11... | collective-permute-start | bytes 1769480 | tf_op jit(solution)/shard_map/ppermute | solution.py:34
  171.1 8.1 %collective-permute-start.17 = (bf16[4,256,128]{2,1,0:T(8,128)(2,1)}, bf16[4,256,128]{2,1,0:T(8,128)(2,1)}, u32[]{:S(2)}, u32[]{:S(2)}) collective-permute-start(bf16[4,256,128]{2,1,0:T(8,128)(2,1)} %slice.192), channel_id=1, source_target_pairs={{0,16},{8,24},{16,0},{24,8},{1,17},{9,25},{17,1},{25,9},{2,18},{10... | collective-permute-start | bytes 786440 | tf_op jit(solution)/shard_map/ppermute | solution.py:34
  180.3 21.2 %copy-start = (f32[4,256,128]{2,1,0:T(8,128)}, f32[4,256,128]{2,1,0:T(8,128)S(1)}, u32[]{:S(2)}) copy-start(f32[4,256,128]{2,1,0:T(8,128)S(1)} %slice_add_fusion) | copy-start | bytes 1572868
  185.2 28.8 %collective-permute-start.29 = (bf16[416,384]{1,0:T(8,128)(2,1)}, bf16[416,384]{1,0:T(8,128)(2,1)}, u32[]{:S(2)}, u32[]{:S(2)}) collective-permute-start(bf16[416,384]{1,0:T(8,128)(2,1)} %get-tuple-element.117), channel_id=1, source_target_pairs={{0,1},{1,0},{2,3},{3,2},{4,5},{5,4},{6,7},{7,6},{8,9},{9,8},{10,11... | collective-permute-start | bytes 958472 | tf_op jit(solution)/shard_map/ppermute | solution.py:34
  185.7 18.7 %collective-permute-start.19 = (bf16[2,256,128]{2,1,0:T(8,128)(2,1)S(1)}, bf16[2,256,128]{2,1,0:T(8,128)(2,1)S(1)}, u32[]{:S(2)}, u32[]{:S(2)}) collective-permute-start(bf16[2,256,128]{2,1,0:T(8,128)(2,1)S(1)} %slice.193), channel_id=1, source_target_pairs={{0,4},{2,6},{4,0},{6,2},{1,5},{3,7},{5,1},{7,3},{8,12},{10,14},{12... | collective-permute-start | bytes 393224 | tf_op jit(solution)/shard_map/ppermute | solution.py:34
  201.5 21.1 %collective-permute-start.34 = (bf16[768,384]{1,0:T(8,128)(2,1)}, bf16[768,384]{1,0:T(8,128)(2,1)S(1)}, u32[]{:S(2)}, u32[]{:S(2)}) collective-permute-start(bf16[768,384]{1,0:T(8,128)(2,1)} %get-tuple-element.124), channel_id=1, source_target_pairs={{0,16},{8,24},{16,0},{24,8},{1,17},{9,25},{17,1},{25,9},{2,18},{10... | collective-permute-start | bytes 1769480 | tf_op jit(solution)/shard_map/ppermute | solution.py:34
  208.0 5.0 %collective-permute-start.24 = (bf16[144,384]{1,0:T(8,128)(2,1)}, bf16[144,384]{1,0:T(8,128)(2,1)S(1)}, u32[]{:S(2)}, u32[]{:S(2)}) collective-permute-start(bf16[144,384]{1,0:T(8,128)(2,1)} %get-tuple-element.114), channel_id=1, source_target_pairs={{0,1},{1,0},{2,3},{3,2},{4,5},{5,4},{6,7},{7,6},{8,9},{9,8},{10,11... | collective-permute-start | bytes 331784 | tf_op jit(solution)/shard_map/ppermute | solution.py:34
  209.9 6.6 %collective-permute-start.22 = (bf16[256,128]{1,0:T(8,128)(2,1)S(1)}, bf16[256,128]{1,0:T(8,128)(2,1)S(1)}, u32[]{:S(2)}, u32[]{:S(2)}) collective-permute-start(bf16[256,128]{1,0:T(8,128)(2,1)S(1)} %get-tuple-element.134), channel_id=1, source_target_pairs={{0,2},{2,0},{4,6},{6,4},{1,3},{3,1},{5,7},{7,5},{8,10},{10,8},{12,... | collective-permute-start | bytes 196616 | tf_op jit(solution)/shard_map/ppermute | solution.py:34
  213.9 8.5 %collective-permute-start.25 = (bf16[144,384]{1,0:T(8,128)(2,1)S(1)}, bf16[144,384]{1,0:T(8,128)(2,1)S(1)}, u32[]{:S(2)}, u32[]{:S(2)}) collective-permute-start(bf16[144,384]{1,0:T(8,128)(2,1)S(1)} %fusion.4), channel_id=1, source_target_pairs={{0,8},{8,0},{16,24},{24,16},{1,9},{9,1},{17,25},{25,17},{2,10},{10... | collective-permute-start | bytes 331784 | tf_op jit(solution)/shard_map/ppermute | solution.py:34
  215.0 9.4 %collective-permute-start.30 = (bf16[416,384]{1,0:T(8,128)(2,1)S(1)}, bf16[416,384]{1,0:T(8,128)(2,1)}, u32[]{:S(2)}, u32[]{:S(2)}) collective-permute-start(bf16[416,384]{1,0:T(8,128)(2,1)S(1)} %add_convert_fusion.4), channel_id=1, source_target_pairs={{8,12},{10,14},{12,8},{14,10},{24,28},{26,30},{28,24},{30,26},{9,1... | collective-permute-start | bytes 958472 | tf_op jit(solution)/shard_map/ppermute | solution.py:43
  221.2 14.1 %collective-permute-start.23 = (bf16[2,256,384]{2,1,0:T(8,128)(2,1)}, bf16[2,256,384]{2,1,0:T(8,128)(2,1)S(1)}, u32[]{:S(2)}, u32[]{:S(2)}) collective-permute-start(bf16[2,256,384]{2,1,0:T(8,128)(2,1)} %get-tuple-element.110), channel_id=1, source_target_pairs={{0,1},{1,0},{2,3},{3,2},{4,5},{5,4},{6,7},{7,6},{8,9},{9,8},{10,11... | collective-permute-start | bytes 1179656 | tf_op jit(solution)/shard_map/ppermute | solution.py:34
  222.5 5.3 %collective-permute-start.26 = (bf16[144,384]{1,0:T(8,128)(2,1)S(1)}, bf16[144,384]{1,0:T(8,128)(2,1)S(1)}, u32[]{:S(2)}, u32[]{:S(2)}) collective-permute-start(bf16[144,384]{1,0:T(8,128)(2,1)S(1)} %get-tuple-element.126), channel_id=1, source_target_pairs={{0,16},{8,24},{16,0},{24,8},{1,17},{9,25},{17,1},{25,9},{2,18},{10... | collective-permute-start | bytes 331784 | tf_op jit(solution)/shard_map/ppermute | solution.py:34
  222.7 12.5 %copy-start.9 = (bf16[2,256,384]{2,1,0:T(8,128)(2,1)S(1)}, bf16[2,256,384]{2,1,0:T(8,128)(2,1)}, u32[]{:S(2)}) copy-start(bf16[2,256,384]{2,1,0:T(8,128)(2,1)} %get-tuple-element.109) | copy-start | bytes 1179652
  222.8 24.0 %collective-permute-start.35 = (bf16[768,384]{1,0:T(8,128)(2,1)S(1)}, bf16[768,384]{1,0:T(8,128)(2,1)S(1)}, u32[]{:S(2)}, u32[]{:S(2)}) collective-permute-start(bf16[768,384]{1,0:T(8,128)(2,1)S(1)} %add_convert_fusion.1), channel_id=1, source_target_pairs={{0,8},{8,0},{16,24},{24,16},{1,9},{9,1},{17,25},{25,17},{2,10},{10... | collective-permute-start | bytes 1769480 | tf_op jit(solution)/shard_map/ppermute | solution.py:34
  227.8 6.0 %collective-permute-start.27 = (bf16[144,384]{1,0:T(8,128)(2,1)S(1)}, bf16[144,384]{1,0:T(8,128)(2,1)S(1)}, u32[]{:S(2)}, u32[]{:S(2)}) collective-permute-start(bf16[144,384]{1,0:T(8,128)(2,1)S(1)} %fusion.5), channel_id=1, source_target_pairs={{0,2},{2,0},{4,6},{6,4},{1,3},{3,1},{5,7},{7,5},{8,10},{10,8},{12,... | collective-permute-start | bytes 331784 | tf_op jit(solution)/shard_map/ppermute | solution.py:34
  227.9 9.1 %collective-permute-start.31 = (bf16[208,384]{1,0:T(8,128)(2,1)S(1)}, bf16[208,384]{1,0:T(8,128)(2,1)S(1)}, u32[]{:S(2)}, u32[]{:S(2)}) collective-permute-start(bf16[208,384]{1,0:T(8,128)(2,1)S(1)} %constant_dynamic-slice_fusion.1), channel_id=1, source_target_pairs={{0,8},{8,0},{16,24},{24,16},{1,9},{9,1},{17,25},{25,17},{2,10},{10... | collective-permute-start | bytes 479240 | tf_op jit(solution)/shard_map/ppermute | solution.py:34
  233.8 7.7 %collective-permute-start.28 = (bf16[144,384]{1,0:T(8,128)(2,1)S(1)}, bf16[144,384]{1,0:T(8,128)(2,1)S(1)}, u32[]{:S(2)}, u32[]{:S(2)}) collective-permute-start(bf16[144,384]{1,0:T(8,128)(2,1)S(1)} %fusion.7), channel_id=1, source_target_pairs={{0,4},{2,6},{4,0},{6,2},{1,5},{3,7},{5,1},{7,3},{8,12},{10,14},{12... | collective-permute-start | bytes 331784 | tf_op jit(solution)/shard_map/ppermute | solution.py:34
  237.1 5.4 %collective-permute-start.32 = (bf16[208,384]{1,0:T(8,128)(2,1)S(1)}, bf16[208,384]{1,0:T(8,128)(2,1)S(1)}, u32[]{:S(2)}, u32[]{:S(2)}) collective-permute-start(bf16[208,384]{1,0:T(8,128)(2,1)S(1)} %fusion.3), channel_id=1, source_target_pairs={{0,16},{8,24},{16,0},{24,8},{1,17},{9,25},{17,1},{25,9},{2,18},{10... | collective-permute-start | bytes 479240 | tf_op jit(solution)/shard_map/ppermute | solution.py:34
  242.5 1.5 collective-permute-start.33
  (13 other events, 40.5 us)

commit v5 on v4

--- a/solution.py
+++ b/solution.py
@@ -449,12 +449,18 @@
     half_rot = ROT // 2
     exponent = lax.rem(lane, half_rot).astype(F32) * (1.0 / half_rot)
     frequency = jnp.where(lane < ROT, 1.0 / jnp.exp(exponent * jnp.log(jnp.full_like(exponent, 10000.0))), 0.0)
-    for i, (slot, half) in enumerate([(slot, col) for slot in ORDER] + [(0, 1 - col)]):
+    insides = []
+    for half in (col, 1 - col):
+        angles = (inside + half * HALF).astype(F32) * frequency
+        insides.append((jnp.cos(angles), jnp.sin(angles)))
+    for i, slot in enumerate(ORDER + (0,)):
         block = lax.bitwise_xor(seq, slot // 2) * shape.row_count + lax.bitwise_xor(row, slot % 2)
         start = (block - first_of(meta_ref, block, shape)) * BLOCK
-        angles = (inside + (start + half * HALF)).astype(F32) * frequency
-        cos_ref[i] = jnp.cos(angles)
-        turned = jnp.sin(angles)
+        angles = jnp.full((8, 2 * HD), start, jnp.int32).astype(F32) * frequency[:8, :]
+        cos_start, sin_start = jnp.cos(angles)[0:1, :], jnp.sin(angles)[0:1, :]
+        cos_in, sin_in = insides[i // 4]
+        cos_ref[i] = cos_in * cos_start - sin_in * sin_start
+        turned = sin_in * cos_start + cos_in * sin_start
         sin_ref[i] = jnp.where(lane < half_rot, -turned, jnp.where(lane < ROT, turned, 0.0))
 
 

time: 251 us -> 250 us (level)
    ppermute x29, starting transfers between devices: 43 us -> 45.6 us  [swap(): return lax.ppermute(value, axis, [(i, i ^ bit) for i in range(count)])]
where the time goes in v5:
time: 250 us
  Pallas kernels  81.9 us (33%)
  waiting for transfers between devices  73 us (29%)
  starting transfers between devices  55.5 us (22%)
  other arithmetic  25.2 us (10%)
  local copies, waits for them, and re-layouts  13 us (5%)
    ppermute x29, waiting for transfers between devices, swap(): return lax.ppermute(value, axis, [(i, i ^ bit) for i in range(count)])  73 us
    pallas_call x1, Pallas kernels, attention(): pl.pallas_call(functools.partial(attention_kernel, shape=shape), grid_spe...  47 us
    ppermute x29, starting transfers between devices, swap(): return lax.ppermute(value, axis, [(i, i ^ bit) for i in range(count)])  45.6 us
    pallas_call x1, Pallas kernels, feed_forward(): pl.pallas_call(forward_kernel, grid=(4,), in_specs=[pl.BlockSpec(memory_s...  16.2 us
    ppermute x6, starting transfers between devices, swap_some(): return lax.ppermute(value, ('seq', 'row', 'col'), pairs)  8.5 us
  transfers between devices with their start and end apart: 36, of which 19 were waited for; matrix products, arithmetic and copies ran while one was open for 10% of the time, Pallas kernels for 32%

profile of v5, /device:TPU:0, one launch (start us, length us, event | category | flops | bytes accessed | tf_op | source)
XLA Modules:
  0.0 249.7 jit_solution(5344244566869374586)
XLA Ops:
  2.8 1.3 concatenate.32.where_ref.meta_ref
  4.1 2.4 prologue.1
  6.5 3.0 %collective-permute-start = (bf16[400,384]{1,0:T(8,128)(2,1)}, bf16[400,384]{1,0:T(8,128)(2,1)S(1)}, u32[]{:S(2)}, u32[]{:S(2)}) collective-permute-start(bf16[400,384]{1,0:T(8,128)(2,1)} %get-tuple-element.70.pack_ref), channel_id=1, source_target_pairs={{0,1},{1,0},{2,3},{3,2},{4,5},{5,4},{6,7},{7,6},{8,9},{9,8},{10,11... | collective-permute-start | bytes 921608 | tf_op jit(solution)/shard_map/ppermute | solution.py:34
  9.4 2.9 %pack_weights.1 = (bf16[1952,384]{1,0:T(8,128)(2,1)}, bf16[976,384]{1,0:T(8,128)(2,1)}) custom-call(s32[22]{0:T(128)} %concatenate.32.where_ref.meta_ref, bf16[192,384]{1,0:T(8,128)(2,1)} %bitcast.30, bf16[192,384]{1,0:T(8,128)(2,1)} %ow_ref.1, bf16[384,768]{1,0:T(8,128)(2,1)} %up_ref.1, bf16[768,384]{1,0:T(8,128)(2,1)} %down_ref.1, f32[8,384]{1,0:T(8,128)} %reshape.57.vec_ref), custom_call_target="tpu_custom_call" | custom-call | tf_op jit(solution)/shard_map/pack_weights/pallas_call | solution.py:721
  13.0 3.9 %collective-permute-done.got_ref = bf16[400,384]{1,0:T(8,128)(2,1)S(1)} collective-permute-done((bf16[400,384]{1,0:T(8,128)(2,1)}, bf16[400,384]{1,0:T(8,128)(2,1)S(1)}, u32[]{:S(2)}, u32[]{:S(2)}) %collective-permute-start) | collective-permute-done | bytes 307232 | tf_op jit(solution)/shard_map/ppermute | solution.py:34
  16.9 3.6 %collective-permute-start.7 = (bf16[1952,384]{1,0:T(8,128)(2,1)}, bf16[1952,384]{1,0:T(8,128)(2,1)S(1)}, u32[]{:S(2)}, u32[]{:S(2)}) collective-permute-start(bf16[1952,384]{1,0:T(8,128)(2,1)} %get-tuple-element.81.pack_ref), channel_id=1, source_target_pairs={{0,1},{1,0},{2,3},{3,2},{4,5},{5,4},{6,7},{7,6},{16,17},{17,16},{1... | collective-permute-start | bytes 4497416 | tf_op jit(solution)/shard_map/ppermute | solution.py:57
  20.6 3.0 %tables.1 = (f32[5,256,128]{2,1,0:T(8,128)}, f32[5,256,128]{2,1,0:T(8,128)}) custom-call(s32[22]{0:T(128)} %concatenate.32.where_ref.meta_ref), custom_call_target="tpu_custom_call" | custom-call | tf_op jit(solution)/shard_map/tables/pallas_call | solution.py:469
  23.5 3.5 %own_pairs.1 = (bf16[1,512,128]{2,1,0:T(8,128)(2,1)}, bf16[2,256,768]{2,1,0:T(8,128)(2,1)}, bf16[128,768]{1,0:T(8,128)(2,1)}, f32[8,768]{1,0:T(8,128)}) custom-call(bf16[512,768]{1,0:T(8,128)(2,1)} %get-tuple-element.68.x_ref, bf16[256,384]{1,0:T(8,128)(2,1)} %get-tuple-element.69.mine_ref, bf16[400,384]{1,0:T(8,128)(2,1)} %get-tuple-element.70.pack_ref, ...), custom_call_target="tpu_custom_call" | custom-call | tf_op jit(solution)/shard_map/own_pairs/pallas_call | solution.py:768
  27.1 1.6 collective-permute-start.1
  28.7 7.3 %collective-permute-done.1 = bf16[1,512,128]{2,1,0:T(8,128)(2,1)S(1)} collective-permute-done((bf16[1,512,128]{2,1,0:T(8,128)(2,1)}, bf16[1,512,128]{2,1,0:T(8,128)(2,1)S(1)}, u32[]{:S(2)}, u32[]{:S(2)}) %collective-permute-start.1) | collective-permute-done | bytes 131104 | tf_op jit(solution)/shard_map/ppermute | solution.py:34
  38.5 2.0 collective-permute-start.3
  40.4 2.4 collective-permute-start.2
  42.8 10.5 %collective-permute-done.3 = bf16[2,512,128]{2,1,0:T(8,128)(2,1)S(1)} collective-permute-done((bf16[2,512,128]{2,1,0:T(8,128)(2,1)S(1)}, bf16[2,512,128]{2,1,0:T(8,128)(2,1)S(1)}, u32[]{:S(2)}, u32[]{:S(2)}) %collective-permute-start.3) | collective-permute-done | bytes 262176 | tf_op jit(solution)/shard_map/ppermute | solution.py:34
  56.0 1.4 collective-permute-start.8
  57.4 6.3 %collective-permute-done.2.both1_ref = bf16[2,256,768]{2,1,0:T(8,128)(2,1)S(1)} collective-permute-done((bf16[2,256,768]{2,1,0:T(8,128)(2,1)}, bf16[2,256,768]{2,1,0:T(8,128)(2,1)S(1)}, u32[]{:S(2)}, u32[]{:S(2)}) %collective-permute-start.2) | collective-permute-done | bytes 786464 | tf_op jit(solution)/shard_map/ppermute | solution.py:34
  63.7 5.7 %collective-permute-done.8 = bf16[4,512,128]{2,1,0:T(8,128)(2,1)S(1)} collective-permute-done((bf16[4,512,128]{2,1,0:T(8,128)(2,1)S(1)}, bf16[4,512,128]{2,1,0:T(8,128)(2,1)S(1)}, u32[]{:S(2)}, u32[]{:S(2)}) %collective-permute-start.8) | collective-permute-done | bytes 524320 | tf_op jit(solution)/shard_map/ppermute | solution.py:34
  69.4 1.4 collective-permute-start.10
  71.5 1.1 collective-permute-done.10.both2_ref
  72.7 1.1 collective-permute-done.11.both3_ref
  74.7 16.2 %feed_forward.1 = (bf16[4,256,768]{2,1,0:T(8,128)(2,1)}, bf16[4,256,768]{2,1,0:T(8,128)(2,1)}, f32[4,256,768]{2,1,0:T(8,128)}, f32[4,256,768]{2,1,0:T(8,128)}, b...) custom-call(s32[22]{0:T(128)} %concatenate.32.where_ref.meta_ref, ...), custom_call_target="tpu_custom_call" | custom-call | flops 7000000000 | bytes 20000000 | tf_op jit(solution)/shard_map/feed_forward/pallas_call | solution.py:629
  91.0 2.1 collective-permute-start.13
  94.0 47.0 %attention.1 = (f32[2,2,256,768]{3,2,1,0:T(8,128)}, bf16[2,2,256,768]{3,2,1,0:T(8,128)(2,1)}, bf16[416,384]{1,0:T(8,128)(2,1)}, bf16[416,384]{1,0:T(8,128)(2,1)}...) custom-call(s32[22]{0:T(128)} %concatenate.32.where_ref.meta_ref, ...), custom_call_target="tpu_custom_call" | custom-call | flops 24000000000 | bytes 30000000 | tf_op jit(solution)/shard_map/attention/pallas_call | solution.py:403
  141.0 6.4 %collective-permute-start.14 = (bf16[8,512,128]{2,1,0:T(8,128)(2,1)}, bf16[8,512,128]{2,1,0:T(8,128)(2,1)S(1)}, u32[]{:S(2)}, u32[]{:S(2)}) collective-permute-start(bf16[8,512,128]{2,1,0:T(8,128)(2,1)} %get-tuple-element.99), channel_id=1, source_target_pairs={{0,8},{8,0},{16,24},{24,16},{1,9},{9,1},{17,25},{25,17},{2,10},{10... | collective-permute-start | bytes 3145736 | tf_op jit(solution)/shard_map/ppermute | solution.py:34
  147.4 2.5 %collective-permute-done.14 = bf16[8,512,128]{2,1,0:T(8,128)(2,1)S(1)} collective-permute-done((bf16[8,512,128]{2,1,0:T(8,128)(2,1)}, bf16[8,512,128]{2,1,0:T(8,128)(2,1)S(1)}, u32[]{:S(2)}, u32[]{:S(2)}) %collective-permute-start.14) | collective-permute-done | bytes 1048608 | tf_op jit(solution)/shard_map/ppermute | solution.py:34
  149.9 2.5 %add_convert_fusion.3 = bf16[8,256,128]{2,1,0:T(8,128)(2,1)} fusion(f32[8,512,128]{2,1,0:T(8,128)} %get-tuple-element.97, bf16[8,512,128]{2,1,0:T(8,128)(2,1)S(1)} %collective-permute-done.14), kind=kLoop, calls=%fused_computation.8 | loop fusion | flops 786432 | bytes 2097152 | tf_op jit(solution)/shard_map/convert_element_type | solution.py:1008
  152.8 1.9 broadcast_select_fusion
  155.5 2.4 collective-permute-done.20
  157.9 2.0 fusion.1
  160.0 2.8 %fusion = bf16[2,256,768]{2,1,0:T(8,128)(2,1)} fusion(f32[2,2,256,768]{3,2,1,0:T(8,128)} %get-tuple-element.100.keep_ref, bf16[2,2,256,768]{3,2,1,0:T(8,128)(2,1)} %collective-permute-done.16.core_ref), kind=kLoop, calls=%fused_computation.9 | loop fusion | flops 1179648 | bytes 3145728 | tf_op jit(solution)/shard_map/convert_element_type | solution.py:1011
  162.8 6.7 %collective-permute-done.15 = bf16[8,256,128]{2,1,0:T(8,128)(2,1)S(1)} collective-permute-done((bf16[8,256,128]{2,1,0:T(8,128)(2,1)}, bf16[8,256,128]{2,1,0:T(8,128)(2,1)S(1)}, u32[]{:S(2)}, u32[]{:S(2)}) %collective-permute-start.15) | collective-permute-done | bytes 524320 | tf_op jit(solution)/shard_map/ppermute | solution.py:34
  170.8 2.0 collective-permute-start.17
  174.5 4.5 %collective-permute-done.17 = bf16[4,256,128]{2,1,0:T(8,128)(2,1)} collective-permute-done((bf16[4,256,128]{2,1,0:T(8,128)(2,1)}, bf16[4,256,128]{2,1,0:T(8,128)(2,1)}, u32[]{:S(2)}, u32[]{:S(2)}) %collective-permute-start.17) | collective-permute-done | bytes 262176 | tf_op jit(solution)/shard_map/ppermute | solution.py:34
  180.0 4.7 %collective-permute-done.21 = bf16[768,384]{1,0:T(8,128)(2,1)} collective-permute-done((bf16[768,384]{1,0:T(8,128)(2,1)}, bf16[768,384]{1,0:T(8,128)(2,1)}, u32[]{:S(2)}, u32[]{:S(2)}) %collective-permute-start.21) | collective-permute-done | bytes 589856 | tf_op jit(solution)/shard_map/ppermute | solution.py:34
  185.2 13.9 %collective-permute-start.19 = (bf16[2,256,128]{2,1,0:T(8,128)(2,1)S(1)}, bf16[2,256,128]{2,1,0:T(8,128)(2,1)S(1)}, u32[]{:S(2)}, u32[]{:S(2)}) collective-permute-start(bf16[2,256,128]{2,1,0:T(8,128)(2,1)S(1)} %slice.193), channel_id=1, source_target_pairs={{0,4},{2,6},{4,0},{6,2},{1,5},{3,7},{5,1},{7,3},{8,12},{10,14},{12... | collective-permute-start | bytes 393224 | tf_op jit(solution)/shard_map/ppermute | solution.py:34
  199.1 2.3 reduce-precision_convert_fusion
  202.1 2.0 collective-permute-done.19.got_ref
  204.7 2.9 %pair_sums.1 = (f32[144,384]{1,0:T(8,128)}, bf16[144,384]{1,0:T(8,128)(2,1)}) custom-call(f32[2,256,128]{2,1,0:T(8,128)} %slice.130.keep_ref, bf16[2,256,128]{2,1,0:T(8,128)(2,1)} %copy-done.7, f32[5,256,128]{2,1,0:T(8,128)} %get-tuple-element.74.cos_ref, f32[5,256,128]{2,1,0:T(8,128)} %get-tuple-element.75.sin_ref, ...), custom_call_target="tpu_custom_call" | custom-call | tf_op jit(solution)/shard_map/pair_sums/pallas_call | solution.py:825
  207.6 1.2 collective-permute-start.24
  209.8 2.8 %collective-permute-done.24 = bf16[144,384]{1,0:T(8,128)(2,1)S(1)} collective-permute-done((bf16[144,384]{1,0:T(8,128)(2,1)}, bf16[144,384]{1,0:T(8,128)(2,1)S(1)}, u32[]{:S(2)}, u32[]{:S(2)}) %collective-permute-start.24) | collective-permute-done | bytes 110624 | tf_op jit(solution)/shard_map/ppermute | solution.py:34
  214.7 1.4 collective-permute-start.30
  216.7 4.1 %own_rows.1 = (bf16[2,256,384]{2,1,0:T(8,128)(2,1)}, bf16[2,256,384]{2,1,0:T(8,128)(2,1)}) custom-call(f32[1,256,128]{2,1,0:T(8,128)} %get-tuple-element.135.own_ref, bf16[256,128]{1,0:T(8,128)(2,1)} %copy-done.12, f32[5,256,128]{2,1,0:T(8,128)} %get-tuple-element.74.cos_ref, f32[5,256,128]{2,1,0:T(8,128)} %get-tuple-element.75.sin_ref, ...), custom_call_target="tpu_custom_call" | custom-call | tf_op jit(solution)/shard_map/own_rows/pallas_call | solution.py:885
  220.8 1.2 collective-permute-start.23
  222.3 1.7 collective-permute-start.35
  224.1 3.3 %collective-permute-done.26 = bf16[144,384]{1,0:T(8,128)(2,1)S(1)} collective-permute-done((bf16[144,384]{1,0:T(8,128)(2,1)S(1)}, bf16[144,384]{1,0:T(8,128)(2,1)S(1)}, u32[]{:S(2)}, u32[]{:S(2)}) %collective-permute-start.26) | collective-permute-done | bytes 110624 | tf_op jit(solution)/shard_map/ppermute | solution.py:34
  227.5 2.5 collective-permute-start.31
  230.0 3.4 %collective-permute-done.27 = bf16[144,384]{1,0:T(8,128)(2,1)S(1)} collective-permute-done((bf16[144,384]{1,0:T(8,128)(2,1)S(1)}, bf16[144,384]{1,0:T(8,128)(2,1)S(1)}, u32[]{:S(2)}, u32[]{:S(2)}) %collective-permute-start.27) | collective-permute-done | bytes 110624 | tf_op jit(solution)/shard_map/ppermute | solution.py:34
  233.4 1.8 collective-permute-start.28
  237.1 4.4 %collective-permute-done.28 = bf16[144,384]{1,0:T(8,128)(2,1)S(1)} collective-permute-done((bf16[144,384]{1,0:T(8,128)(2,1)S(1)}, bf16[144,384]{1,0:T(8,128)(2,1)S(1)}, u32[]{:S(2)}, u32[]{:S(2)}) %collective-permute-start.28) | collective-permute-done | bytes 110624 | tf_op jit(solution)/shard_map/ppermute | solution.py:34
  (137 shorter events, 31.7 us)
Async XLA Ops:
  6.5 10.4 %collective-permute-start = (bf16[400,384]{1,0:T(8,128)(2,1)}, bf16[400,384]{1,0:T(8,128)(2,1)S(1)}, u32[]{:S(2)}, u32[]{:S(2)}) collective-permute-start(bf16[400,384]{1,0:T(8,128)(2,1)} %get-tuple-element.70.pack_ref), channel_id=1, source_target_pairs={{0,1},{1,0},{2,3},{3,2},{4,5},{5,4},{6,7},{7,6},{8,9},{9,8},{10,11... | collective-permute-start | bytes 921608 | tf_op jit(solution)/shard_map/ppermute | solution.py:34
  12.3 23.8 %collective-permute-start.4 = (bf16[976,384]{1,0:T(8,128)(2,1)}, bf16[976,384]{1,0:T(8,128)(2,1)S(1)}, u32[]{:S(2)}, u32[]{:S(2)}) collective-permute-start(bf16[976,384]{1,0:T(8,128)(2,1)} %get-tuple-element.79), channel_id=1, source_target_pairs={{8,12},{9,13},{10,14},{11,15},{12,8},{13,9},{14,10},{15,11},{24,28... | collective-permute-start | bytes 2248712 | tf_op jit(solution)/shard_map/ppermute | solution.py:57
  16.9 38.0 %collective-permute-start.7 = (bf16[1952,384]{1,0:T(8,128)(2,1)}, bf16[1952,384]{1,0:T(8,128)(2,1)S(1)}, u32[]{:S(2)}, u32[]{:S(2)}) collective-permute-start(bf16[1952,384]{1,0:T(8,128)(2,1)} %get-tuple-element.81.pack_ref), channel_id=1, source_target_pairs={{0,1},{1,0},{2,3},{3,2},{4,5},{5,4},{6,7},{7,6},{16,17},{17,16},{1... | collective-permute-start | bytes 4497416 | tf_op jit(solution)/shard_map/ppermute | solution.py:57
  27.1 42.3 %copy-start.17 = (bf16[2,256,768]{2,1,0:T(8,128)(2,1)S(1)}, bf16[2,256,768]{2,1,0:T(8,128)(2,1)}, u32[]{:S(2)}) copy-start(bf16[2,256,768]{2,1,0:T(8,128)(2,1)} %get-tuple-element.85.both0_ref) | copy-start | bytes 2359300
  27.1 43.8 %copy-start.3 = (bf16[1,512,128]{2,1,0:T(8,128)(2,1)S(1)}, bf16[1,512,128]{2,1,0:T(8,128)(2,1)}, u32[]{:S(2)}) copy-start(bf16[1,512,128]{2,1,0:T(8,128)(2,1)} %get-tuple-element.77) | copy-start | bytes 393220
  27.1 9.0 %collective-permute-start.1 = (bf16[1,512,128]{2,1,0:T(8,128)(2,1)}, bf16[1,512,128]{2,1,0:T(8,128)(2,1)S(1)}, u32[]{:S(2)}, u32[]{:S(2)}) collective-permute-start(bf16[1,512,128]{2,1,0:T(8,128)(2,1)} %get-tuple-element.77), channel_id=1, source_target_pairs={{0,2},{2,0},{4,6},{6,4},{1,3},{3,1},{5,7},{7,5},{8,10},{10,8},{12,... | collective-permute-start | bytes 393224 | tf_op jit(solution)/shard_map/ppermute | solution.py:34
  36.1 34.9 %copy-start.21 = (bf16[976,384]{1,0:T(8,128)(2,1)}, bf16[976,384]{1,0:T(8,128)(2,1)S(1)}, u32[]{:S(2)}) copy-start(bf16[976,384]{1,0:T(8,128)(2,1)S(1)} %collective-permute-done.4.z_ref) | copy-start | bytes 2248708
  36.1 17.2 %collective-permute-start.5 = (bf16[976,384]{1,0:T(8,128)(2,1)S(1)}, bf16[976,384]{1,0:T(8,128)(2,1)S(1)}, u32[]{:S(2)}, u32[]{:S(2)}) collective-permute-start(bf16[976,384]{1,0:T(8,128)(2,1)S(1)} %collective-permute-done.4.z_ref), channel_id=1, source_target_pairs={{8,24},{9,25},{10,26},{11,27},{12,28},{13,29},{14,30},{15,31},{24,... | collective-permute-start | bytes 2248712 | tf_op jit(solution)/shard_map/ppermute | solution.py:57
  36.8 17.2 %collective-permute-start.6 = (bf16[976,384]{1,0:T(8,128)(2,1)S(1)}, bf16[976,384]{1,0:T(8,128)(2,1)S(1)}, u32[]{:S(2)}, u32[]{:S(2)}) collective-permute-start(bf16[976,384]{1,0:T(8,128)(2,1)S(1)} %collective-permute-done.4.z_ref), channel_id=1, source_target_pairs={{8,9},{9,8},{10,11},{11,10},{12,13},{13,12},{14,15},{15,14},{24,25... | collective-permute-start | bytes 2248712 | tf_op jit(solution)/shard_map/ppermute | solution.py:57
  38.5 14.9 %collective-permute-start.3 = (bf16[2,512,128]{2,1,0:T(8,128)(2,1)S(1)}, bf16[2,512,128]{2,1,0:T(8,128)(2,1)S(1)}, u32[]{:S(2)}, u32[]{:S(2)}) collective-permute-start(bf16[2,512,128]{2,1,0:T(8,128)(2,1)S(1)} %pad_maximum_fusion.5), channel_id=1, source_target_pairs={{0,4},{2,6},{4,0},{6,2},{1,5},{3,7},{5,1},{7,3},{8,12},{10,14},{12... | collective-permute-start | bytes 786440 | tf_op jit(solution)/shard_map/ppermute | solution.py:34
  40.4 23.3 %collective-permute-start.2 = (bf16[2,256,768]{2,1,0:T(8,128)(2,1)}, bf16[2,256,768]{2,1,0:T(8,128)(2,1)S(1)}, u32[]{:S(2)}, u32[]{:S(2)}) collective-permute-start(bf16[2,256,768]{2,1,0:T(8,128)(2,1)} %get-tuple-element.85.both0_ref), channel_id=1, source_target_pairs={{0,2},{2,0},{4,6},{6,4},{1,3},{3,1},{5,7},{7,5},{8,10},{10,8},{12,... | collective-permute-start | bytes 2359304 | tf_op jit(solution)/shard_map/ppermute | solution.py:34
  53.3 16.0 %copy-start.22 = (bf16[976,384]{1,0:T(8,128)(2,1)}, bf16[976,384]{1,0:T(8,128)(2,1)S(1)}, u32[]{:S(2)}) copy-start(bf16[976,384]{1,0:T(8,128)(2,1)S(1)} %collective-permute-done.5.x_got_ref) | copy-start | bytes 2248708
  53.3 10.4 %collective-permute-start.9 = (bf16[976,384]{1,0:T(8,128)(2,1)S(1)}, bf16[976,384]{1,0:T(8,128)(2,1)S(1)}, u32[]{:S(2)}, u32[]{:S(2)}) collective-permute-start(bf16[976,384]{1,0:T(8,128)(2,1)S(1)} %collective-permute-done.5.x_got_ref), channel_id=1, source_target_pairs={{8,9},{9,8},{10,11},{11,10},{12,13},{13,12},{14,15},{15,14},{24,25... | collective-permute-start | bytes 2248712 | tf_op jit(solution)/shard_map/ppermute | solution.py:57
  54.9 16.1 %copy-start.15 = (bf16[1952,384]{1,0:T(8,128)(2,1)}, bf16[1952,384]{1,0:T(8,128)(2,1)S(1)}, u32[]{:S(2)}) copy-start(bf16[1952,384]{1,0:T(8,128)(2,1)S(1)} %collective-permute-done.7.even_ref) | copy-start | bytes 4497412
  56.0 13.3 %collective-permute-start.8 = (bf16[4,512,128]{2,1,0:T(8,128)(2,1)S(1)}, bf16[4,512,128]{2,1,0:T(8,128)(2,1)S(1)}, u32[]{:S(2)}, u32[]{:S(2)}) collective-permute-start(bf16[4,512,128]{2,1,0:T(8,128)(2,1)S(1)} %pad_maximum_fusion.2), channel_id=1, source_target_pairs={{0,16},{8,24},{16,0},{24,8},{1,17},{9,25},{17,1},{25,9},{2,18},{10... | collective-permute-start | bytes 1572872 | tf_op jit(solution)/shard_map/ppermute | solution.py:34
  63.7 9.0 %copy-start.18 = (bf16[2,256,768]{2,1,0:T(8,128)(2,1)}, bf16[2,256,768]{2,1,0:T(8,128)(2,1)S(1)}, u32[]{:S(2)}) copy-start(bf16[2,256,768]{2,1,0:T(8,128)(2,1)S(1)} %collective-permute-done.2.both1_ref) | copy-start | bytes 2359300
  69.4 3.3 %collective-permute-start.10 = (bf16[2,256,768]{2,1,0:T(8,128)(2,1)S(1)}, bf16[2,256,768]{2,1,0:T(8,128)(2,1)S(1)}, u32[]{:S(2)}, u32[]{:S(2)}) collective-permute-start(bf16[2,256,768]{2,1,0:T(8,128)(2,1)S(1)} %copy-done.17), channel_id=1, source_target_pairs={{0,8},{8,0},{16,24},{24,16},{1,9},{9,1},{17,25},{25,17},{2,10},{10... | collective-permute-start | bytes 2359304 | tf_op jit(solution)/shard_map/ppermute | solution.py:34
  70.8 3.0 %collective-permute-start.11 = (bf16[2,256,768]{2,1,0:T(8,128)(2,1)S(1)}, bf16[2,256,768]{2,1,0:T(8,128)(2,1)S(1)}, u32[]{:S(2)}, u32[]{:S(2)}) collective-permute-start(bf16[2,256,768]{2,1,0:T(8,128)(2,1)S(1)} %collective-permute-done.2.both1_ref), channel_id=1, source_target_pairs={{0,8},{8,0},{16,24},{24,16},{1,9},{9,1},{17,25},{25,17},{2,10},{10... | collective-permute-start | bytes 2359304 | tf_op jit(solution)/shard_map/ppermute | solution.py:34
  71.0 19.9 %copy-start.13 = (bf16[8,512,128]{2,1,0:T(8,128)(2,1)}, bf16[8,512,128]{2,1,0:T(8,128)(2,1)S(1)}, u32[]{:S(2)}) copy-start(bf16[8,512,128]{2,1,0:T(8,128)(2,1)S(1)} %constant_dynamic-update-slice_fusion.kv0_ref) | copy-start | bytes 3145732
  71.1 22.0 %collective-permute-start.12 = (bf16[8,512,128]{2,1,0:T(8,128)(2,1)S(1)}, bf16[8,512,128]{2,1,0:T(8,128)(2,1)S(1)}, u32[]{:S(2)}, u32[]{:S(2)}) collective-permute-start(bf16[8,512,128]{2,1,0:T(8,128)(2,1)S(1)} %constant_dynamic-update-slice_fusion.kv0_ref), channel_id=1, source_target_pairs={{0,8},{8,0},{16,24},{24,16},{1,9},{9,1},{17,25},{25,17},{2,10},{10... | collective-permute-start | bytes 3145736 | tf_op jit(solution)/shard_map/ppermute | solution.py:34
  91.0 50.0 %collective-permute-start.13 = (bf16[2,1536,384]{2,1,0:T(8,128)(2,1)}, bf16[2,1536,384]{2,1,0:T(8,128)(2,1)}, u32[]{:S(2)}, u32[]{:S(2)}) collective-permute-start(bf16[2,1536,384]{2,1,0:T(8,128)(2,1)} %get-tuple-element.105), channel_id=1, source_target_pairs={{8,12},{9,13},{10,14},{11,15},{12,8},{13,9},{14,10},{15,11},{24,28... | collective-permute-start | bytes 7077896 | tf_op jit(solution)/shard_map/ppermute | solution.py:57
  141.0 8.9 %collective-permute-start.14 = (bf16[8,512,128]{2,1,0:T(8,128)(2,1)}, bf16[8,512,128]{2,1,0:T(8,128)(2,1)S(1)}, u32[]{:S(2)}, u32[]{:S(2)}) collective-permute-start(bf16[8,512,128]{2,1,0:T(8,128)(2,1)} %get-tuple-element.99), channel_id=1, source_target_pairs={{0,8},{8,0},{16,24},{24,16},{1,9},{9,1},{17,25},{25,17},{2,10},{10... | collective-permute-start | bytes 3145736 | tf_op jit(solution)/shard_map/ppermute | solution.py:34
  152.4 7.5 %collective-permute-start.16 = (bf16[2,2,256,768]{3,2,1,0:T(8,128)(2,1)}, bf16[2,2,256,768]{3,2,1,0:T(8,128)(2,1)}, u32[]{:S(2)}, u32[]{:S(2)}) collective-permute-start(bf16[2,2,256,768]{3,2,1,0:T(8,128)(2,1)} %get-tuple-element.102), channel_id=1, source_target_pairs={{0,8},{8,0},{16,24},{24,16},{1,9},{9,1},{17,25},{25,17},{2,10},{10... | collective-permute-start | bytes 4718600 | tf_op jit(solution)/shard_map/ppermute | solution.py:34
  154.9 3.0 %collective-permute-start.20 = (bf16[2,768,384]{2,1,0:T(8,128)(2,1)S(1)}, bf16[2,768,384]{2,1,0:T(8,128)(2,1)}, u32[]{:S(2)}, u32[]{:S(2)}) collective-permute-start(bf16[2,768,384]{2,1,0:T(8,128)(2,1)S(1)} %constant_dynamic-slice_fusion.2), channel_id=1, source_target_pairs={{0,8},{8,0},{16,24},{24,16},{1,9},{9,1},{17,25},{25,17},{2,10},{10... | collective-permute-start | bytes 3538952 | tf_op jit(solution)/shard_map/ppermute | solution.py:34
  155.1 14.4 %collective-permute-start.15 = (bf16[8,256,128]{2,1,0:T(8,128)(2,1)}, bf16[8,256,128]{2,1,0:T(8,128)(2,1)S(1)}, u32[]{:S(2)}, u32[]{:S(2)}) collective-permute-start(bf16[8,256,128]{2,1,0:T(8,128)(2,1)} %add_convert_fusion.3), channel_id=1, source_target_pairs={{0,1},{1,0},{2,3},{3,2},{4,5},{5,4},{6,7},{7,6},{8,9},{9,8},{10,11... | collective-permute-start | bytes 1572872 | tf_op jit(solution)/shard_map/ppermute | solution.py:34
  160.0 9.9 %copy-start.2 = (f32[8,512,128]{2,1,0:T(8,128)S(1)}, f32[8,512,128]{2,1,0:T(8,128)}, u32[]{:S(2)}) copy-start(f32[8,512,128]{2,1,0:T(8,128)} %get-tuple-element.97) | copy-start | bytes 6291460
  160.0 9.9 %copy-start.5 = (bf16[8,512,128]{2,1,0:T(8,128)(2,1)S(1)}, bf16[8,512,128]{2,1,0:T(8,128)(2,1)}, u32[]{:S(2)}) copy-start(bf16[8,512,128]{2,1,0:T(8,128)(2,1)} %copy-done.4) | copy-start | bytes 3145732
  162.8 22.4 %collective-permute-start.18 = (bf16[2,256,768]{2,1,0:T(8,128)(2,1)}, bf16[2,256,768]{2,1,0:T(8,128)(2,1)}, u32[]{:S(2)}, u32[]{:S(2)}) collective-permute-start(bf16[2,256,768]{2,1,0:T(8,128)(2,1)} %fusion), channel_id=1, source_target_pairs={{0,2},{2,0},{4,6},{6,4},{1,3},{3,1},{5,7},{7,5},{8,10},{10,8},{12,... | collective-permute-start | bytes 2359304 | tf_op jit(solution)/shard_map/ppermute | solution.py:34
  169.5 15.2 %collective-permute-start.21 = (bf16[768,384]{1,0:T(8,128)(2,1)}, bf16[768,384]{1,0:T(8,128)(2,1)}, u32[]{:S(2)}, u32[]{:S(2)}) collective-permute-start(bf16[768,384]{1,0:T(8,128)(2,1)} %fusion.1), channel_id=1, source_target_pairs={{0,1},{1,0},{2,3},{3,2},{4,5},{5,4},{6,7},{7,6},{8,9},{9,8},{10,11... | collective-permute-start | bytes 1769480 | tf_op jit(solution)/shard_map/ppermute | solution.py:34
  170.8 8.2 %collective-permute-start.17 = (bf16[4,256,128]{2,1,0:T(8,128)(2,1)}, bf16[4,256,128]{2,1,0:T(8,128)(2,1)}, u32[]{:S(2)}, u32[]{:S(2)}) collective-permute-start(bf16[4,256,128]{2,1,0:T(8,128)(2,1)} %slice.192), channel_id=1, source_target_pairs={{0,16},{8,24},{16,0},{24,8},{1,17},{9,25},{17,1},{25,9},{2,18},{10... | collective-permute-start | bytes 786440 | tf_op jit(solution)/shard_map/ppermute | solution.py:34
  180.0 21.4 %copy-start = (f32[4,256,128]{2,1,0:T(8,128)}, f32[4,256,128]{2,1,0:T(8,128)S(1)}, u32[]{:S(2)}) copy-start(f32[4,256,128]{2,1,0:T(8,128)S(1)} %slice_add_fusion) | copy-start | bytes 1572868
  184.7 28.9 %collective-permute-start.29 = (bf16[416,384]{1,0:T(8,128)(2,1)}, bf16[416,384]{1,0:T(8,128)(2,1)}, u32[]{:S(2)}, u32[]{:S(2)}) collective-permute-start(bf16[416,384]{1,0:T(8,128)(2,1)} %get-tuple-element.117), channel_id=1, source_target_pairs={{0,1},{1,0},{2,3},{3,2},{4,5},{5,4},{6,7},{7,6},{8,9},{9,8},{10,11... | collective-permute-start | bytes 958472 | tf_op jit(solution)/shard_map/ppermute | solution.py:34
  185.2 18.9 %collective-permute-start.19 = (bf16[2,256,128]{2,1,0:T(8,128)(2,1)S(1)}, bf16[2,256,128]{2,1,0:T(8,128)(2,1)S(1)}, u32[]{:S(2)}, u32[]{:S(2)}) collective-permute-start(bf16[2,256,128]{2,1,0:T(8,128)(2,1)S(1)} %slice.193), channel_id=1, source_target_pairs={{0,4},{2,6},{4,0},{6,2},{1,5},{3,7},{5,1},{7,3},{8,12},{10,14},{12... | collective-permute-start | bytes 393224 | tf_op jit(solution)/shard_map/ppermute | solution.py:34
  201.4 20.8 %collective-permute-start.34 = (bf16[768,384]{1,0:T(8,128)(2,1)}, bf16[768,384]{1,0:T(8,128)(2,1)S(1)}, u32[]{:S(2)}, u32[]{:S(2)}) collective-permute-start(bf16[768,384]{1,0:T(8,128)(2,1)} %get-tuple-element.124), channel_id=1, source_target_pairs={{0,16},{8,24},{16,0},{24,8},{1,17},{9,25},{17,1},{25,9},{2,18},{10... | collective-permute-start | bytes 1769480 | tf_op jit(solution)/shard_map/ppermute | solution.py:34
  207.6 5.0 %collective-permute-start.24 = (bf16[144,384]{1,0:T(8,128)(2,1)}, bf16[144,384]{1,0:T(8,128)(2,1)S(1)}, u32[]{:S(2)}, u32[]{:S(2)}) collective-permute-start(bf16[144,384]{1,0:T(8,128)(2,1)} %get-tuple-element.114), channel_id=1, source_target_pairs={{0,1},{1,0},{2,3},{3,2},{4,5},{5,4},{6,7},{7,6},{8,9},{9,8},{10,11... | collective-permute-start | bytes 331784 | tf_op jit(solution)/shard_map/ppermute | solution.py:34
  209.4 6.6 %collective-permute-start.22 = (bf16[256,128]{1,0:T(8,128)(2,1)S(1)}, bf16[256,128]{1,0:T(8,128)(2,1)S(1)}, u32[]{:S(2)}, u32[]{:S(2)}) collective-permute-start(bf16[256,128]{1,0:T(8,128)(2,1)S(1)} %get-tuple-element.134), channel_id=1, source_target_pairs={{0,2},{2,0},{4,6},{6,4},{1,3},{3,1},{5,7},{7,5},{8,10},{10,8},{12,... | collective-permute-start | bytes 196616 | tf_op jit(solution)/shard_map/ppermute | solution.py:34
  213.5 8.5 %collective-permute-start.25 = (bf16[144,384]{1,0:T(8,128)(2,1)S(1)}, bf16[144,384]{1,0:T(8,128)(2,1)S(1)}, u32[]{:S(2)}, u32[]{:S(2)}) collective-permute-start(bf16[144,384]{1,0:T(8,128)(2,1)S(1)} %fusion.4), channel_id=1, source_target_pairs={{0,8},{8,0},{16,24},{24,16},{1,9},{9,1},{17,25},{25,17},{2,10},{10... | collective-permute-start | bytes 331784 | tf_op jit(solution)/shard_map/ppermute | solution.py:34
  214.7 9.4 %collective-permute-start.30 = (bf16[416,384]{1,0:T(8,128)(2,1)S(1)}, bf16[416,384]{1,0:T(8,128)(2,1)}, u32[]{:S(2)}, u32[]{:S(2)}) collective-permute-start(bf16[416,384]{1,0:T(8,128)(2,1)S(1)} %add_convert_fusion.4), channel_id=1, source_target_pairs={{8,12},{10,14},{12,8},{14,10},{24,28},{26,30},{28,24},{30,26},{9,1... | collective-permute-start | bytes 958472 | tf_op jit(solution)/shard_map/ppermute | solution.py:43
  220.8 14.5 %collective-permute-start.23 = (bf16[2,256,384]{2,1,0:T(8,128)(2,1)}, bf16[2,256,384]{2,1,0:T(8,128)(2,1)S(1)}, u32[]{:S(2)}, u32[]{:S(2)}) collective-permute-start(bf16[2,256,384]{2,1,0:T(8,128)(2,1)} %get-tuple-element.110), channel_id=1, source_target_pairs={{0,1},{1,0},{2,3},{3,2},{4,5},{5,4},{6,7},{7,6},{8,9},{9,8},{10,11... | collective-permute-start | bytes 1179656 | tf_op jit(solution)/shard_map/ppermute | solution.py:34
  222.0 5.3 %collective-permute-start.26 = (bf16[144,384]{1,0:T(8,128)(2,1)S(1)}, bf16[144,384]{1,0:T(8,128)(2,1)S(1)}, u32[]{:S(2)}, u32[]{:S(2)}) collective-permute-start(bf16[144,384]{1,0:T(8,128)(2,1)S(1)} %get-tuple-element.126), channel_id=1, source_target_pairs={{0,16},{8,24},{16,0},{24,8},{1,17},{9,25},{17,1},{25,9},{2,18},{10... | collective-permute-start | bytes 331784 | tf_op jit(solution)/shard_map/ppermute | solution.py:34
  222.3 12.9 %copy-start.9 = (bf16[2,256,384]{2,1,0:T(8,128)(2,1)S(1)}, bf16[2,256,384]{2,1,0:T(8,128)(2,1)}, u32[]{:S(2)}) copy-start(bf16[2,256,384]{2,1,0:T(8,128)(2,1)} %get-tuple-element.109) | copy-start | bytes 1179652
  222.3 24.4 %collective-permute-start.35 = (bf16[768,384]{1,0:T(8,128)(2,1)S(1)}, bf16[768,384]{1,0:T(8,128)(2,1)S(1)}, u32[]{:S(2)}, u32[]{:S(2)}) collective-permute-start(bf16[768,384]{1,0:T(8,128)(2,1)S(1)} %add_convert_fusion.1), channel_id=1, source_target_pairs={{0,8},{8,0},{16,24},{24,16},{1,9},{9,1},{17,25},{25,17},{2,10},{10... | collective-permute-start | bytes 1769480 | tf_op jit(solution)/shard_map/ppermute | solution.py:34
  227.4 6.0 %collective-permute-start.27 = (bf16[144,384]{1,0:T(8,128)(2,1)S(1)}, bf16[144,384]{1,0:T(8,128)(2,1)S(1)}, u32[]{:S(2)}, u32[]{:S(2)}) collective-permute-start(bf16[144,384]{1,0:T(8,128)(2,1)S(1)} %fusion.5), channel_id=1, source_target_pairs={{0,2},{2,0},{4,6},{6,4},{1,3},{3,1},{5,7},{7,5},{8,10},{10,8},{12,... | collective-permute-start | bytes 331784 | tf_op jit(solution)/shard_map/ppermute | solution.py:34
  227.5 9.5 %collective-permute-start.31 = (bf16[208,384]{1,0:T(8,128)(2,1)S(1)}, bf16[208,384]{1,0:T(8,128)(2,1)S(1)}, u32[]{:S(2)}, u32[]{:S(2)}) collective-permute-start(bf16[208,384]{1,0:T(8,128)(2,1)S(1)} %constant_dynamic-slice_fusion.1), channel_id=1, source_target_pairs={{0,8},{8,0},{16,24},{24,16},{1,9},{9,1},{17,25},{25,17},{2,10},{10... | collective-permute-start | bytes 479240 | tf_op jit(solution)/shard_map/ppermute | solution.py:34
  233.4 8.1 %collective-permute-start.28 = (bf16[144,384]{1,0:T(8,128)(2,1)S(1)}, bf16[144,384]{1,0:T(8,128)(2,1)S(1)}, u32[]{:S(2)}, u32[]{:S(2)}) collective-permute-start(bf16[144,384]{1,0:T(8,128)(2,1)S(1)} %fusion.7), channel_id=1, source_target_pairs={{0,4},{2,6},{4,0},{6,2},{1,5},{3,7},{5,1},{7,3},{8,12},{10,14},{12... | collective-permute-start | bytes 331784 | tf_op jit(solution)/shard_map/ppermute | solution.py:34
  237.1 5.4 %collective-permute-start.32 = (bf16[208,384]{1,0:T(8,128)(2,1)S(1)}, bf16[208,384]{1,0:T(8,128)(2,1)S(1)}, u32[]{:S(2)}, u32[]{:S(2)}) collective-permute-start(bf16[208,384]{1,0:T(8,128)(2,1)S(1)} %fusion.3), channel_id=1, source_target_pairs={{0,16},{8,24},{16,0},{24,8},{1,17},{9,25},{17,1},{25,9},{2,18},{10... | collective-permute-start | bytes 479240 | tf_op jit(solution)/shard_map/ppermute | solution.py:34
  242.2 6.9 %copy-start.14 = (f32[384]{0:T(512)}, f32[384]{0:T(512)S(1)}, u32[]{:S(2)}) copy-start(f32[384]{0:T(512)S(1)} %get-tuple-element.178) | copy-start | bytes 4612
  242.5 1.5 collective-permute-start.33
  (13 other events, 39.4 us)
